TPU v7x, 256 devices: a whole 4x4x8 slice. The times are simulated.
256 devices in a mesh: path: 32 (over x, z), mp: 2 (over core), period: 4 (over y).
Axes of the slice: x: 4, y: 4, z: 8, core: 2. Of those that a mesh axis runs over, the one named last changes fastest.
Arguments:
- tiles: bfloat16 [4096, 256, 256], P(('path', 'mp')), may hold values from -0.375 to 0.375
- tile_rows: int32 [4096], P(('path', 'mp')), may hold values from 0 to 7
- tile_cols: int32 [4096], P(('path', 'mp')), may hold values from 0 to 1023, as said below
- tile_counts: int32 [64], P(('path', 'mp')), may hold values from 8 to 64, as said below
- data: float32 [262144], P(('period', 'path')), parts along dimension 0, may hold values from -6 to 6
Outputs:
- solution: float32 [2097152], P(('period', 'path', 'mp')), parts along dimension 0
- left_vector: float32 [262144], P(('period', 'path')), parts along dimension 0
There are 4 independent parts, one for each index of `period`. A program takes and returns all parts, laid end to end along the dimension named above; an argument that names none is the same for every part. Nothing has to cross between parts.
Inputs may be any that keep to these rules, and one draw needn't show every extreme that they name: `tile_counts`: slots from the strip's count on are unused; some strips are full. `tile_cols`: among all 64 slots of one strip, at most 8 name cell tiles t with the same t // 32, and in every strip some value of t // 32 is named by exactly 8 slots.
All inputs are finite; a program needn't handle non-finite values.
Results may differ from a plain program's by a relative error of at most 0.0066.
Values may be sent and summed in bfloat16 or wider, within the bound.
No kernel may reach another device: no remote copies, remote signals or barrier semaphores. Data moves between devices by JAX's collectives and lax.ppermute only.
A program may use at most 64 MiB of HBM per device.

v0:
```python
import jax
import jax.numpy as jnp
from jax import lax
from jax.sharding import PartitionSpec as P

CT_DEV = 32
ITERS = 2


def on_device(tiles, tile_rows, tile_cols, tile_counts, data):
    tile = tiles.shape[1]
    slots = tiles.shape[0]
    row_tiles = data.shape[0] // tile
    npath = lax.axis_size("path")
    half_tiles = CT_DEV * npath
    limit = max(2, max(slots // 8, (slots + npath - 1) // npath))
    live = lax.iota(jnp.int32, slots) < tile_counts[0]
    row_onehot = (
        (tile_rows[None, :] == lax.iota(jnp.int32, row_tiles)[:, None]) & live[None, :]
    ).astype(jnp.float32)
    col_onehot = (
        (tile_cols[None, :] == lax.iota(jnp.int32, half_tiles)[:, None]) & live[None, :]
    ).astype(jnp.float32)
    owner = tile_cols // CT_DEV
    inside = tile_cols % CT_DEV
    same_owner = (owner[:, None] == owner[None, :]).astype(jnp.int32)
    earlier = (lax.iota(jnp.int32, slots)[None, :] < lax.iota(jnp.int32, slots)[:, None]).astype(
        jnp.int32
    )
    rank = jnp.sum(same_owner * earlier, axis=1)
    target = owner * limit + rank
    place = lax.iota(jnp.int32, npath * limit)[:, None] == target[None, :]
    place_live = (place & live[None, :]).astype(jnp.float32)
    slot_inside = (
        jnp.sum(jnp.where(place, inside[None, :], 0), axis=1)
        - 1
        + jnp.sum(place.astype(jnp.int32), axis=1)
    )
    send_index = jnp.where(jnp.sum(place_live, axis=1) > 0, slot_inside, -1).reshape(npath, limit)

    def forward_prods(picked):
        prods = jnp.einsum("sij,sj->si", tiles, picked, preferred_element_type=jnp.float32)
        local = jnp.dot(row_onehot, prods, precision=lax.Precision.HIGHEST).reshape(-1)
        return lax.psum(local, "mp")

    def backward_prods(left_b):
        picked = left_b.reshape(row_tiles, tile)[tile_rows]
        return jnp.einsum("sij,si->sj", tiles, picked, preferred_element_type=jnp.float32)

    def row_norm(left):
        return jnp.sqrt(lax.psum(jnp.sum(left * left), "path") + 1e-12)

    def col_norm(own):
        return jnp.sqrt(lax.psum(jnp.sum(own * own), ("path", "mp")) + 1e-12)

    def right_step(left, state, beta, asked):
        prods = backward_prods(left.astype(jnp.bfloat16))
        partial_cols = jnp.dot(col_onehot, prods, precision=lax.Precision.HIGHEST).reshape(-1)
        own = lax.psum_scatter(partial_cols, "path", scatter_dimension=0, tiled=True)
        if state is not None:
            own = own - beta * state
        alpha = col_norm(own)
        own = own / alpha
        return (own, own, alpha, asked)

    beta = row_norm(data)
    left = data / beta
    phibar = beta
    asked = send_index
    state, right, alpha, asked = right_step(left, None, beta, asked)
    search = right
    rhobar = alpha
    solution = jnp.zeros_like(right)
    for step in range(ITERS):
        half_b = lax.all_gather(state.astype(jnp.bfloat16), "path", axis=0, tiled=True)
        forward_picked = half_b.reshape(half_tiles, tile)[tile_cols]
        left = forward_prods(forward_picked) - alpha * left
        beta = row_norm(left)
        left = left / beta
        state, right, alpha, asked = right_step(left, state, beta, asked)
        rho = jnp.sqrt(rhobar * rhobar + beta * beta)
        cosine = rhobar / rho
        sine = beta / rho
        theta = sine * alpha
        rhobar = -cosine * alpha
        phi = cosine * phibar
        phibar = sine * phibar
        solution = solution + phi / rho * search
        search = right - theta / rho * search
    total_rows = row_tiles * tile * npath
    return (solution, left * jnp.sqrt(jnp.float32(total_rows)))


def solution(mesh):
    placed = (
        P(("path", "mp"), None, None),
        P(("path", "mp")),
        P(("path", "mp")),
        P(("path", "mp")),
        P(("period", "path")),
    )
    return jax.shard_map(
        on_device,
        mesh=mesh,
        in_specs=placed,
        out_specs=(P(("period", "path", "mp")), P(("period", "path"))),
        check_vma=False,
    )
```

profile of v0, /device:TPU:16, one launch (start us, length us, event | category | flops | bytes accessed | tf_op | source)
XLA Modules:
  0.0 916.6 jit_solution(12098558276543920752)
XLA Ops:
  7.2 0.0 copy-start.1
  7.2 0.0 all-reduce.5.cloned.1.call-start
  7.2 1.3 multiply_reduce_fusion.4
  8.5 78.3 %psum.49 = f32[]{:T(128)} all-reduce(f32[]{:T(128)} %multiply_reduce_fusion.4), channel_id=1, replica_groups=mesh['path'=32,'mp'=2,'period'=4] {'path'}, use_global_device_ids=true, to_apply=%region_1.0 | all-reduce | flops 1 | bytes 8 | tf_op jit(solution)/shard_map/psum | solution.py:51
  87.5 0.7 fusion.27
  88.2 0.7 compare_select_fusion.1
  89.6 0.7 gather_fusion
  90.3 0.0 copy-start.3
  90.3 4.6 fusion.21
  94.8 0.0 copy-done.1
  94.9 0.6 convolution_bitcast_fusion.1
  95.4 1.6 copy.15
  97.0 0.0 all-reduce.5.cloned.1.call-update
  97.0 0.0 all-reduce.7.cloned.1.call-start
  97.1 0.0 copy-done.3
  97.1 0.6 dynamic-slice
  98.3 143.0 %all-reduce.5.cloned.1.call-done = f32[262144]{0:T(1024)} async-done(((f32[262144]{0:T(1024)}), f32[262144]{0:T(1024)}) %all-reduce.5.cloned.1.call-update) | async-done | bytes 1048592
  241.4 1.4 multiply_reduce_fusion.1
  242.8 124.7 %psum.50 = f32[]{:T(128)} all-reduce(f32[]{:T(128)} %multiply_reduce_fusion.1), channel_id=1, replica_groups=mesh['path'=32,'mp'=2,'period'=4] {'path','mp'}, use_global_device_ids=true, to_apply=%region_4.0 | all-reduce | flops 1 | bytes 8 | tf_op jit(solution)/shard_map/psum | solution.py:54
  368.1 0.8 fusion.33
  368.9 46.3 %all_gather.6 = bf16[262144]{0:T(1024)(128)(2,1)S(1)} all-gather(bf16[8192]{0:T(1024)(128)(2,1)S(1)} %fusion.33), channel_id=1, replica_groups=mesh['path'=32,'mp'=2,'period'=4] {'path'}, dimensions={0}, use_global_device_ids=true | all-gather | bytes 540672 | tf_op jit(solution)/shard_map/all_gather | solution.py:75
  415.2 0.2 reshape.36
  415.4 0.7 gather_fusion.1
  416.1 5.6 fusion.18
  421.7 0.0 copy-done.2
  421.7 0.1 convolution_bitcast_fusion.3
  421.9 2.5 psum.51
  424.4 0.6 multiply_reduce_fusion.3
  425.0 72.9 %psum.52 = f32[]{:T(128)} all-reduce(f32[]{:T(128)} %get-tuple-element.2), channel_id=1, replica_groups=mesh['path'=32,'mp'=2,'period'=4] {'path'}, use_global_device_ids=true, to_apply=%region_7.0 | all-reduce | flops 1 | bytes 8 | tf_op jit(solution)/shard_map/psum | solution.py:51
  498.6 0.7 gather_fusion.2
  499.3 4.6 fusion.15
  503.9 0.6 convolution_bitcast_fusion
  504.5 1.5 copy.17
  506.0 0.0 all-reduce.7.cloned.1.call-update
  506.2 144.1 %all-reduce.7.cloned.1.call-done = f32[262144]{0:T(1024)} async-done(((f32[262144]{0:T(1024)}), f32[262144]{0:T(1024)}) %all-reduce.7.cloned.1.call-update) | async-done | bytes 1048592
  650.3 1.4 multiply_reduce_fusion
  651.7 124.7 %psum.53 = f32[]{:T(128)} all-reduce(f32[]{:T(128)} %multiply_reduce_fusion), channel_id=1, replica_groups=mesh['path'=32,'mp'=2,'period'=4] {'path','mp'}, use_global_device_ids=true, to_apply=%region_10.0 | all-reduce | flops 1 | bytes 8 | tf_op jit(solution)/shard_map/psum | solution.py:54
  777.1 0.8 fusion.23
  777.9 46.3 %all_gather.7 = bf16[262144]{0:T(1024)(128)(2,1)S(1)} all-gather(bf16[8192]{0:T(1024)(128)(2,1)S(1)} %fusion.23), channel_id=1, replica_groups=mesh['path'=32,'mp'=2,'period'=4] {'path'}, dimensions={0}, use_global_device_ids=true | all-gather | bytes 540672 | tf_op jit(solution)/shard_map/all_gather | solution.py:75
  824.2 0.2 reshape.40
  824.4 0.7 gather_fusion.3
  825.1 5.6 fusion.12
  830.7 0.1 convolution_bitcast_fusion.2
  830.9 2.5 psum.54
  833.4 0.6 multiply_reduce_fusion.2
  834.0 72.9 %psum.55 = f32[]{:T(128)} all-reduce(f32[]{:T(128)} %multiply_reduce_fusion.2), channel_id=1, replica_groups=mesh['path'=32,'mp'=2,'period'=4] {'path'}, use_global_device_ids=true, to_apply=%region_13.0 | all-reduce | flops 1 | bytes 8 | tf_op jit(solution)/shard_map/psum | solution.py:51
  907.6 0.6 divide_multiply_fusion
  908.4 1.4 multiply_add_fusion
  (12 shorter events, 0.1 us)
Async XLA Ops:
  7.2 87.7 %copy-start.1 = (s32[64]{0:T(128)S(1)}, s32[64]{0:T(128)}, u32[]{:S(2)}) copy-start(s32[64]{0:T(128)} %param.7) | copy-start | bytes 772
  7.2 234.2 %all-reduce.5.cloned.1.call-start = ((), (), s32[]{:S(2)}) async-start(), calls=%async_computation | async-start | bytes 2097152
  90.3 6.8 copy-start.3
  94.9 326.9 %copy-start.2 = (s32[64]{0:T(128)S(1)}, s32[64]{0:T(128)}, u32[]{:S(2)}) copy-start(s32[64]{0:T(128)} %param.6) | copy-start | bytes 772
  94.9 329.5 %copy-start = (f32[2048]{0:T(1024)S(1)}, f32[2048]{0:T(1024)}, u32[]{:S(2)}) copy-start(f32[2048]{0:T(1024)} %param.9) | copy-start | bytes 24580
  97.0 553.2 %all-reduce.7.cloned.1.call-start = ((), (), s32[]{:S(2)}) async-start(), calls=%async_computation.1 | async-start | bytes 2097152
Sparse Core Ops, SparseCore 0:
  97.1 144.1 all-reduce.4
  506.2 144.0 all-reduce.6
where the time goes:
time: 918 us; the launch traced here: 917 us
  blocking collectives  571 us (62%)
  waiting for transfers between devices  287 us (31%)
  matrix products  21.9 us (2%)
  between operations  19.3 us (2%)
  other arithmetic  10.3 us (1%)
    unnamed x4, waiting for transfers between devices  287 us
    psum x2, blocking collectives, col_norm(): return jnp.sqrt(lax.psum(jnp.sum(own * own), ('path', 'mp')) + 1e-12)  249 us
    psum x3, blocking collectives, row_norm(): return jnp.sqrt(lax.psum(jnp.sum(left * left), 'path') + 1e-12)  224 us
    all_gather x2, blocking collectives, on_device(): lax.all_gather(state.astype(jnp.bfloat16), 'path', axis=0, tiled=True)  92.6 us
  transfers between devices with their start and end apart: 2, of which 2 were waited for; matrix products, arithmetic and copies ran while one was open for 0% of the time, Pallas kernels for 0%

commit v1 on v0

v1 whole, which is shorter than its diff:
```python
import jax
import jax.numpy as jnp
from jax import lax
from jax.experimental import pallas as pl
from jax.experimental.pallas import tpu as pltpu
from jax.sharding import PartitionSpec as P

CT_DEV = 32
EPS = 1e-12
CHUNKS = 8
META = 128
F32 = jnp.float32
BF16 = jnp.bfloat16
VMEM = pl.BlockSpec(memory_space=pltpu.VMEM)
SMEM = pl.BlockSpec(memory_space=pltpu.SMEM)
ANY = pl.BlockSpec(memory_space=pl.ANY)


def iota(shape, dim):
    return lax.broadcasted_iota(jnp.int32, shape, dim)


def onehot(mask):
    return jnp.where(mask, 1.0, 0.0).astype(BF16)


def dot(a, b, ca, cb):
    return lax.dot_general(a, b, (((ca,), (cb,)), ((), ())), preferred_element_type=F32)


def total(x):
    return jnp.sum(jnp.sum(x, axis=1, keepdims=True), axis=0, keepdims=True)


def load_pairs(ref, rows):
    return jnp.concatenate(
        [ref[pl.ds(0, rows, stride=2), :], ref[pl.ds(1, rows, stride=2), :]], axis=1
    )


def store_pairs(ref, value, rows):
    half = value.shape[1] // 2
    ref[pl.ds(0, rows, stride=2), :] = value[:, :half]
    ref[pl.ds(1, rows, stride=2), :] = value[:, half:]


def pieces(lane, value):
    high = value.astype(BF16).astype(F32)
    rest = value - high
    middle = rest.astype(BF16).astype(F32)
    low = rest - middle
    return jnp.where(lane == 1, high, jnp.where(lane == 2, middle, jnp.where(lane == 3, low, 0.0)))


def sum_pieces(meta, limit):
    lane = iota(meta.shape, 1)
    return total(jnp.where((lane >= 1) & (lane <= 3), meta, 0.0)) * (1.0 / limit)


def column_of(row):
    n = row.shape[1]
    return jnp.sum(jnp.where(iota((n, n), 0) == iota((n, n), 1), row, 0), axis=1, keepdims=True)


def placement(cols_ref, count_ref, npath, limit):
    cols = cols_ref[...]
    slots = cols.shape[1]
    owner = lax.div(cols, CT_DEV)
    inside = cols - owner * CT_DEV
    owner_col = column_of(owner)
    earlier = iota((slots, slots), 0) < iota((slots, slots), 1)
    same = (owner_col == owner) & earlier
    rank = jnp.sum(jnp.where(same, 1, 0), axis=0, keepdims=True)
    live = iota(cols.shape, 1) < count_ref[0]
    target = jnp.where(live, owner * limit + rank, -1)
    place = onehot(iota((npath * limit, slots), 0) == target)
    return place, inside


def start_tiles(tiles_ref, held, sems):
    step = held.shape[0] // CHUNKS
    copies = []
    for k in range(CHUNKS):
        part = pl.ds(k * step, step)
        copies.append(pltpu.make_async_copy(tiles_ref.at[part], held.at[part], sems.at[k]))
        copies[-1].start()
    return copies


def backward(copies, held, rows_ref, left):
    slots, tile = held.shape[0], held.shape[1]
    row_tiles = left.shape[0]
    row_hot = onehot(iota((row_tiles, slots), 0) == rows_ref[...])
    picked = dot(row_hot, left.astype(BF16), 0, 0)
    step = slots // CHUNKS
    sub = iota((step, tile), 0)
    out = []
    for k in range(CHUNKS):
        copies[k].wait()
        block = picked[k * step : (k + 1) * step]
        acc = jnp.zeros((step, tile), F32)
        for i in range(step):
            acc += dot(jnp.where(sub == i, block, 0.0).astype(BF16), held[k * step + i], 1, 0)
        out.append(acc.astype(BF16))
    return jnp.concatenate(out, axis=0)


def forward(copies, held, rows_ref, picked, row_tiles):
    slots, tile = held.shape[0], held.shape[1]
    step = slots // CHUNKS
    row_hot = jnp.where(iota((row_tiles, slots), 0) == rows_ref[...], 1.0, 0.0)
    acc = jnp.zeros((row_tiles, tile), F32)
    for k in range(CHUNKS):
        copies[k].wait()
        for i in range(step):
            s = k * step + i
            lhs = row_hot[:, s : s + 1] * picked[s : s + 1, :]
            acc += dot(lhs.astype(BF16), held[s], 1, 1)
    return acc


def send_terms(send_ref, place, inside, prods, norm):
    npath, limit, width = send_ref.shape
    slots, tile = prods.shape
    meta = jnp.where(iota((slots, META), 1) == 0, column_of(inside) + 1, 0)
    out = dot(place, jnp.concatenate([prods, meta.astype(F32).astype(BF16)], axis=1), 1, 0)
    lane = iota((npath * limit, META), 1)
    tail = out[:, tile:] + pieces(lane, norm)
    full = jnp.concatenate([out[:, :tile], tail], axis=1)
    send_ref[...] = full.astype(BF16).reshape(npath, limit, width)


def first_kernel(count_ref, rows_ref, cols_ref, data_ref, tiles_ref, send_ref, held, sems):
    npath, limit, _ = send_ref.shape
    copies = start_tiles(tiles_ref, held, sems)
    place, inside = placement(cols_ref, count_ref, npath, limit)
    left = load_pairs(data_ref, data_ref.shape[0] // 2)
    prods = backward(copies, held, rows_ref, left)
    send_terms(send_ref, place, inside, prods, total(left * left))


def owner_parts(recv_ref, index_ref):
    npath, limit, width = recv_ref.shape
    rows = npath * limit
    tile = width - META
    recv = recv_ref[...].reshape(rows, width)
    index = index_ref[...].reshape(rows, width)[:, tile:].astype(F32)
    hot = onehot(index[:, 0:1].astype(jnp.int32) == iota((rows, CT_DEV), 1) + 1)
    own = dot(hot, recv[:, :tile], 0, 0)
    return hot, own, sum_pieces(recv[:, tile:].astype(F32), limit)


def answer(send_ref, hot, own, norm):
    npath, limit, width = send_ref.shape
    picked = dot(hot, own.astype(BF16), 1, 0)
    tail = pieces(iota((npath * limit, META), 1), norm)
    full = jnp.concatenate([picked, tail], axis=1)
    send_ref[...] = full.astype(BF16).reshape(npath, limit, width)


def spread(value):
    return jnp.broadcast_to(value, (1, META))


def first_owner_kernel(recv_ref, send_ref, own_ref, scal_ref):
    hot, own, norm = owner_parts(recv_ref, recv_ref)
    own_ref[...] = own
    scal_ref[...] = jnp.broadcast_to(norm, scal_ref.shape)
    answer(send_ref, hot, own, total(own * own))


def forward_kernel(count_ref, rows_ref, cols_ref, recv_ref, tiles_ref, out_ref, held, sems):
    npath, limit, width = recv_ref.shape
    tile = width - META
    copies = start_tiles(tiles_ref, held, sems)
    place, _ = placement(cols_ref, count_ref, npath, limit)
    recv = recv_ref[...].reshape(npath * limit, width)
    picked = dot(place, recv[:, :tile], 0, 0)
    norm = sum_pieces(recv[:, tile:].astype(F32), limit)
    row_tiles = out_ref.shape[0]
    acc = forward(copies, held, rows_ref, picked, row_tiles)
    out_ref[...] = jnp.concatenate([acc, jnp.broadcast_to(norm, (row_tiles, META))], axis=1)


def second_kernel(
    count_ref, rows_ref, cols_ref, data_ref, sums_ref, scal_ref, tiles_ref,
    send_ref, left_ref, out_scal_ref, held, sems,
):
    npath, limit, width = send_ref.shape
    tile = width - META
    copies = start_tiles(tiles_ref, held, sems)
    place, inside = placement(cols_ref, count_ref, npath, limit)
    beta_sq = scal_ref[0:1, 0:1] + EPS
    beta = jnp.sqrt(beta_sq)
    alpha = jnp.sqrt(sums_ref[0:1, tile : tile + 1] / beta_sq + EPS)
    data = load_pairs(data_ref, data_ref.shape[0] // 2)
    left = sums_ref[:, :tile] / (beta * alpha) - (alpha / beta) * data
    left_ref[...] = left
    out_scal_ref[...] = jnp.zeros_like(out_scal_ref)
    out_scal_ref[0:1, :] = spread(beta)
    out_scal_ref[1:2, :] = spread(alpha)
    prods = backward(copies, held, rows_ref, left)
    send_terms(send_ref, place, inside, prods, total(left * left))


def second_owner_kernel(recv_ref, index_ref, own_ref, scal_ref, send_ref, next_ref, out_scal_ref):
    hot, terms, norm = owner_parts(recv_ref, index_ref)
    beta0, alpha0 = scal_ref[0:1, 0:1], scal_ref[1:2, 0:1]
    beta1 = jnp.sqrt(norm + EPS)
    own = terms / beta1 - own_ref[...] * (beta1 / (beta0 * alpha0))
    next_ref[...] = own
    out_scal_ref[...] = jnp.broadcast_to(beta1, out_scal_ref.shape)
    answer(send_ref, hot, own, total(own * own))


def third_kernel(sums_ref, left_ref, beta_ref, send_ref, next_ref, alpha_ref):
    npath, limit, _ = send_ref.shape
    tile = left_ref.shape[1]
    alpha = jnp.sqrt(sums_ref[0:1, tile : tile + 1] + EPS)
    left = sums_ref[:, :tile] / alpha - left_ref[...] * (alpha / beta_ref[0:1, 0:1])
    next_ref[...] = left
    alpha_ref[...] = jnp.broadcast_to(alpha, alpha_ref.shape)
    tail = pieces(iota((npath * limit, META), 1), total(left * left))
    send_ref[...] = tail.astype(BF16).reshape(npath, limit, META)


def final_kernel(
    total_rows, recv_ref, left_ref, own0_ref, own1_ref, scal_ref, beta_ref, alpha_ref,
    solution_ref, out_ref,
):
    npath, limit, _ = recv_ref.shape
    norm = sum_pieces(recv_ref[...].astype(F32).reshape(npath * limit, META), limit)
    beta2 = jnp.sqrt(norm + EPS)
    beta0, alpha0 = scal_ref[0:1, 0:1], scal_ref[1:2, 0:1]
    beta1, alpha1 = beta_ref[0:1, 0:1], alpha_ref[0:1, 0:1]
    rho1 = jnp.sqrt(alpha0 * alpha0 + beta1 * beta1)
    cosine, sine = alpha0 / rho1, beta1 / rho1
    theta = sine * alpha1
    rhobar = -cosine * alpha1
    phi1, phibar = cosine * beta0, sine * beta0
    rho2 = jnp.sqrt(rhobar * rhobar + beta2 * beta2)
    phi2 = rhobar / rho2 * phibar
    right0 = own0_ref[...] / (beta0 * alpha0)
    right1 = own1_ref[...] / alpha1
    search = right1 - (theta / rho1) * right0
    answer_ = (phi1 / rho1) * right0 + (phi2 / rho2) * search
    store_pairs(solution_ref, answer_, answer_.shape[0])
    left = left_ref[...] * (total_rows**0.5 / beta2)
    store_pairs(out_ref, left, left.shape[0])


def call(kernel, ins, outs, scratch=(), flops=0, moved=0):
    shapes = [jax.ShapeDtypeStruct(s, d) for s, d in outs]
    return pl.pallas_call(
        kernel,
        in_specs=ins,
        out_specs=[VMEM] * len(outs),
        out_shape=shapes,
        scratch_shapes=scratch,
        cost_estimate=pl.CostEstimate(flops=flops, bytes_accessed=moved, transcendentals=0),
    )


def on_device(tiles, tile_rows, tile_cols, tile_counts, data):
    slots, tile, _ = tiles.shape
    row_tiles = data.shape[0] // tile
    npath = lax.axis_size("path")
    limit = max(2, max(slots // 8, (slots + npath - 1) // npath))
    width = tile + META
    rows = tile_rows.reshape(1, slots)
    cols = tile_cols.reshape(1, slots)
    data = data.reshape(row_tiles * 2, tile // 2)
    held = [pltpu.VMEM(tiles.shape, tiles.dtype), pltpu.SemaphoreType.DMA((CHUNKS,))]
    payload = ((npath, limit, width), BF16)
    scal = ((8, META), F32)
    own_shape = ((CT_DEV, tile), F32)
    left_shape = ((row_tiles, tile), F32)
    work = dict(scratch=held, flops=2 * 8 * tiles.size, moved=2 * tiles.size)

    def swap(x):
        return lax.all_to_all(x, "path", 0, 0, tiled=True)

    (send,) = call(first_kernel, [SMEM, VMEM, VMEM, VMEM, ANY], [payload], **work)(
        tile_counts, rows, cols, data, tiles
    )
    index = swap(send)
    send, own0, scal0 = call(first_owner_kernel, [VMEM], [payload, own_shape, scal])(index)
    recv = swap(send)
    pass_forward = call(
        forward_kernel, [SMEM, VMEM, VMEM, VMEM, ANY], [((row_tiles, width), F32)], **work
    )
    (part,) = pass_forward(tile_counts, rows, cols, recv, tiles)
    sums = lax.psum(part, "mp")
    send, left, scal1 = call(
        second_kernel, [SMEM] + [VMEM] * 5 + [ANY], [payload, left_shape, scal], **work
    )(tile_counts, rows, cols, data, sums, scal0, tiles)
    recv = swap(send)
    send, own1, beta1 = call(second_owner_kernel, [VMEM] * 4, [payload, own_shape, scal])(
        recv, index, own0, scal1
    )
    recv = swap(send)
    (part,) = pass_forward(tile_counts, rows, cols, recv, tiles)
    sums = lax.psum(part, "mp")
    send, left, alpha1 = call(
        third_kernel, [VMEM] * 3, [((npath, limit, META), BF16), left_shape, scal]
    )(sums, left, beta1)
    recv = swap(send)
    total_rows = row_tiles * tile * npath

    def last(*refs):
        final_kernel(total_rows, *refs)

    solution, left = call(
        last, [VMEM] * 7, [((CT_DEV * 2, tile // 2), F32), ((row_tiles * 2, tile // 2), F32)]
    )(recv, left, own0, own1, scal1, beta1, alpha1)
    return solution.reshape(-1), left.reshape(-1)


def solution(mesh):
    placed = (
        P(("path", "mp"), None, None),
        P(("path", "mp")),
        P(("path", "mp")),
        P(("path", "mp")),
        P(("period", "path")),
    )
    return jax.shard_map(
        on_device,
        mesh=mesh,
        in_specs=placed,
        out_specs=(P(("period", "path", "mp")), P(("period", "path"))),
        check_vma=False,
    )
```

time: 918 us -> 130 us (0.14)
  blocking collectives: 571 us -> 93.8 us
  waiting for transfers between devices: 287 us -> 0 us
  Pallas kernels: 0 us -> 34.3 us
  matrix products: 21.9 us -> 0 us
  between operations: 19.3 us -> 1.31 us
  other arithmetic: 10.3 us -> 0 us
    psum x7 -> x2, blocking collectives: 478 us -> 9.16 us  [on_device(): sums = lax.psum(part, 'mp')]
    unnamed x4 -> x0, waiting for transfers between devices: 287 us -> none
    all_gather x2 -> x0, blocking collectives: 92.6 us -> none  [on_device(): lax.all_gather(state.astype(jnp.bfloat16), 'path', axis=0, tiled=True)]
    all_to_all x0 -> x5, blocking collectives: none -> 84.7 us  [swap(): return lax.all_to_all(x, 'path', 0, 0, tiled=True)]
    pallas_call x0 -> x8, Pallas kernels: none -> 34.3 us  [the longest x2 14.9 us: on_device(): part, = pass_forward(tile_counts, rows, cols, recv, tiles)]
    dot_general x8 -> x0, matrix products: 21.9 us -> none  [the longest x2 11.3 us: forward_prods(): jnp.einsum('sij,sj->si', tiles, picked, preferred_element_type=jnp.float32)]
  transfers between devices with their start and end apart: 2 -> 0, of which waited for: 2 -> 0; matrix products, arithmetic and copies ran while one was open for 0% -> 0% of each run, Pallas kernels for 0% -> 0%
where the time goes in v1:
time: 130 us; the launch traced here: 129 us
  blocking collectives  93.8 us (72%)
  Pallas kernels  34.3 us (26%)
  between operations  1.31 us (1%)
    all_to_all x5, blocking collectives, swap(): return lax.all_to_all(x, 'path', 0, 0, tiled=True)  84.7 us
    pallas_call x2, Pallas kernels, on_device(): part, = pass_forward(tile_counts, rows, cols, recv, tiles)  14.9 us
    psum x2, blocking collectives, on_device(): sums = lax.psum(part, 'mp')  9.16 us
    pallas_call x1, Pallas kernels, on_device(): call(second_kernel, [SMEM] + [VMEM] * 5 + [ANY], [payload, left_shape, sc...  5.99 us
    pallas_call x1, Pallas kernels, on_device(): call(first_kernel, [SMEM, VMEM, VMEM, VMEM, ANY], [payload], **work)  5.98 us

profile of v1, /device:TPU:16, one launch (start us, length us, event | category | flops | bytes accessed | tf_op | source)
XLA Modules:
  0.0 129.4 jit_solution(4802404066998599174)
XLA Ops:
  1.3 6.0 %shard_map.68 = bf16[32,8,384]{2,1,0:T(8,128)(2,1)} custom-call(s32[1]{0:T(128)S(6)} %copy.7.count_ref, s32[1,64]{1,0:T(1,128)} %bitcast.7, s32[1,64]{1,0:T(1,128)} %bitcast.11, f32[16,128]{1,0:T(8,128)} %bitcast.5, bf16[64,256,256]{2,1,0:T(8,128)(2,1)} %tiles_ref.7), custom_call_target="tpu_custom_call" | custom-call | flops 67108864 | bytes 8388608 | tf_op jit(solution)/shard_map/pallas_call | solution.py:283
  7.3 22.7 %all_to_all.25.recv_ref.index_ref = bf16[32,8,384]{2,1,0:T(8,128)(2,1)} all-to-all(bf16[32,8,384]{2,1,0:T(8,128)(2,1)} %shard_map.68), channel_id=1, replica_groups=mesh['path'=32,'mp'=2,'period'=4] {'path'}, dimensions={0} | all-to-all | bytes 393216 | tf_op jit(solution)/shard_map/all_to_all | solution.py:281
  30.0 2.0 %shard_map.69 = (bf16[32,8,384]{2,1,0:T(8,128)(2,1)}, f32[32,256]{1,0:T(8,128)}, f32[8,128]{1,0:T(8,128)}) custom-call(bf16[32,8,384]{2,1,0:T(8,128)(2,1)} %all_to_all.25.recv_ref.index_ref), custom_call_target="tpu_custom_call" | custom-call | tf_op jit(solution)/shard_map/pallas_call | solution.py:287
  32.1 15.3 %all_to_all.26.recv_ref = bf16[32,8,384]{2,1,0:T(8,128)(2,1)} all-to-all(bf16[32,8,384]{2,1,0:T(8,128)(2,1)} %get-tuple-element.16), channel_id=1, replica_groups=mesh['path'=32,'mp'=2,'period'=4] {'path'}, dimensions={0} | all-to-all | bytes 393216 | tf_op jit(solution)/shard_map/all_to_all | solution.py:281
  47.3 7.4 %shard_map.70 = f32[8,384]{1,0:T(8,128)} custom-call(s32[1]{0:T(128)S(6)} %copy.7.count_ref, s32[1,64]{1,0:T(1,128)} %bitcast.8, s32[1,64]{1,0:T(1,128)} %bitcast.12, bf16[32,8,384]{2,1,0:T(8,128)(2,1)} %all_to_all.26.recv_ref, bf16[64,256,256]{2,1,0:T(8,128)(2,1)} %tiles_ref.7), custom_call_target="tpu_custom_call" | custom-call | flops 67108864 | bytes 8388608 | tf_op jit(solution)/shard_map/pallas_call | solution.py:292
  54.8 4.6 %psum.14.sums_ref = f32[8,384]{1,0:T(8,128)} all-reduce(f32[8,384]{1,0:T(8,128)} %shard_map.70), channel_id=1, replica_groups=mesh['path'=32,'mp'=2,'period'=4] {'mp'}, use_global_device_ids=true, to_apply=%region_0.0 | all-reduce | flops 3072 | bytes 24576 | tf_op jit(solution)/shard_map/psum | solution.py:293
  59.4 6.0 %shard_map.71 = (bf16[32,8,384]{2,1,0:T(8,128)(2,1)}, f32[8,256]{1,0:T(8,128)}, f32[8,128]{1,0:T(8,128)}) custom-call(s32[1]{0:T(128)S(6)} %copy.7.count_ref, s32[1,64]{1,0:T(1,128)} %bitcast.9, s32[1,64]{1,0:T(1,128)} %bitcast.13, f32[16,128]{1,0:T(8,128)} %bitcast.6, f32[8,384]{1,0:T(8,128)} %psum.14.sums_ref, f32[8,128]{1,0:T(8,128)} %get-tuple-element.17.scal_ref, ...), custom_call_target="tpu_custom_call" | custom-call | flops 67108864 | bytes 8388608 | tf_op jit(solution)/shard_map/pallas_call | solution.py:294
  65.4 16.6 %all_to_all.27.recv_ref = bf16[32,8,384]{2,1,0:T(8,128)(2,1)} all-to-all(bf16[32,8,384]{2,1,0:T(8,128)(2,1)} %get-tuple-element.18), channel_id=1, replica_groups=mesh['path'=32,'mp'=2,'period'=4] {'path'}, dimensions={0} | all-to-all | bytes 393216 | tf_op jit(solution)/shard_map/all_to_all | solution.py:281
  81.9 2.1 %shard_map.72 = (bf16[32,8,384]{2,1,0:T(8,128)(2,1)}, f32[32,256]{1,0:T(8,128)}, f32[8,128]{1,0:T(8,128)}) custom-call(bf16[32,8,384]{2,1,0:T(8,128)(2,1)} %all_to_all.27.recv_ref, bf16[32,8,384]{2,1,0:T(8,128)(2,1)} %all_to_all.25.recv_ref.index_ref, f32[32,256]{1,0:T(8,128)} %get-tuple-element.19.own_ref.refs_2_, f32[8,128]{1,0:T(8,128)} %get-tuple-element.20.scal_ref.refs_4_), custom_call_target="tpu_custom_call" | custom-call | tf_op jit(solution)/shard_map/pallas_call | solution.py:298
  84.1 15.5 %all_to_all.28.recv_ref = bf16[32,8,384]{2,1,0:T(8,128)(2,1)} all-to-all(bf16[32,8,384]{2,1,0:T(8,128)(2,1)} %get-tuple-element.21), channel_id=1, replica_groups=mesh['path'=32,'mp'=2,'period'=4] {'path'}, dimensions={0} | all-to-all | bytes 393216 | tf_op jit(solution)/shard_map/all_to_all | solution.py:281
  99.6 7.4 %shard_map.73 = f32[8,384]{1,0:T(8,128)} custom-call(s32[1]{0:T(128)S(6)} %copy.7.count_ref, s32[1,64]{1,0:T(1,128)} %bitcast.10, s32[1,64]{1,0:T(1,128)} %bitcast.14, bf16[32,8,384]{2,1,0:T(8,128)(2,1)} %all_to_all.28.recv_ref, bf16[64,256,256]{2,1,0:T(8,128)(2,1)} %tiles_ref.7), custom_call_target="tpu_custom_call" | custom-call | flops 67108864 | bytes 8388608 | tf_op jit(solution)/shard_map/pallas_call | solution.py:302
  107.0 4.6 %psum.15.sums_ref = f32[8,384]{1,0:T(8,128)} all-reduce(f32[8,384]{1,0:T(8,128)} %shard_map.73), channel_id=1, replica_groups=mesh['path'=32,'mp'=2,'period'=4] {'mp'}, use_global_device_ids=true, to_apply=%region_1.0 | all-reduce | flops 3072 | bytes 24576 | tf_op jit(solution)/shard_map/psum | solution.py:303
  111.6 1.5 %shard_map.74 = (bf16[32,8,128]{2,1,0:T(8,128)(2,1)}, f32[8,256]{1,0:T(8,128)}, f32[8,128]{1,0:T(8,128)}) custom-call(f32[8,384]{1,0:T(8,128)} %psum.15.sums_ref, f32[8,256]{1,0:T(8,128)} %get-tuple-element.22.left_ref, f32[8,128]{1,0:T(8,128)} %get-tuple-element.23.beta_ref.refs_5_), custom_call_target="tpu_custom_call" | custom-call | tf_op jit(solution)/shard_map/pallas_call | solution.py:304
  113.1 14.6 %all_to_all.29.refs_0_ = bf16[32,8,128]{2,1,0:T(8,128)(2,1)} all-to-all(bf16[32,8,128]{2,1,0:T(8,128)(2,1)} %get-tuple-element.24), channel_id=1, replica_groups=mesh['path'=32,'mp'=2,'period'=4] {'path'}, dimensions={0} | all-to-all | bytes 131072 | tf_op jit(solution)/shard_map/all_to_all | solution.py:281
  127.7 1.7 %shard_map.75 = (f32[64,128]{1,0:T(8,128)}, f32[16,128]{1,0:T(8,128)}) custom-call(bf16[32,8,128]{2,1,0:T(8,128)(2,1)} %all_to_all.29.refs_0_, f32[8,256]{1,0:T(8,128)} %get-tuple-element.25.refs_1_, f32[32,256]{1,0:T(8,128)} %get-tuple-element.19.own_ref.refs_2_, f32[32,256]{1,0:T(8,128)} %get-tuple-element.26.refs_3_, ...), custom_call_target="tpu_custom_call" | custom-call | tf_op jit(solution)/shard_map/pallas_call | solution.py:313

commit v2 on v1

--- a/solution.py
+++ b/solution.py
@@ -9,11 +9,13 @@
 EPS = 1e-12
 CHUNKS = 8
 META = 128
+LIMIT = 12 << 20
+FIRST_LIMIT = 50 << 20
 F32 = jnp.float32
 BF16 = jnp.bfloat16
 VMEM = pl.BlockSpec(memory_space=pltpu.VMEM)
 SMEM = pl.BlockSpec(memory_space=pltpu.SMEM)
-ANY = pl.BlockSpec(memory_space=pl.ANY)
+HBM = pl.BlockSpec(memory_space=pltpu.HBM)
 
 
 def iota(shape, dim):
@@ -87,7 +89,7 @@
     return copies
 
 
-def backward(copies, held, rows_ref, left):
+def backward(held, rows_ref, left, copies=None):
     slots, tile = held.shape[0], held.shape[1]
     row_tiles = left.shape[0]
     row_hot = onehot(iota((row_tiles, slots), 0) == rows_ref[...])
@@ -96,7 +98,8 @@
     sub = iota((step, tile), 0)
     out = []
     for k in range(CHUNKS):
-        copies[k].wait()
+        if copies is not None:
+            copies[k].wait()
         block = picked[k * step : (k + 1) * step]
         acc = jnp.zeros((step, tile), F32)
         for i in range(step):
@@ -105,13 +108,12 @@
     return jnp.concatenate(out, axis=0)
 
 
-def forward(copies, held, rows_ref, picked, row_tiles):
+def forward(held, rows_ref, picked, row_tiles):
     slots, tile = held.shape[0], held.shape[1]
     step = slots // CHUNKS
     row_hot = jnp.where(iota((row_tiles, slots), 0) == rows_ref[...], 1.0, 0.0)
     acc = jnp.zeros((row_tiles, tile), F32)
     for k in range(CHUNKS):
-        copies[k].wait()
         for i in range(step):
             s = k * step + i
             lhs = row_hot[:, s : s + 1] * picked[s : s + 1, :]
@@ -130,12 +132,12 @@
     send_ref[...] = full.astype(BF16).reshape(npath, limit, width)
 
 
-def first_kernel(count_ref, rows_ref, cols_ref, data_ref, tiles_ref, send_ref, held, sems):
+def first_kernel(count_ref, rows_ref, cols_ref, data_ref, tiles_ref, send_ref, held_ref, sems):
     npath, limit, _ = send_ref.shape
-    copies = start_tiles(tiles_ref, held, sems)
+    copies = start_tiles(tiles_ref, held_ref, sems)
     place, inside = placement(cols_ref, count_ref, npath, limit)
     left = load_pairs(data_ref, data_ref.shape[0] // 2)
-    prods = backward(copies, held, rows_ref, left)
+    prods = backward(held_ref, rows_ref, left, copies)
     send_terms(send_ref, place, inside, prods, total(left * left))
 
 
@@ -169,37 +171,36 @@
     answer(send_ref, hot, own, total(own * own))
 
 
-def forward_kernel(count_ref, rows_ref, cols_ref, recv_ref, tiles_ref, out_ref, held, sems):
+def forward_kernel(count_ref, rows_ref, cols_ref, recv_ref, tiles_ref, out_ref):
     npath, limit, width = recv_ref.shape
     tile = width - META
-    copies = start_tiles(tiles_ref, held, sems)
     place, _ = placement(cols_ref, count_ref, npath, limit)
     recv = recv_ref[...].reshape(npath * limit, width)
     picked = dot(place, recv[:, :tile], 0, 0)
     norm = sum_pieces(recv[:, tile:].astype(F32), limit)
     row_tiles = out_ref.shape[0]
-    acc = forward(copies, held, rows_ref, picked, row_tiles)
+    acc = forward(tiles_ref, rows_ref, picked, row_tiles)
     out_ref[...] = jnp.concatenate([acc, jnp.broadcast_to(norm, (row_tiles, META))], axis=1)
 
 
 def second_kernel(
-    count_ref, rows_ref, cols_ref, data_ref, sums_ref, scal_ref, tiles_ref,
-    send_ref, left_ref, out_scal_ref, held, sems,
+    count_ref, rows_ref, cols_ref, data_ref, part_ref, other_ref, scal_ref, tiles_ref,
+    send_ref, left_ref, out_scal_ref,
 ):
     npath, limit, width = send_ref.shape
     tile = width - META
-    copies = start_tiles(tiles_ref, held, sems)
     place, inside = placement(cols_ref, count_ref, npath, limit)
+    sums = part_ref[...] + other_ref[...]
     beta_sq = scal_ref[0:1, 0:1] + EPS
     beta = jnp.sqrt(beta_sq)
-    alpha = jnp.sqrt(sums_ref[0:1, tile : tile + 1] / beta_sq + EPS)
+    alpha = jnp.sqrt(sums[0:1, tile : tile + 1] / beta_sq + EPS)
     data = load_pairs(data_ref, data_ref.shape[0] // 2)
-    left = sums_ref[:, :tile] / (beta * alpha) - (alpha / beta) * data
+    left = sums[:, :tile] / (beta * alpha) - (alpha / beta) * data
     left_ref[...] = left
     out_scal_ref[...] = jnp.zeros_like(out_scal_ref)
     out_scal_ref[0:1, :] = spread(beta)
     out_scal_ref[1:2, :] = spread(alpha)
-    prods = backward(copies, held, rows_ref, left)
+    prods = backward(tiles_ref, rows_ref, left)
     send_terms(send_ref, place, inside, prods, total(left * left))
 
 
@@ -213,11 +214,12 @@
     answer(send_ref, hot, own, total(own * own))
 
 
-def third_kernel(sums_ref, left_ref, beta_ref, send_ref, next_ref, alpha_ref):
+def third_kernel(part_ref, other_ref, left_ref, beta_ref, send_ref, next_ref, alpha_ref):
     npath, limit, _ = send_ref.shape
     tile = left_ref.shape[1]
-    alpha = jnp.sqrt(sums_ref[0:1, tile : tile + 1] + EPS)
-    left = sums_ref[:, :tile] / alpha - left_ref[...] * (alpha / beta_ref[0:1, 0:1])
+    sums = part_ref[...] + other_ref[...]
+    alpha = jnp.sqrt(sums[0:1, tile : tile + 1] + EPS)
+    left = sums[:, :tile] / alpha - left_ref[...] * (alpha / beta_ref[0:1, 0:1])
     next_ref[...] = left
     alpha_ref[...] = jnp.broadcast_to(alpha, alpha_ref.shape)
     tail = pieces(iota((npath * limit, META), 1), total(left * left))
@@ -249,7 +251,7 @@
     store_pairs(out_ref, left, left.shape[0])
 
 
-def call(kernel, ins, outs, scratch=(), flops=0, moved=0):
+def call(kernel, ins, outs, scratch=(), flops=0, moved=0, room=LIMIT):
     shapes = [jax.ShapeDtypeStruct(s, d) for s, d in outs]
     return pl.pallas_call(
         kernel,
@@ -257,6 +259,7 @@
         out_specs=[VMEM] * len(outs),
         out_shape=shapes,
         scratch_shapes=scratch,
+        compiler_params=pltpu.CompilerParams(vmem_limit_bytes=room),
         cost_estimate=pl.CostEstimate(flops=flops, bytes_accessed=moved, transcendentals=0),
     )
 
@@ -270,40 +273,45 @@
     rows = tile_rows.reshape(1, slots)
     cols = tile_cols.reshape(1, slots)
     data = data.reshape(row_tiles * 2, tile // 2)
-    held = [pltpu.VMEM(tiles.shape, tiles.dtype), pltpu.SemaphoreType.DMA((CHUNKS,))]
     payload = ((npath, limit, width), BF16)
     scal = ((8, META), F32)
     own_shape = ((CT_DEV, tile), F32)
     left_shape = ((row_tiles, tile), F32)
-    work = dict(scratch=held, flops=2 * 8 * tiles.size, moved=2 * tiles.size)
+    work = dict(flops=2 * 8 * tiles.size, moved=2 * tiles.size)
 
     def swap(x):
         return lax.all_to_all(x, "path", 0, 0, tiled=True)
 
-    (send,) = call(first_kernel, [SMEM, VMEM, VMEM, VMEM, ANY], [payload], **work)(
-        tile_counts, rows, cols, data, tiles
-    )
+    held = [pltpu.VMEM(tiles.shape, tiles.dtype), pltpu.SemaphoreType.DMA((CHUNKS,))]
+    (send,) = call(
+        first_kernel,
+        [SMEM, VMEM, VMEM, VMEM, HBM],
+        [payload],
+        scratch=held,
+        room=FIRST_LIMIT,
+        **work,
+    )(tile_counts, rows, cols, data, tiles)
     index = swap(send)
     send, own0, scal0 = call(first_owner_kernel, [VMEM], [payload, own_shape, scal])(index)
     recv = swap(send)
     pass_forward = call(
-        forward_kernel, [SMEM, VMEM, VMEM, VMEM, ANY], [((row_tiles, width), F32)], **work
+        forward_kernel, [SMEM, VMEM, VMEM, VMEM, VMEM], [((row_tiles, width), F32)], **work
     )
     (part,) = pass_forward(tile_counts, rows, cols, recv, tiles)
-    sums = lax.psum(part, "mp")
+    sums = (part, lax.ppermute(part, "mp", [(0, 1), (1, 0)]))
     send, left, scal1 = call(
-        second_kernel, [SMEM] + [VMEM] * 5 + [ANY], [payload, left_shape, scal], **work
-    )(tile_counts, rows, cols, data, sums, scal0, tiles)
+        second_kernel, [SMEM] + [VMEM] * 7, [payload, left_shape, scal], **work
+    )(tile_counts, rows, cols, data, *sums, scal0, tiles)
     recv = swap(send)
     send, own1, beta1 = call(second_owner_kernel, [VMEM] * 4, [payload, own_shape, scal])(
         recv, index, own0, scal1
     )
     recv = swap(send)
     (part,) = pass_forward(tile_counts, rows, cols, recv, tiles)
-    sums = lax.psum(part, "mp")
+    sums = (part, lax.ppermute(part, "mp", [(0, 1), (1, 0)]))
     send, left, alpha1 = call(
-        third_kernel, [VMEM] * 3, [((npath, limit, META), BF16), left_shape, scal]
-    )(sums, left, beta1)
+        third_kernel, [VMEM] * 4, [((npath, limit, META), BF16), left_shape, scal]
+    )(*sums, left, beta1)
     recv = swap(send)
     total_rows = row_tiles * tile * npath
 

time: 130 us -> 101 us (0.78)
  Pallas kernels: 34.3 us -> 12.9 us
  blocking collectives: 93.8 us -> 81.3 us
  local copies, waits for them, and re-layouts: 0 us -> 2.4 us
  waiting for transfers between devices: 0 us -> 2.33 us
    pallas_call x2, Pallas kernels: 14.9 us -> 4.98 us  [on_device(): part, = pass_forward(tile_counts, rows, cols, recv, tiles)]
    psum x2 -> x0, blocking collectives: 9.16 us -> none  [on_device(): sums = lax.psum(part, 'mp')]
    pallas_call x3, Pallas kernels: 13.5 us -> 6.26 us  [the longest x1 4.57 us: on_device(): call(first_kernel, [SMEM, VMEM, VMEM, VMEM, HBM], [payload], scratch=held...]
    all_to_all x5, blocking collectives: 84.7 us -> 81.3 us  [swap(): return lax.all_to_all(x, 'path', 0, 0, tiled=True)]
    unnamed x0 -> x8, local copies, waits for them, and re-layouts: none -> 2.4 us
    ppermute x0 -> x2, waiting for transfers between devices: none -> 2.33 us  [on_device(): sums = (part, lax.ppermute(part, 'mp', [(0, 1), (1, 0)]))]
    pallas_call x1, Pallas kernels: 2.15 us -> 0.45 us  [on_device(): call(second_owner_kernel, [VMEM] * 4, [payload, own_shape, scal])]
    pallas_call x1, Pallas kernels: 2.05 us -> 0.44 us  [on_device(): call(first_owner_kernel, [VMEM], [payload, own_shape, scal])(index)]
  transfers between devices with their start and end apart: 0 -> 2, of which waited for: 0 -> 2; matrix products, arithmetic and copies ran while one was open for 0% -> 0% of each run, Pallas kernels for 0% -> 0%
where the time goes in v2:
time: 101 us; the launch traced here: 100 us
  blocking collectives  81.3 us (80%)
  Pallas kernels  12.9 us (13%)
  local copies, waits for them, and re-layouts  2.4 us (2%)
  waiting for transfers between devices  2.33 us (2%)
  between operations  1.5 us (1%)
    all_to_all x5, blocking collectives, swap(): return lax.all_to_all(x, 'path', 0, 0, tiled=True)  81.3 us
    pallas_call x2, Pallas kernels, on_device(): part, = pass_forward(tile_counts, rows, cols, recv, tiles)  4.98 us
    pallas_call x1, Pallas kernels, on_device(): call(first_kernel, [SMEM, VMEM, VMEM, VMEM, HBM], [payload], scratch=held...  4.57 us
    unnamed x8, local copies, waits for them, and re-layouts  2.4 us
    ppermute x2, waiting for transfers between devices, on_device(): sums = (part, lax.ppermute(part, 'mp', [(0, 1), (1, 0)]))  2.33 us
  transfers between devices with their start and end apart: 2, of which 2 were waited for; matrix products, arithmetic and copies ran while one was open for 0% of the time, Pallas kernels for 0%

profile of v2, /device:TPU:16, one launch (start us, length us, event | category | flops | bytes accessed | tf_op | source)
XLA Modules:
  0.0 100.4 jit_solution(11367686168005042887)
XLA Ops:
  0.6 0.0 copy-start
  1.4 0.0 copy-start.1
  1.4 0.8 copy-done.1
  2.2 0.0 copy-start.2
  2.2 0.9 copy-done.2
  3.2 0.0 copy-start.3
  3.2 0.7 copy-done.3
  3.8 4.6 %shard_map.68 = bf16[32,8,384]{2,1,0:T(8,128)(2,1)S(1)} custom-call(s32[1]{0:T(128)S(6)} %copy.7.count_ref, s32[1,64]{1,0:T(1,128)S(1)} %bitcast.7, s32[1,64]{1,0:T(1,128)S(1)} %bitcast.11, f32[16,128]{1,0:T(8,128)S(1)} %bitcast.5, bf16[64,256,256]{2,1,0:T(8,128)(2,1)} %tiles_ref.7), custom_call_target="tpu_custom_call" | custom-call | flops 67108864 | bytes 8388608 | tf_op jit(solution)/shard_map/pallas_call | solution.py:286
  8.4 22.4 %all_to_all.25.recv_ref.index_ref = bf16[32,8,384]{2,1,0:T(8,128)(2,1)S(1)} all-to-all(bf16[32,8,384]{2,1,0:T(8,128)(2,1)S(1)} %shard_map.68), channel_id=1, replica_groups=mesh['path'=32,'mp'=2,'period'=4] {'path'}, dimensions={0} | all-to-all | bytes 393216 | tf_op jit(solution)/shard_map/all_to_all | solution.py:283
  30.8 0.4 shard_map.69
  31.3 14.8 %all_to_all.26.recv_ref = bf16[32,8,384]{2,1,0:T(8,128)(2,1)S(1)} all-to-all(bf16[32,8,384]{2,1,0:T(8,128)(2,1)S(1)} %get-tuple-element.16), channel_id=1, replica_groups=mesh['path'=32,'mp'=2,'period'=4] {'path'}, dimensions={0} | all-to-all | bytes 393216 | tf_op jit(solution)/shard_map/all_to_all | solution.py:283
  46.0 0.0 copy-done
  46.1 2.5 %shard_map.70.part_ref = f32[8,384]{1,0:T(8,128)S(1)} custom-call(s32[1]{0:T(128)S(6)} %copy.7.count_ref, s32[1,64]{1,0:T(1,128)S(1)} %bitcast.8, s32[1,64]{1,0:T(1,128)S(1)} %bitcast.12, bf16[32,8,384]{2,1,0:T(8,128)(2,1)S(1)} %all_to_all.26.recv_ref, bf16[64,256,256]{2,1,0:T(8,128)(2,1)S(1)} %copy-done), custom_call_target="tpu_custom_call" | custom-call | flops 67108864 | bytes 8388608 | tf_op jit(solution)/shard_map/pallas_call | solution.py:300
  48.5 0.0 collective-permute-start
  48.6 1.2 %collective-permute-done.other_ref = f32[8,384]{1,0:T(8,128)S(1)} collective-permute-done((f32[8,384]{1,0:T(8,128)S(1)}, f32[8,384]{1,0:T(8,128)S(1)}, u32[]{:S(2)}, u32[]{:S(2)}) %collective-permute-start) | collective-permute-done | bytes 12320 | tf_op jit(solution)/shard_map/ppermute | solution.py:301
  49.7 1.5 %shard_map.71 = (bf16[32,8,384]{2,1,0:T(8,128)(2,1)S(1)}, f32[8,256]{1,0:T(8,128)S(1)}, f32[8,128]{1,0:T(8,128)S(1)}) custom-call(s32[1]{0:T(128)S(6)} %copy.7.count_ref, s32[1,64]{1,0:T(1,128)S(1)} %bitcast.9, s32[1,64]{1,0:T(1,128)S(1)} %bitcast.13, f32[16,128]{1,0:T(8,128)S(1)} %bitcast.6, f32[8,384]{1,0:T(8,128)S(1)} %shard_map.70.part_ref, ...), custom_call_target="tpu_custom_call" | custom-call | flops 67108864 | bytes 8388608 | tf_op jit(solution)/shard_map/pallas_call | solution.py:302
  51.3 15.5 %all_to_all.27.recv_ref = bf16[32,8,384]{2,1,0:T(8,128)(2,1)S(1)} all-to-all(bf16[32,8,384]{2,1,0:T(8,128)(2,1)S(1)} %get-tuple-element.18), channel_id=1, replica_groups=mesh['path'=32,'mp'=2,'period'=4] {'path'}, dimensions={0} | all-to-all | bytes 393216 | tf_op jit(solution)/shard_map/all_to_all | solution.py:283
  66.8 0.4 shard_map.72
  67.3 14.7 %all_to_all.28.recv_ref = bf16[32,8,384]{2,1,0:T(8,128)(2,1)S(1)} all-to-all(bf16[32,8,384]{2,1,0:T(8,128)(2,1)S(1)} %get-tuple-element.21), channel_id=1, replica_groups=mesh['path'=32,'mp'=2,'period'=4] {'path'}, dimensions={0} | all-to-all | bytes 393216 | tf_op jit(solution)/shard_map/all_to_all | solution.py:283
  82.0 2.5 %shard_map.73.part_ref = f32[8,384]{1,0:T(8,128)S(1)} custom-call(s32[1]{0:T(128)S(6)} %copy.7.count_ref, s32[1,64]{1,0:T(1,128)S(1)} %bitcast.10, s32[1,64]{1,0:T(1,128)S(1)} %bitcast.14, bf16[32,8,384]{2,1,0:T(8,128)(2,1)S(1)} %all_to_all.28.recv_ref, bf16[64,256,256]{2,1,0:T(8,128)(2,1)S(1)} %copy-done), custom_call_target="tpu_custom_call" | custom-call | flops 67108864 | bytes 8388608 | tf_op jit(solution)/shard_map/pallas_call | solution.py:310
  84.5 0.0 collective-permute-start.1
  84.5 1.2 %collective-permute-done.1.other_ref = f32[8,384]{1,0:T(8,128)S(1)} collective-permute-done((f32[8,384]{1,0:T(8,128)S(1)}, f32[8,384]{1,0:T(8,128)S(1)}, u32[]{:S(2)}, u32[]{:S(2)}) %collective-permute-start.1) | collective-permute-done | bytes 12320 | tf_op jit(solution)/shard_map/ppermute | solution.py:311
  85.7 0.1 shard_map.74
  85.8 13.8 %all_to_all.29.refs_0_ = bf16[32,8,128]{2,1,0:T(8,128)(2,1)S(1)} all-to-all(bf16[32,8,128]{2,1,0:T(8,128)(2,1)S(1)} %get-tuple-element.24), channel_id=1, replica_groups=mesh['path'=32,'mp'=2,'period'=4] {'path'}, dimensions={0} | all-to-all | bytes 131072 | tf_op jit(solution)/shard_map/all_to_all | solution.py:283
  99.6 0.8 shard_map.75
Async XLA Ops:
  0.6 45.4 %copy-start = (bf16[64,256,256]{2,1,0:T(8,128)(2,1)S(1)}, bf16[64,256,256]{2,1,0:T(8,128)(2,1)}, u32[]{:S(2)}) copy-start(bf16[64,256,256]{2,1,0:T(8,128)(2,1)} %tiles_ref.7) | copy-start | bytes 25165828
  1.4 0.8 copy-start.1
  2.2 0.9 copy-start.2
  3.2 0.7 copy-start.3
  48.5 1.2 %collective-permute-start = (f32[8,384]{1,0:T(8,128)S(1)}, f32[8,384]{1,0:T(8,128)S(1)}, u32[]{:S(2)}, u32[]{:S(2)}) collective-permute-start(f32[8,384]{1,0:T(8,128)S(1)} %shard_map.70.part_ref), channel_id=1, source_target_pairs={{0,4},{4,0},{1,5},{5,1},{2,6},{6,2},{3,7},{7,3},{8,12},{12,8},{9,1... | collective-permute-start | bytes 36872 | tf_op jit(solution)/shard_map/ppermute | solution.py:301
  84.5 1.2 %collective-permute-start.1 = (f32[8,384]{1,0:T(8,128)S(1)}, f32[8,384]{1,0:T(8,128)S(1)}, u32[]{:S(2)}, u32[]{:S(2)}) collective-permute-start(f32[8,384]{1,0:T(8,128)S(1)} %shard_map.73.part_ref), channel_id=1, source_target_pairs={{0,4},{4,0},{1,5},{5,1},{2,6},{6,2},{3,7},{7,3},{8,12},{12,8},{9,1... | collective-permute-start | bytes 36872 | tf_op jit(solution)/shard_map/ppermute | solution.py:311

commit v3 on v2

v3 whole, which is shorter than its diff:
```python
import jax
import jax.numpy as jnp
from jax import lax
from jax.experimental import pallas as pl
from jax.experimental.pallas import tpu as pltpu
from jax.sharding import PartitionSpec as P

CT_DEV = 32
EPS = 1e-12
CHUNKS = 8
META = 128
LIMIT = 12 << 20
FIRST_LIMIT = 50 << 20
F32 = jnp.float32
BF16 = jnp.bfloat16
VMEM = pl.BlockSpec(memory_space=pltpu.VMEM)
SMEM = pl.BlockSpec(memory_space=pltpu.SMEM)
HBM = pl.BlockSpec(memory_space=pltpu.HBM)


def iota(shape, dim):
    return lax.broadcasted_iota(jnp.int32, shape, dim)


def onehot(mask):
    return jnp.where(mask, 1.0, 0.0).astype(BF16)


def dot(a, b, ca, cb):
    return lax.dot_general(a, b, (((ca,), (cb,)), ((), ())), preferred_element_type=F32)


def total(x):
    return jnp.sum(jnp.sum(x, axis=1, keepdims=True), axis=0, keepdims=True)


def load_pairs(ref, rows):
    return jnp.concatenate(
        [ref[pl.ds(0, rows, stride=2), :], ref[pl.ds(1, rows, stride=2), :]], axis=1
    )


def store_pairs(ref, value, rows):
    half = value.shape[1] // 2
    ref[pl.ds(0, rows, stride=2), :] = value[:, :half]
    ref[pl.ds(1, rows, stride=2), :] = value[:, half:]


def pieces(lane, value):
    high = value.astype(BF16).astype(F32)
    rest = value - high
    middle = rest.astype(BF16).astype(F32)
    low = rest - middle
    return jnp.where(lane == 1, high, jnp.where(lane == 2, middle, jnp.where(lane == 3, low, 0.0)))


def sum_pieces(meta):
    lane = iota(meta.shape, 1)
    return total(jnp.where((lane >= 1) & (lane <= 3), meta, 0.0))


def split(x):
    high = x.astype(BF16)
    low = (x - high.astype(F32)).astype(BF16)
    return jnp.concatenate([high, low], axis=0)


def fold(x):
    half = x.shape[0] // 2
    return x[:half] + x[half:]


def start_tiles(tiles_ref, held, sems):
    step = held.shape[0] // CHUNKS
    copies = []
    for k in range(CHUNKS):
        part = pl.ds(k * step, step)
        copies.append(pltpu.make_async_copy(tiles_ref.at[part], held.at[part], sems.at[k]))
        copies[-1].start()
    return copies


def backward(held, rows_ref, left, copies=None):
    slots, tile = held.shape[0], held.shape[1]
    row_tiles = left.shape[0]
    row_hot = onehot(iota((row_tiles, slots), 0) == rows_ref[...])
    both = split(left)
    high = dot(row_hot, both[:row_tiles], 0, 0)
    low = dot(row_hot, both[row_tiles:], 0, 0)
    step = slots // CHUNKS
    sub = iota((2 * step, tile), 0)
    out = []
    for k in range(CHUNKS):
        if copies is not None:
            copies[k].wait()
        part = slice(k * step, (k + 1) * step)
        block = jnp.concatenate([high[part], low[part]], axis=0)
        acc = jnp.zeros((2 * step, tile), F32)
        for i in range(step):
            mine = (sub == i) | (sub == i + step)
            acc += dot(jnp.where(mine, block, 0.0).astype(BF16), held[k * step + i], 1, 0)
        out.append(fold(acc).astype(BF16))
    return jnp.concatenate(out, axis=0)


def forward(held, rows_ref, picked, row_tiles):
    slots, tile = held.shape[0], held.shape[1]
    row_hot = jnp.where(iota((row_tiles, slots), 0) == rows_ref[...], 1.0, 0.0)
    acc = jnp.zeros((2 * row_tiles, tile), F32)
    for s in range(slots):
        lhs = split(row_hot[:, s : s + 1] * picked[s : s + 1, :])
        acc += dot(lhs, held[s], 1, 1)
    return fold(acc)


def cell_of(cols_ref, count_ref):
    cols = cols_ref[...]
    owner = lax.div(cols, CT_DEV)
    live = iota(cols.shape, 1) < count_ref[0]
    return jnp.where(live, owner + 1, 0), cols - owner * CT_DEV


def send_terms(send_ref, cols_ref, count_ref, prods, norm):
    npath = send_ref.shape[0]
    half = prods.shape[1] // 2
    owner, inside = cell_of(cols_ref, count_ref)
    index = jnp.concatenate([owner, inside], axis=1).astype(F32)
    sub, lane = iota((8, META), 0), iota((8, META), 1)
    meta = jnp.where(sub == 0, index, jnp.where(sub == 1, pieces(lane, norm), 0.0))
    message = jnp.concatenate([prods[:, :half], prods[:, half:], meta.astype(BF16)], axis=0)
    for q in range(npath):
        send_ref[q] = message


def first_kernel(count_ref, rows_ref, cols_ref, data_ref, tiles_ref, send_ref, held_ref, sems):
    copies = start_tiles(tiles_ref, held_ref, sems)
    left = load_pairs(data_ref, data_ref.shape[0] // 2)
    prods = backward(held_ref, rows_ref, left, copies)
    send_terms(send_ref, cols_ref, count_ref, prods, total(left * left))


def all_cells(recv_ref, index_ref, slots, full_ref):
    npath = recv_ref.shape[0]
    group = full_ref.shape[1] // slots
    acc = None
    norm = jnp.zeros((1, 1), F32)
    for b in range(npath // group):
        sources = range(b * group, (b + 1) * group)
        metas = [index_ref[q, 2 * slots :, :].astype(F32) for q in sources]
        norms = [recv_ref[q, 2 * slots :, :].astype(F32)[1:2] for q in sources]
        for n in norms:
            norm += sum_pieces(n)
        owner = jnp.concatenate([m[0:1, :slots] for m in metas], axis=1)
        inside = jnp.concatenate([m[0:1, slots:] for m in metas], axis=1)
        shape = (CT_DEV, group * slots)
        hot = jnp.where(iota(shape, 0).astype(F32) == inside, 1.0, 0.0)
        owner = jnp.broadcast_to(owner, shape)
        mask = jnp.concatenate(
            [jnp.where(owner == o + 1.0, hot, 0.0).astype(BF16) for o in range(npath)], axis=0
        )
        block = jnp.concatenate(
            [
                jnp.concatenate([recv_ref[q, :slots, :] for q in sources], axis=0),
                jnp.concatenate([recv_ref[q, slots : 2 * slots, :] for q in sources], axis=0),
            ],
            axis=1,
        )
        term = dot(mask, block, 1, 0)
        if b == 0:
            full_ref[...] = term
        else:
            full_ref[...] += term
    return norm


def pick(cols_ref, count_ref, full_ref):
    slots = cols_ref.shape[1]
    cells = full_ref.shape[0]
    live = iota((1, slots), 1) < count_ref[0]
    cell = jnp.where(live, cols_ref[...], -1)
    hot = onehot(iota((cells, slots), 0) == cell)
    full = full_ref[...]
    high = full.astype(BF16)
    low = (full - high.astype(F32)).astype(BF16)
    return dot(hot, high, 0, 0) + dot(hot, low, 0, 0)


def finish_forward(count_ref, rows_ref, cols_ref, full_ref, tiles_ref, part_ref, own_ref):
    row_tiles = part_ref.shape[0]
    full = full_ref[...]
    norm = total(full * full)
    acc = forward(tiles_ref, rows_ref, pick(cols_ref, count_ref, full_ref), row_tiles)
    part_ref[...] = jnp.concatenate([acc, jnp.broadcast_to(norm, (row_tiles, META))], axis=1)
    me = lax.axis_index("path")
    own_ref[...] = full_ref[pl.ds(pl.multiple_of(me * CT_DEV, CT_DEV), CT_DEV), :]


def spread(value):
    return jnp.broadcast_to(value, (1, META))


def first_forward_kernel(
    count_ref, rows_ref, cols_ref, recv_ref, tiles_ref, part_ref, full_ref, own_ref, scal_ref
):
    norm = all_cells(recv_ref, recv_ref, tiles_ref.shape[0], full_ref)
    scal_ref[...] = jnp.broadcast_to(norm, scal_ref.shape)
    finish_forward(count_ref, rows_ref, cols_ref, full_ref, tiles_ref, part_ref, own_ref)


def second_kernel(
    count_ref, rows_ref, cols_ref, data_ref, part_ref, other_ref, scal_ref, tiles_ref,
    send_ref, left_ref, out_scal_ref,
):
    tile = left_ref.shape[1]
    sums = part_ref[...] + other_ref[...]
    beta_sq = scal_ref[0:1, 0:1] + EPS
    beta = jnp.sqrt(beta_sq)
    alpha = jnp.sqrt(sums[0:1, tile : tile + 1] / beta_sq + EPS)
    data = load_pairs(data_ref, data_ref.shape[0] // 2)
    left = sums[:, :tile] / (beta * alpha) - (alpha / beta) * data
    left_ref[...] = left
    out_scal_ref[...] = jnp.zeros_like(out_scal_ref)
    out_scal_ref[0:1, :] = spread(beta)
    out_scal_ref[1:2, :] = spread(alpha)
    prods = backward(tiles_ref, rows_ref, left)
    send_terms(send_ref, cols_ref, count_ref, prods, total(left * left))


def second_forward_kernel(
    count_ref, rows_ref, cols_ref, recv_ref, before_ref, scal_ref, tiles_ref,
    part_ref, own_ref, out_scal_ref, full_ref,
):
    norm = all_cells(recv_ref, recv_ref, tiles_ref.shape[0], full_ref)
    beta0, alpha0 = scal_ref[0:1, 0:1], scal_ref[1:2, 0:1]
    beta1 = jnp.sqrt(norm + EPS)
    full_ref[...] = full_ref[...] / beta1 - before_ref[...] * (beta1 / (beta0 * alpha0))
    out_scal_ref[...] = jnp.broadcast_to(beta1, out_scal_ref.shape)
    finish_forward(count_ref, rows_ref, cols_ref, full_ref, tiles_ref, part_ref, own_ref)


def third_kernel(part_ref, other_ref, left_ref, beta_ref, send_ref, next_ref, alpha_ref):
    npath = send_ref.shape[0]
    tile = left_ref.shape[1]
    sums = part_ref[...] + other_ref[...]
    alpha = jnp.sqrt(sums[0:1, tile : tile + 1] + EPS)
    left = sums[:, :tile] / alpha - left_ref[...] * (alpha / beta_ref[0:1, 0:1])
    next_ref[...] = left
    alpha_ref[...] = jnp.broadcast_to(alpha, alpha_ref.shape)
    sub, lane = iota((8, META), 0), iota((8, META), 1)
    message = jnp.where(sub == 0, pieces(lane, total(left * left)), 0.0).astype(BF16)
    for q in range(npath):
        send_ref[q] = message


def final_kernel(
    total_rows, recv_ref, left_ref, own0_ref, own1_ref, scal_ref, beta_ref, alpha_ref,
    solution_ref, out_ref,
):
    npath = recv_ref.shape[0]
    norm = sum_pieces(recv_ref[...].astype(F32).reshape(npath * 8, META))
    beta2 = jnp.sqrt(norm + EPS)
    beta0, alpha0 = scal_ref[0:1, 0:1], scal_ref[1:2, 0:1]
    beta1, alpha1 = beta_ref[0:1, 0:1], alpha_ref[0:1, 0:1]
    rho1 = jnp.sqrt(alpha0 * alpha0 + beta1 * beta1)
    cosine, sine = alpha0 / rho1, beta1 / rho1
    theta = sine * alpha1
    rhobar = -cosine * alpha1
    phi1, phibar = cosine * beta0, sine * beta0
    rho2 = jnp.sqrt(rhobar * rhobar + beta2 * beta2)
    phi2 = rhobar / rho2 * phibar
    right0 = own0_ref[...] / (beta0 * alpha0)
    right1 = own1_ref[...] / alpha1
    search = right1 - (theta / rho1) * right0
    answer_ = (phi1 / rho1) * right0 + (phi2 / rho2) * search
    store_pairs(solution_ref, answer_, answer_.shape[0])
    left = left_ref[...] * (total_rows**0.5 / beta2)
    store_pairs(out_ref, left, left.shape[0])


def call(kernel, ins, outs, scratch=(), flops=0, moved=0, room=LIMIT):
    shapes = [jax.ShapeDtypeStruct(s, d) for s, d in outs]
    return pl.pallas_call(
        kernel,
        in_specs=ins,
        out_specs=[VMEM] * len(outs),
        out_shape=shapes,
        scratch_shapes=scratch,
        compiler_params=pltpu.CompilerParams(vmem_limit_bytes=room),
        cost_estimate=pl.CostEstimate(flops=flops, bytes_accessed=moved, transcendentals=0),
    )


def on_device(tiles, tile_rows, tile_cols, tile_counts, data):
    slots, tile, _ = tiles.shape
    row_tiles = data.shape[0] // tile
    npath = lax.axis_size("path")
    rows = tile_rows.reshape(1, slots)
    cols = tile_cols.reshape(1, slots)
    data = data.reshape(row_tiles * 2, tile // 2)
    held = [pltpu.VMEM(tiles.shape, tiles.dtype), pltpu.SemaphoreType.DMA((CHUNKS,))]
    payload = ((npath, 2 * slots + 8, META), BF16)
    short = ((npath, 8, META), BF16)
    scal = ((8, META), F32)
    full_shape = (npath * CT_DEV, tile)
    own_shape = ((CT_DEV, tile), F32)
    left_shape = ((row_tiles, tile), F32)
    part_shape = ((row_tiles, tile + META), F32)
    work = dict(flops=2 * 8 * tiles.size, moved=2 * tiles.size)

    def swap(x):
        return lax.all_to_all(x, "path", 0, 0, tiled=True)

    def other_half(x):
        return lax.ppermute(x, "mp", [(0, 1), (1, 0)])

    (send,) = call(
        first_kernel,
        [SMEM, VMEM, VMEM, VMEM, HBM],
        [payload],
        scratch=held,
        room=FIRST_LIMIT,
        **work,
    )(tile_counts, rows, cols, data, tiles)
    recv = swap(send)
    part, full, own0, scal0 = call(
        first_forward_kernel,
        [SMEM] + [VMEM] * 4,
        [part_shape, (full_shape, F32), own_shape, scal],
        **work,
    )(tile_counts, rows, cols, recv, tiles)
    send, left, scal1 = call(
        second_kernel, [SMEM] + [VMEM] * 7, [payload, left_shape, scal], **work
    )(tile_counts, rows, cols, data, part, other_half(part), scal0, tiles)
    recv = swap(send)
    part, own1, beta1 = call(
        second_forward_kernel,
        [SMEM] + [VMEM] * 6,
        [part_shape, own_shape, scal],
        scratch=[pltpu.VMEM(full_shape, F32)],
        **work,
    )(tile_counts, rows, cols, recv, full, scal1, tiles)
    send, left, alpha1 = call(third_kernel, [VMEM] * 4, [short, left_shape, scal])(
        part, other_half(part), left, beta1
    )
    recv = swap(send)
    total_rows = row_tiles * tile * npath

    def last(*refs):
        final_kernel(total_rows, *refs)

    solution, left = call(
        last, [VMEM] * 7, [((CT_DEV * 2, tile // 2), F32), ((row_tiles * 2, tile // 2), F32)]
    )(recv, left, own0, own1, scal1, beta1, alpha1)
    return solution.reshape(-1), left.reshape(-1)


def solution(mesh):
    placed = (
        P(("path", "mp"), None, None),
        P(("path", "mp")),
        P(("path", "mp")),
        P(("path", "mp")),
        P(("period", "path")),
    )
    return jax.shard_map(
        on_device,
        mesh=mesh,
        in_specs=placed,
        out_specs=(P(("period", "path", "mp")), P(("period", "path"))),
        check_vma=False,
    )
```

time: 101 us -> 116 us (1.15)
  blocking collectives: 81.3 us -> 91.5 us
  Pallas kernels: 12.9 us -> 18.6 us
    all_to_all x5 -> x3, blocking collectives: 81.3 us -> 91.5 us  [swap(): return lax.all_to_all(x, 'path', 0, 0, tiled=True)]
    pallas_call x5 -> x3, Pallas kernels: 6.01 us -> 11.7 us  [the longest x1 5.81 us: on_device(): call(first_forward_kernel, [SMEM] + [VMEM] * 4, [part_shape, (full_shape,...]
where the time goes in v3:
time: 116 us
  blocking collectives  91.5 us (79%)
  Pallas kernels  18.6 us (16%)
  waiting for transfers between devices  2.41 us (2%)
  local copies, waits for them, and re-layouts  2 us (2%)
  between operations  1.33 us (1%)
    all_to_all x3, blocking collectives, swap(): return lax.all_to_all(x, 'path', 0, 0, tiled=True)  91.5 us
    pallas_call x1, Pallas kernels, on_device(): call(first_forward_kernel, [SMEM] + [VMEM] * 4, [part_shape, (full_shape,...  5.81 us
    pallas_call x1, Pallas kernels, on_device(): call(second_forward_kernel, [SMEM] + [VMEM] * 6, [part_shape, own_shape,...  5.77 us
    pallas_call x1, Pallas kernels, on_device(): call(first_kernel, [SMEM, VMEM, VMEM, VMEM, HBM], [payload], scratch=held...  4.64 us
    ppermute x2, waiting for transfers between devices, other_half(): return lax.ppermute(x, 'mp', [(0, 1), (1, 0)])  2.41 us
  transfers between devices with their start and end apart: 2, of which 2 were waited for; matrix products, arithmetic and copies ran while one was open for 0% of the time, Pallas kernels for 0%

profile of v3, /device:TPU:16, one launch (start us, length us, event | category | flops | bytes accessed | tf_op | source)
XLA Modules:
  0.0 115.8 jit_solution(2628595872263731462)
XLA Ops:
  1.3 0.0 copy-start.1
  1.3 0.7 copy-done.1
  2.0 0.0 copy-start.2
  2.0 0.7 copy-done.2
  2.6 0.0 copy-start.3
  2.6 0.7 copy-done.3
  3.3 0.0 copy-start
  3.3 4.6 %shard_map.68 = bf16[32,136,128]{2,1,0:T(8,128)(2,1)S(1)} custom-call(s32[1]{0:T(128)S(6)} %copy.7.count_ref, s32[1,64]{1,0:T(1,128)S(1)} %bitcast.7, s32[1,64]{1,0:T(1,128)S(1)} %bitcast.11, f32[16,128]{1,0:T(8,128)S(1)} %bitcast.5, bf16[64,256,256]{2,1,0:T(8,128)(2,1)} %tiles_ref.7), custom_call_target="tpu_custom_call" | custom-call | flops 67108864 | bytes 8388608 | tf_op jit(solution)/shard_map/pallas_call | solution.py:316
  7.9 42.9 %all_to_all.15.recv_ref = bf16[32,136,128]{2,1,0:T(8,128)(2,1)S(1)} all-to-all(bf16[32,136,128]{2,1,0:T(8,128)(2,1)S(1)} %shard_map.68), channel_id=1, replica_groups=mesh['path'=32,'mp'=2,'period'=4] {'path'}, dimensions={0} | all-to-all | bytes 2228224 | tf_op jit(solution)/shard_map/all_to_all | solution.py:311
  50.9 0.0 copy-done
  50.9 5.8 %shard_map.69 = (f32[8,384]{1,0:T(8,128)S(1)}, f32[1024,256]{1,0:T(8,128)S(1)}, f32[32,256]{1,0:T(8,128)S(1)}, f32[8,128]{1,0:T(8,128)S(1)}) custom-call(s32[1]{0:T(128)S(6)} %copy.7.count_ref, s32[1,64]{1,0:T(1,128)S(1)} %bitcast.8, s32[1,64]{1,0:T(1,128)S(1)} %bitcast.12, bf16[32,136,128]{2,1,0:T(8,128)(2,1)S(1)} %all_to_all.15.recv_ref, ...), custom_call_target="tpu_custom_call" | custom-call | flops 67108864 | bytes 8388608 | tf_op jit(solution)/shard_map/pallas_call | solution.py:325
  56.7 0.0 collective-permute-start
  56.7 1.2 %collective-permute-done.other_ref = f32[8,384]{1,0:T(8,128)S(1)} collective-permute-done((f32[8,384]{1,0:T(8,128)S(1)}, f32[8,384]{1,0:T(8,128)S(1)}, u32[]{:S(2)}, u32[]{:S(2)}) %collective-permute-start) | collective-permute-done | bytes 12320 | tf_op jit(solution)/shard_map/ppermute | solution.py:314
  57.9 1.4 %shard_map.70 = (bf16[32,136,128]{2,1,0:T(8,128)(2,1)S(1)}, f32[8,256]{1,0:T(8,128)S(1)}, f32[8,128]{1,0:T(8,128)S(1)}) custom-call(s32[1]{0:T(128)S(6)} %copy.7.count_ref, s32[1,64]{1,0:T(1,128)S(1)} %bitcast.9, s32[1,64]{1,0:T(1,128)S(1)} %bitcast.13, f32[16,128]{1,0:T(8,128)S(1)} %bitcast.6, f32[8,384]{1,0:T(8,128)S(1)} %get-tuple-element.17.part_ref, ...), custom_call_target="tpu_custom_call" | custom-call | flops 67108864 | bytes 8388608 | tf_op jit(solution)/shard_map/pallas_call | solution.py:331
  59.3 35.3 %all_to_all.16.recv_ref = bf16[32,136,128]{2,1,0:T(8,128)(2,1)S(1)} all-to-all(bf16[32,136,128]{2,1,0:T(8,128)(2,1)S(1)} %get-tuple-element.19), channel_id=1, replica_groups=mesh['path'=32,'mp'=2,'period'=4] {'path'}, dimensions={0} | all-to-all | bytes 2228224 | tf_op jit(solution)/shard_map/all_to_all | solution.py:311
  94.7 5.8 %shard_map.71 = (f32[8,384]{1,0:T(8,128)S(1)}, f32[32,256]{1,0:T(8,128)S(1)}, f32[8,128]{1,0:T(8,128)S(1)}) custom-call(s32[1]{0:T(128)S(6)} %copy.7.count_ref, s32[1,64]{1,0:T(1,128)S(1)} %bitcast.10, s32[1,64]{1,0:T(1,128)S(1)} %bitcast.14, bf16[32,136,128]{2,1,0:T(8,128)(2,1)S(1)} %all_to_all.16.recv_ref, f32[1024,256]{1,0:T(8,128)S(1)} %get-tuple-element.20.before_ref, ...), custom_call_target="tpu_custom_call" | custom-call | flops 67108864 | bytes 8388608 | tf_op jit(solution)/shard_map/pallas_call | solution.py:335
  100.4 0.0 collective-permute-start.1
  100.4 1.2 %collective-permute-done.1.other_ref = f32[8,384]{1,0:T(8,128)S(1)} collective-permute-done((f32[8,384]{1,0:T(8,128)S(1)}, f32[8,384]{1,0:T(8,128)S(1)}, u32[]{:S(2)}, u32[]{:S(2)}) %collective-permute-start.1) | collective-permute-done | bytes 12320 | tf_op jit(solution)/shard_map/ppermute | solution.py:314
  101.6 0.1 shard_map.72
  101.8 13.2 %all_to_all.17.refs_0_ = bf16[32,8,128]{2,1,0:T(8,128)(2,1)S(1)} all-to-all(bf16[32,8,128]{2,1,0:T(8,128)(2,1)S(1)} %get-tuple-element.25), channel_id=1, replica_groups=mesh['path'=32,'mp'=2,'period'=4] {'path'}, dimensions={0} | all-to-all | bytes 131072 | tf_op jit(solution)/shard_map/all_to_all | solution.py:311
  115.0 0.8 shard_map.73
Async XLA Ops:
  1.3 0.7 copy-start.1
  2.0 0.7 copy-start.2
  2.6 0.7 copy-start.3
  3.3 47.6 %copy-start = (bf16[64,256,256]{2,1,0:T(8,128)(2,1)S(1)}, bf16[64,256,256]{2,1,0:T(8,128)(2,1)}, u32[]{:S(2)}) copy-start(bf16[64,256,256]{2,1,0:T(8,128)(2,1)} %tiles_ref.7) | copy-start | bytes 25165828
  56.7 1.2 %collective-permute-start = (f32[8,384]{1,0:T(8,128)S(1)}, f32[8,384]{1,0:T(8,128)S(1)}, u32[]{:S(2)}, u32[]{:S(2)}) collective-permute-start(f32[8,384]{1,0:T(8,128)S(1)} %get-tuple-element.17.part_ref), channel_id=1, source_target_pairs={{0,4},{4,0},{1,5},{5,1},{2,6},{6,2},{3,7},{7,3},{8,12},{12,8},{9,1... | collective-permute-start | bytes 36872 | tf_op jit(solution)/shard_map/ppermute | solution.py:314
  100.4 1.2 %collective-permute-start.1 = (f32[8,384]{1,0:T(8,128)S(1)}, f32[8,384]{1,0:T(8,128)S(1)}, u32[]{:S(2)}, u32[]{:S(2)}) collective-permute-start(f32[8,384]{1,0:T(8,128)S(1)} %get-tuple-element.22.part_ref), channel_id=1, source_target_pairs={{0,4},{4,0},{1,5},{5,1},{2,6},{6,2},{3,7},{7,3},{8,12},{12,8},{9,1... | collective-permute-start | bytes 36872 | tf_op jit(solution)/shard_map/ppermute | solution.py:314

commit v4 on v2

v4 whole, which is shorter than its diff:
```python
import jax
import jax.numpy as jnp
from jax import lax
from jax.experimental import pallas as pl
from jax.experimental.pallas import tpu as pltpu
from jax.sharding import PartitionSpec as P

CT_DEV = 32
EPS = 1e-12
CHUNKS = 8
META = 128
LIMIT = 12 << 20
FIRST_LIMIT = 40 << 20
F32 = jnp.float32
BF16 = jnp.bfloat16
VMEM = pl.BlockSpec(memory_space=pltpu.VMEM)
HBM = pl.BlockSpec(memory_space=pltpu.HBM)


def iota(shape, dim):
    return lax.broadcasted_iota(jnp.int32, shape, dim)


def onehot(mask):
    return jnp.where(mask, 1.0, 0.0).astype(BF16)


def dot(a, b, ca, cb):
    return lax.dot_general(a, b, (((ca,), (cb,)), ((), ())), preferred_element_type=F32)


def total(x):
    return jnp.sum(jnp.sum(x, axis=1, keepdims=True), axis=0, keepdims=True)


def load_pairs(ref, rows):
    return jnp.concatenate(
        [ref[pl.ds(0, rows, stride=2), :], ref[pl.ds(1, rows, stride=2), :]], axis=1
    )


def store_pairs(ref, value, rows):
    half = value.shape[1] // 2
    ref[pl.ds(0, rows, stride=2), :] = value[:, :half]
    ref[pl.ds(1, rows, stride=2), :] = value[:, half:]


def pieces(lane, value):
    high = value.astype(BF16).astype(F32)
    rest = value - high
    middle = rest.astype(BF16).astype(F32)
    low = rest - middle
    return jnp.where(lane == 1, high, jnp.where(lane == 2, middle, jnp.where(lane == 3, low, 0.0)))


def sum_pieces(meta):
    lane = iota(meta.shape, 1)
    return total(jnp.where((lane >= 1) & (lane <= 3), meta, 0.0))


def split(x):
    high = x.astype(BF16)
    low = (x - high.astype(F32)).astype(BF16)
    return jnp.concatenate([high, low], axis=0)


def fold(x):
    half = x.shape[0] // 2
    return x[:half] + x[half:]


def data_of(table_ref):
    return load_pairs(table_ref.at[: table_ref.shape[0] - 8], (table_ref.shape[0] - 8) // 2)


def slots_of(table_ref):
    base = table_ref.shape[0] - 8
    slots = META // 2
    both = table_ref[base : base + 1, :].astype(jnp.int32)
    count = table_ref[base + 1 : base + 2, 0:1].astype(jnp.int32)
    return both[:, slots:], both[:, :slots], count


def column_of(row):
    n = row.shape[1]
    return jnp.sum(jnp.where(iota((n, n), 0) == iota((n, n), 1), row, 0), axis=1, keepdims=True)


def placement(cols, count, npath, limit):
    slots = cols.shape[1]
    owner = lax.div(cols, CT_DEV)
    inside = cols - owner * CT_DEV
    owner_col = column_of(owner)
    earlier = iota((slots, slots), 0) < iota((slots, slots), 1)
    same = (owner_col == owner) & earlier
    rank = jnp.sum(jnp.where(same, 1, 0), axis=0, keepdims=True)
    live = iota(cols.shape, 1) < count
    target = jnp.where(live, owner * limit + rank, -1)
    key = jnp.where(live, cols, -CT_DEV)
    place = onehot(iota((npath * limit, slots), 0) == target)
    return place, inside, key


def start_tiles(tiles_ref, held, sems):
    step = held.shape[0] // CHUNKS
    copies = []
    for k in range(CHUNKS):
        part = pl.ds(k * step, step)
        copies.append(pltpu.make_async_copy(tiles_ref.at[part], held.at[part], sems.at[k]))
        copies[-1].start()
    return copies


def backward(held, rows, left, copies=None):
    slots, tile = held.shape[0], held.shape[1]
    row_tiles = left.shape[0]
    row_hot = onehot(iota((row_tiles, slots), 0) == rows)
    both = split(left)
    high = dot(row_hot, both[:row_tiles], 0, 0)
    low = dot(row_hot, both[row_tiles:], 0, 0)
    step = slots // CHUNKS
    sub = iota((2 * step, tile), 0)
    out = []
    for k in range(CHUNKS):
        if copies is not None:
            copies[k].wait()
        part = slice(k * step, (k + 1) * step)
        block = jnp.concatenate([high[part], low[part]], axis=0)
        acc = jnp.zeros((2 * step, tile), F32)
        for i in range(step):
            mine = (sub == i) | (sub == i + step)
            acc += dot(jnp.where(mine, block, 0.0).astype(BF16), held[k * step + i], 1, 0)
        out.append(fold(acc).astype(BF16))
    return jnp.concatenate(out, axis=0)


def forward(held, rows, picked, row_tiles, exact):
    slots, tile = held.shape[0], held.shape[1]
    row_hot = jnp.where(iota((row_tiles, slots), 0) == rows, 1.0, 0.0)
    acc = jnp.zeros((row_tiles if exact else 2 * row_tiles, tile), F32)
    for s in range(slots):
        lhs = row_hot[:, s : s + 1] * picked[s : s + 1, :]
        acc += dot(lhs.astype(BF16) if exact else split(lhs), held[s], 1, 1)
    return acc if exact else fold(acc)


def first_kernel(table_ref, tiles_ref, send_ref, held_ref, sems):
    npath, limit, width = send_ref.shape
    copies = start_tiles(tiles_ref, held_ref, sems)
    left = data_of(table_ref)
    rows, cols, count = slots_of(table_ref)
    place, inside, key = placement(cols, count, npath, limit)
    slots = key.shape[1]
    lane = iota((slots, META), 1)
    meta = jnp.where(lane == 0, column_of(inside) + 1, 0).astype(F32).astype(BF16)
    owner = lax.div(key + CT_DEV, CT_DEV)
    pair = jnp.where(iota((8, slots), 0) == 0, owner, inside).astype(F32)
    index = jnp.concatenate([jnp.zeros((8, META - slots), F32), pair], axis=1)
    index += pieces(iota((8, META), 1), total(left * left))
    prods = backward(held_ref, rows, left, copies)
    tile = prods.shape[1]
    out = dot(place, jnp.concatenate([prods, meta], axis=1), 1, 0)
    out = out.reshape(npath, limit, width)
    tail = out[:, :, tile:] + jnp.broadcast_to(index[None], (npath, limit, META))
    send_ref[...] = jnp.concatenate([out[:, :, :tile], tail], axis=2).astype(BF16)


def first_owner_kernel(recv_ref, send_ref, own_ref, scal_ref):
    npath, limit, width = recv_ref.shape
    rows = npath * limit
    tile = width - META
    recv = recv_ref[...].reshape(rows, width)
    meta = recv[:, tile:].astype(F32)
    hot = onehot(meta[:, 0:1].astype(jnp.int32) == iota((rows, CT_DEV), 1) + 1)
    own = dot(hot, recv[:, :tile], 0, 0)
    own_ref[...] = own
    scal_ref[...] = jnp.broadcast_to(sum_pieces(meta) * (1.0 / limit), scal_ref.shape)
    tail = pieces(iota((rows, META), 1), total(own * own))
    full = jnp.concatenate([dot(hot, own.astype(BF16), 1, 0), tail], axis=1)
    send_ref[...] = full.astype(BF16).reshape(npath, limit, width)


def first_forward_kernel(table_ref, recv_ref, tiles_ref, out_ref):
    npath, limit, width = recv_ref.shape
    tile = width - META
    row_tiles = out_ref.shape[0]
    slot_rows, cols, count = slots_of(table_ref)
    place = placement(cols, count, npath, limit)[0]
    recv = recv_ref[...].reshape(npath * limit, width)
    picked = dot(place, recv[:, :tile], 0, 0)
    norm = sum_pieces(recv[:, tile:].astype(F32)) * (1.0 / limit)
    acc = forward(tiles_ref, slot_rows, picked, row_tiles, True)
    out_ref[...] = jnp.concatenate([acc, jnp.broadcast_to(norm, (row_tiles, META))], axis=1)


def spread(value):
    return jnp.broadcast_to(value, (1, META))


def second_kernel(
    table_ref, part_ref, other_ref, scal_ref, tiles_ref,
    send_ref, left_ref, image_ref, out_scal_ref,
):
    npath = send_ref.shape[0]
    tile = left_ref.shape[1]
    sums = part_ref[...] + other_ref[...]
    beta_sq = scal_ref[0:1, 0:1] + EPS
    beta = jnp.sqrt(beta_sq)
    norm = sums[0:1, tile : tile + 1]
    alpha_sq = norm / beta_sq + EPS
    alpha = jnp.sqrt(alpha_sq)
    data = data_of(table_ref)
    image = sums[:, :tile] / (beta * alpha)
    left = image - (alpha / beta) * data
    image_ref[...] = image
    left_ref[...] = left
    out_scal_ref[...] = jnp.zeros_like(out_scal_ref)
    out_scal_ref[0:1, :] = spread(beta)
    out_scal_ref[1:2, :] = spread(alpha)
    out_scal_ref[2:3, :] = spread(norm / (beta_sq * alpha_sq))
    prods = backward(tiles_ref, slots_of(table_ref)[0], left)
    for q in range(npath):
        send_ref[q] = prods


def second_forward_kernel(
    table_ref, recv_ref, index_ref, own_ref, scal_ref, tiles_ref,
    part_ref, next_ref,
):
    npath, slots, tile = recv_ref.shape
    row_tiles = part_ref.shape[0]
    group = max(1, tile // slots)
    me = lax.axis_index("path")
    rows, cols, count = slots_of(table_ref)
    live = iota((1, slots), 1) < count
    wanted = column_of(jnp.where(live, cols, -2 * CT_DEV))
    wanted = jnp.concatenate([iota((CT_DEV, 1), 0) + me * CT_DEV, wanted], axis=0).astype(F32)
    acc = jnp.zeros((CT_DEV + slots, tile), F32)
    for b in range(npath // group):
        keys = []
        for q in range(b * group, (b + 1) * group):
            meta = index_ref[q, :, tile:].astype(F32)
            owner, inside = meta[0:1, META - slots :], meta[1:2, META - slots :]
            keys.append((owner - 1.0) * CT_DEV + jnp.where(owner > 0.5, inside, 0.0))
        keys = jnp.concatenate(keys, axis=1)
        block = recv_ref[b * group : (b + 1) * group].reshape(group * slots, tile)
        acc += dot(onehot(wanted == keys), block, 1, 0)
    own, picked = acc[:CT_DEV], acc[CT_DEV:]
    next_ref[...] = own
    before = own_ref[...] / (scal_ref[0:1, 0:1] * scal_ref[1:2, 0:1])
    lane = iota((row_tiles, META), 1)
    tail = jnp.where(lane == 0, total(own * own), jnp.where(lane == 1, total(own * before), 0.0))
    image = forward(tiles_ref, rows, picked, row_tiles, False)
    part_ref[...] = jnp.concatenate([image, tail], axis=1)


def third_kernel(part_ref, other_ref, left_ref, image_ref, send_ref, next_ref):
    npath = send_ref.shape[0]
    tile = left_ref.shape[1]
    sums = part_ref[...] + other_ref[...]
    z, g, u = sums[:, :tile], image_ref[...], left_ref[...]
    next_ref[...] = z
    values = [total(a * b) for a, b in ((u, u), (z, z), (z, g), (z, u), (g, g), (g, u))]
    values += [sums[0:1, tile : tile + 1], sums[0:1, tile + 1 : tile + 2]]
    lane = iota((1, META), 1)
    message = jnp.concatenate([pieces(lane, v) for v in values], axis=0).astype(BF16)
    for q in range(npath):
        send_ref[q] = message


def final_kernel(
    total_rows, recv_ref, next_ref, left_ref, image_ref, own0_ref, own1_ref, scal_ref,
    solution_ref, out_ref,
):
    sums = jnp.sum(recv_ref[...].astype(F32), axis=0)
    uu, zz, zg, zu, gg, gu, yy, yv = [sum_pieces(sums[k : k + 1]) for k in range(8)]
    beta0, alpha0, vv = [scal_ref[k : k + 1, 0:1] for k in range(3)]
    beta1_sq = uu + EPS
    beta1 = jnp.sqrt(beta1_sq)
    alpha1 = jnp.sqrt(jnp.maximum(yy / beta1_sq - 2.0 * yv + beta1_sq * vv, 0.0) + EPS)
    a, b, c = 1.0 / (beta1 * alpha1), -beta1 / alpha1, -alpha1 / beta1
    norm = a * a * zz + b * b * gg + c * c * uu + 2.0 * (a * b * zg + a * c * zu + b * c * gu)
    beta2 = jnp.sqrt(jnp.maximum(norm, 0.0) + EPS)
    rho1 = jnp.sqrt(alpha0 * alpha0 + beta1 * beta1)
    cosine, sine = alpha0 / rho1, beta1 / rho1
    theta = sine * alpha1
    rhobar = -cosine * alpha1
    phi1, phibar = cosine * beta0, sine * beta0
    rho2 = jnp.sqrt(rhobar * rhobar + beta2 * beta2)
    phi2 = rhobar / rho2 * phibar
    right0 = own0_ref[...] / (beta0 * alpha0)
    right1 = (own1_ref[...] / beta1 - beta1 * right0) / alpha1
    search = right1 - (theta / rho1) * right0
    answer = (phi1 / rho1) * right0 + (phi2 / rho2) * search
    store_pairs(solution_ref, answer, answer.shape[0])
    left = a * next_ref[...] + b * image_ref[...] + c * left_ref[...]
    left = left * (total_rows**0.5 / beta2)
    store_pairs(out_ref, left, left.shape[0])


def call(kernel, ins, outs, scratch=(), flops=0, moved=0, room=LIMIT):
    shapes = [jax.ShapeDtypeStruct(s, d) for s, d in outs]
    return pl.pallas_call(
        kernel,
        in_specs=ins,
        out_specs=[VMEM] * len(outs),
        out_shape=shapes,
        scratch_shapes=scratch,
        compiler_params=pltpu.CompilerParams(vmem_limit_bytes=room),
        cost_estimate=pl.CostEstimate(flops=flops, bytes_accessed=moved, transcendentals=0),
    )


def on_device(tiles, tile_rows, tile_cols, tile_counts, data):
    slots, tile, _ = tiles.shape
    row_tiles = data.shape[0] // tile
    npath = lax.axis_size("path")
    limit = max(2, max(slots // 8, (slots + npath - 1) // npath))
    named = jnp.concatenate([tile_cols, tile_rows, jnp.broadcast_to(tile_counts, (META,))])
    named = jnp.pad(named.astype(F32), (0, 8 * META - named.shape[0]))
    table = jnp.concatenate([data, named]).reshape(-1, META)
    held = [pltpu.VMEM(tiles.shape, tiles.dtype), pltpu.SemaphoreType.DMA((CHUNKS,))]
    payload = ((npath, limit, tile + META), BF16)
    scal = ((8, META), F32)
    own_shape = ((CT_DEV, tile), F32)
    left_shape = ((row_tiles, tile), F32)
    part_shape = ((row_tiles, tile + META), F32)
    work = dict(flops=2 * 8 * tiles.size, moved=2 * tiles.size)

    def swap(x):
        return lax.all_to_all(x, "path", 0, 0, tiled=True)

    def other_half(x):
        return lax.ppermute(x, "mp", [(0, 1), (1, 0)])

    send, tiles = call(
        first_kernel,
        [VMEM, HBM],
        [payload, (tiles.shape, tiles.dtype)],
        scratch=held[1:],
        room=FIRST_LIMIT,
        **work,
    )(table, tiles)
    index = swap(send)
    send, own0, scal0 = call(first_owner_kernel, [VMEM], [payload, own_shape, scal])(index)
    recv = swap(send)
    (part,) = call(first_forward_kernel, [VMEM] * 3, [part_shape], **work)(
        table, recv, tiles
    )
    send, left, image, scal1 = call(
        second_kernel,
        [VMEM] * 5,
        [((npath, slots, tile), BF16), left_shape, left_shape, scal],
        **work,
    )(table, part, other_half(part), scal0, tiles)
    recv = swap(send)
    part, own1 = call(
        second_forward_kernel, [VMEM] * 6, [part_shape, own_shape], **work
    )(table, recv, index, own0, scal1, tiles)
    send, mixed = call(third_kernel, [VMEM] * 4, [((npath, 8, META), BF16), left_shape])(
        part, other_half(part), left, image
    )
    recv = swap(send)
    total_rows = row_tiles * tile * npath

    def last(*refs):
        final_kernel(total_rows, *refs)

    solution, left = call(
        last, [VMEM] * 7, [((CT_DEV * 2, tile // 2), F32), ((row_tiles * 2, tile // 2), F32)]
    )(recv, mixed, left, image, own0, own1, scal1)
    return solution.reshape(-1), left.reshape(-1)


def solution(mesh):
    placed = (
        P(("path", "mp"), None, None),
        P(("path", "mp")),
        P(("path", "mp")),
        P(("path", "mp")),
        P(("period", "path")),
    )
    return jax.shard_map(
        on_device,
        mesh=mesh,
        in_specs=placed,
        out_specs=(P(("period", "path", "mp")), P(("period", "path"))),
        check_vma=False,
    )
```

time: 101 us -> 103 us (1.020)
  blocking collectives: 81.3 us -> 84.9 us
  local copies, waits for them, and re-layouts: 2.4 us -> 0.01 us
  other arithmetic: 0 us -> 1.45 us
    all_to_all x5 -> x4, blocking collectives: 81.3 us -> 84.9 us  [swap(): return lax.all_to_all(x, 'path', 0, 0, tiled=True)]
    unnamed x8 -> x0, local copies, waits for them, and re-layouts: 2.4 us -> none
    pallas_call x6 -> x5, Pallas kernels: 11.7 us -> 11.5 us  [the longest x1 4.58 us: on_device(): call(first_kernel, [VMEM, HBM], [payload, (tiles.shape, tiles.dtype)], sc...]
where the time goes in v4:
time: 103 us
  blocking collectives  84.9 us (82%)
  Pallas kernels  12.8 us (12%)
  waiting for transfers between devices  2.37 us (2%)
  other arithmetic  1.45 us (1%)
  between operations  1.33 us (1%)
    all_to_all x4, blocking collectives, swap(): return lax.all_to_all(x, 'path', 0, 0, tiled=True)  84.9 us
    pallas_call x1, Pallas kernels, on_device(): call(first_kernel, [VMEM, HBM], [payload, (tiles.shape, tiles.dtype)], sc...  4.58 us
    pallas_call x1, Pallas kernels, on_device(): call(second_forward_kernel, [VMEM] * 6, [part_shape, own_shape], **work)  2.91 us
    pallas_call x1, Pallas kernels, on_device(): call(first_forward_kernel, [VMEM] * 3, [part_shape], **work)  2.49 us
    ppermute x2, waiting for transfers between devices, other_half(): return lax.ppermute(x, 'mp', [(0, 1), (1, 0)])  2.37 us
  transfers between devices with their start and end apart: 2, of which 2 were waited for; matrix products, arithmetic and copies ran while one was open for 0% of the time, Pallas kernels for 0%

profile of v4, /device:TPU:16, one launch (start us, length us, event | category | flops | bytes accessed | tf_op | source)
XLA Modules:
  0.0 102.9 jit_solution(2738468367867580973)
XLA Ops:
  1.3 0.8 add_convert_fusion
  2.0 0.7 fusion.table_ref
  2.7 4.6 %shard_map.68 = (bf16[32,8,384]{2,1,0:T(8,128)(2,1)S(1)}, bf16[64,256,256]{2,1,0:T(8,128)(2,1)S(1)}) custom-call(f32[24,128]{1,0:T(8,128)S(1)} %fusion.table_ref, bf16[64,256,256]{2,1,0:T(8,128)(2,1)} %tiles_ref.1), custom_call_target="tpu_custom_call" | custom-call | flops 67108864 | bytes 8388608 | tf_op jit(solution)/shard_map/pallas_call | solution.py:336
  7.3 22.4 %all_to_all.20.recv_ref.index_ref = bf16[32,8,384]{2,1,0:T(8,128)(2,1)S(1)} all-to-all(bf16[32,8,384]{2,1,0:T(8,128)(2,1)S(1)} %get-tuple-element.17), channel_id=1, replica_groups=mesh['path'=32,'mp'=2,'period'=4] {'path'}, dimensions={0} | all-to-all | bytes 393216 | tf_op jit(solution)/shard_map/all_to_all | solution.py:331
  29.8 0.4 shard_map.69
  30.2 14.8 %all_to_all.21.recv_ref = bf16[32,8,384]{2,1,0:T(8,128)(2,1)S(1)} all-to-all(bf16[32,8,384]{2,1,0:T(8,128)(2,1)S(1)} %get-tuple-element.18), channel_id=1, replica_groups=mesh['path'=32,'mp'=2,'period'=4] {'path'}, dimensions={0} | all-to-all | bytes 393216 | tf_op jit(solution)/shard_map/all_to_all | solution.py:331
  45.0 2.5 %shard_map.70.part_ref = f32[8,384]{1,0:T(8,128)S(1)} custom-call(f32[24,128]{1,0:T(8,128)S(1)} %fusion.table_ref, bf16[32,8,384]{2,1,0:T(8,128)(2,1)S(1)} %all_to_all.21.recv_ref, bf16[64,256,256]{2,1,0:T(8,128)(2,1)S(1)} %get-tuple-element.19.tiles_ref), custom_call_target="tpu_custom_call" | custom-call | flops 67108864 | bytes 8388608 | tf_op jit(solution)/shard_map/pallas_call | solution.py:347
  47.5 0.0 collective-permute-start
  47.5 1.2 %collective-permute-done.other_ref = f32[8,384]{1,0:T(8,128)S(1)} collective-permute-done((f32[8,384]{1,0:T(8,128)S(1)}, f32[8,384]{1,0:T(8,128)S(1)}, u32[]{:S(2)}, u32[]{:S(2)}) %collective-permute-start) | collective-permute-done | bytes 12320 | tf_op jit(solution)/shard_map/ppermute | solution.py:334
  48.7 1.4 %shard_map.71 = (bf16[32,64,256]{2,1,0:T(8,128)(2,1)S(1)}, f32[8,256]{1,0:T(8,128)S(1)}, f32[8,256]{1,0:T(8,128)S(1)}, f32[8,128]{1,0:T(8,128)S(1)}) custom-call(f32[24,128]{1,0:T(8,128)S(1)} %fusion.table_ref, f32[8,384]{1,0:T(8,128)S(1)} %shard_map.70.part_ref, f32[8,384]{1,0:T(8,128)S(1)} %collective-permute-done.other_ref, ...), custom_call_target="tpu_custom_call" | custom-call | flops 67108864 | bytes 8388608 | tf_op jit(solution)/shard_map/pallas_call | solution.py:350
  50.1 32.7 %all_to_all.22.recv_ref = bf16[32,64,256]{2,1,0:T(8,128)(2,1)S(1)} all-to-all(bf16[32,64,256]{2,1,0:T(8,128)(2,1)S(1)} %get-tuple-element.21), channel_id=1, replica_groups=mesh['path'=32,'mp'=2,'period'=4] {'path'}, dimensions={0} | all-to-all | bytes 2097152 | tf_op jit(solution)/shard_map/all_to_all | solution.py:331
  82.8 2.9 %shard_map.72 = (f32[8,384]{1,0:T(8,128)S(1)}, f32[32,256]{1,0:T(8,128)S(1)}) custom-call(f32[24,128]{1,0:T(8,128)S(1)} %fusion.table_ref, bf16[32,64,256]{2,1,0:T(8,128)(2,1)S(1)} %all_to_all.22.recv_ref, bf16[32,8,384]{2,1,0:T(8,128)(2,1)S(1)} %all_to_all.20.recv_ref.index_ref, f32[32,256]{1,0:T(8,128)S(1)} %get-tuple-element.22.own_ref.refs_4_, ...), custom_call_target="tpu_custom_call" | custom-call | flops 67108864 | bytes 8388608 | tf_op jit(solution)/shard_map/pallas_call | solution.py:357
  85.8 0.0 collective-permute-start.1
  85.8 1.2 %collective-permute-done.1.other_ref = f32[8,384]{1,0:T(8,128)S(1)} collective-permute-done((f32[8,384]{1,0:T(8,128)S(1)}, f32[8,384]{1,0:T(8,128)S(1)}, u32[]{:S(2)}, u32[]{:S(2)}) %collective-permute-start.1) | collective-permute-done | bytes 12320 | tf_op jit(solution)/shard_map/ppermute | solution.py:334
  87.0 0.1 shard_map.73
  87.1 14.9 %all_to_all.23.refs_0_ = bf16[32,8,128]{2,1,0:T(8,128)(2,1)S(1)} all-to-all(bf16[32,8,128]{2,1,0:T(8,128)(2,1)S(1)} %get-tuple-element.27), channel_id=1, replica_groups=mesh['path'=32,'mp'=2,'period'=4] {'path'}, dimensions={0} | all-to-all | bytes 131072 | tf_op jit(solution)/shard_map/all_to_all | solution.py:331
  102.0 0.8 shard_map.74
  (1 shorter events, 0.0 us)
Async XLA Ops:
  47.5 1.2 %collective-permute-start = (f32[8,384]{1,0:T(8,128)S(1)}, f32[8,384]{1,0:T(8,128)S(1)}, u32[]{:S(2)}, u32[]{:S(2)}) collective-permute-start(f32[8,384]{1,0:T(8,128)S(1)} %shard_map.70.part_ref), channel_id=1, source_target_pairs={{0,4},{4,0},{1,5},{5,1},{2,6},{6,2},{3,7},{7,3},{8,12},{12,8},{9,1... | collective-permute-start | bytes 36872 | tf_op jit(solution)/shard_map/ppermute | solution.py:334
  85.8 1.2 %collective-permute-start.1 = (f32[8,384]{1,0:T(8,128)S(1)}, f32[8,384]{1,0:T(8,128)S(1)}, u32[]{:S(2)}, u32[]{:S(2)}) collective-permute-start(f32[8,384]{1,0:T(8,128)S(1)} %get-tuple-element.24.part_ref), channel_id=1, source_target_pairs={{0,4},{4,0},{1,5},{5,1},{2,6},{6,2},{3,7},{7,3},{8,12},{12,8},{9,1... | collective-permute-start | bytes 36872 | tf_op jit(solution)/shard_map/ppermute | solution.py:334

commit v5 on v4

v5 whole, which is shorter than its diff:
```python
import jax
import jax.numpy as jnp
from jax import lax
from jax.experimental import pallas as pl
from jax.experimental.pallas import tpu as pltpu
from jax.sharding import PartitionSpec as P

CT_DEV = 32
EPS = 1e-12
CHUNKS = 8
META = 128
LIMIT = 12 << 20
FIRST_LIMIT = 40 << 20
F32 = jnp.float32
BF16 = jnp.bfloat16
VMEM = pl.BlockSpec(memory_space=pltpu.VMEM)
HBM = pl.BlockSpec(memory_space=pltpu.HBM)


def iota(shape, dim):
    return lax.broadcasted_iota(jnp.int32, shape, dim)


def onehot(mask):
    return jnp.where(mask, 1.0, 0.0).astype(BF16)


def dot(a, b, ca, cb):
    return lax.dot_general(a, b, (((ca,), (cb,)), ((), ())), preferred_element_type=F32)


def total(x):
    return jnp.sum(jnp.sum(x, axis=1, keepdims=True), axis=0, keepdims=True)


def load_pairs(ref, rows):
    return jnp.concatenate(
        [ref[pl.ds(0, rows, stride=2), :], ref[pl.ds(1, rows, stride=2), :]], axis=1
    )


def store_pairs(ref, value, rows):
    half = value.shape[1] // 2
    ref[pl.ds(0, rows, stride=2), :] = value[:, :half]
    ref[pl.ds(1, rows, stride=2), :] = value[:, half:]


def pieces(lane, value):
    high = value.astype(BF16).astype(F32)
    rest = value - high
    middle = rest.astype(BF16).astype(F32)
    low = rest - middle
    return jnp.where(lane == 1, high, jnp.where(lane == 2, middle, jnp.where(lane == 3, low, 0.0)))


def sum_pieces(meta):
    lane = iota(meta.shape, 1)
    return total(jnp.where((lane >= 1) & (lane <= 3), meta, 0.0))


def split(x):
    high = x.astype(BF16)
    low = (x - high.astype(F32)).astype(BF16)
    return jnp.concatenate([high, low], axis=0)


def fold(x):
    half = x.shape[0] // 2
    return x[:half] + x[half:]


def data_of(table_ref):
    return load_pairs(table_ref.at[: table_ref.shape[0] - 8], (table_ref.shape[0] - 8) // 2)


def slots_of(table_ref):
    base = table_ref.shape[0] - 8
    slots = META // 2
    both = table_ref[base : base + 1, :].astype(jnp.int32)
    count = table_ref[base + 1 : base + 2, 0:1].astype(jnp.int32)
    return both[:, slots:], both[:, :slots], count


def column_of(row):
    n = row.shape[1]
    return jnp.sum(jnp.where(iota((n, n), 0) == iota((n, n), 1), row, 0), axis=1, keepdims=True)


def placement(cols, count, npath, limit):
    slots = cols.shape[1]
    owner = lax.div(cols, CT_DEV)
    inside = cols - owner * CT_DEV
    owner_col = column_of(owner)
    earlier = iota((slots, slots), 0) < iota((slots, slots), 1)
    same = (owner_col == owner) & earlier
    rank = jnp.sum(jnp.where(same, 1, 0), axis=0, keepdims=True)
    live = iota(cols.shape, 1) < count
    target = jnp.where(live, owner * limit + rank, -1)
    place = onehot(iota((npath * limit, slots), 0) == target)
    return place, inside


def start_tiles(tiles_ref, held, sems):
    step = held.shape[0] // CHUNKS
    copies = []
    for k in range(CHUNKS):
        part = pl.ds(k * step, step)
        copies.append(pltpu.make_async_copy(tiles_ref.at[part], held.at[part], sems.at[k]))
        copies[-1].start()
    return copies


def backward(held, rows, left, copies=None):
    slots, tile = held.shape[0], held.shape[1]
    row_tiles = left.shape[0]
    row_hot = onehot(iota((row_tiles, slots), 0) == rows)
    both = split(left)
    high = dot(row_hot, both[:row_tiles], 0, 0)
    low = dot(row_hot, both[row_tiles:], 0, 0)
    step = slots // CHUNKS
    sub = iota((2 * step, tile), 0)
    out = []
    for k in range(CHUNKS):
        if copies is not None:
            copies[k].wait()
        part = slice(k * step, (k + 1) * step)
        block = jnp.concatenate([high[part], low[part]], axis=0)
        acc = jnp.zeros((2 * step, tile), F32)
        for i in range(step):
            mine = (sub == i) | (sub == i + step)
            acc += dot(jnp.where(mine, block, 0.0).astype(BF16), held[k * step + i], 1, 0)
        out.append(fold(acc).astype(BF16))
    return jnp.concatenate(out, axis=0)


def forward(held, rows, picked, row_tiles):
    slots, tile = held.shape[0], held.shape[1]
    row_hot = jnp.where(iota((row_tiles, slots), 0) == rows, 1.0, 0.0)
    acc = jnp.zeros((row_tiles, tile), F32)
    for s in range(slots):
        lhs = row_hot[:, s : s + 1] * picked[s : s + 1, :]
        acc += dot(lhs.astype(BF16), held[s], 1, 1)
    return acc


def first_kernel(table_ref, tiles_ref, send_ref, held_ref, sems):
    npath, limit, width = send_ref.shape
    copies = start_tiles(tiles_ref, held_ref, sems)
    left = data_of(table_ref)
    rows, cols, count = slots_of(table_ref)
    place, inside = placement(cols, count, npath, limit)
    slots = cols.shape[1]
    meta = jnp.where(iota((slots, META), 1) == 0, column_of(inside) + 1, 0)
    prods = backward(held_ref, rows, left, copies)
    tile = prods.shape[1]
    terms = jnp.concatenate([prods, meta.astype(F32).astype(BF16)], axis=1)
    out = dot(place, terms, 1, 0)
    lane = iota((1, META), 1)
    sent = out[:, :tile]
    extra = pieces(lane, total(left * left)) + pieces(lane - 3, total(sent * sent))
    full = jnp.concatenate([sent, out[:, tile:] + extra], axis=1)
    send_ref[...] = full.astype(BF16).reshape(npath, limit, width)


def hot_of(meta):
    return onehot(meta[:, 0:1].astype(jnp.int32) == iota((meta.shape[0], CT_DEV), 1) + 1)


def first_owner_kernel(recv_ref, send_ref, own_ref, scal_ref):
    npath, limit, width = recv_ref.shape
    tile = width - META
    recv = recv_ref[...].reshape(npath * limit, width)
    meta = recv[:, tile:].astype(F32)
    hot = hot_of(meta)
    own = dot(hot, recv[:, :tile], 0, 0)
    own_ref[...] = own
    per = jnp.sum(meta, axis=0, keepdims=True) * (1.0 / limit)
    scal_ref[...] = jnp.zeros_like(scal_ref)
    scal_ref[0:1, :] = jnp.broadcast_to(sum_pieces(per), (1, META))
    lane = iota(per.shape, 1)
    guess = jnp.sum(jnp.where((lane >= 4) & (lane <= 6), per, 0.0), axis=1, keepdims=True)
    scal_ref[1:2, :] = jnp.broadcast_to(guess, (1, META))
    send_ref[...] = dot(hot, own.astype(BF16), 1, 0).astype(BF16).reshape(npath, limit, tile)


def forward_kernel(table_ref, recv_ref, tail_ref, tiles_ref, part_ref):
    npath, limit, tile = recv_ref.shape
    row_tiles = part_ref.shape[0]
    rows, cols, count = slots_of(table_ref)
    place, _ = placement(cols, count, npath, limit)
    picked = dot(place, recv_ref[...].reshape(npath * limit, tile), 0, 0)
    part_ref[:, :tile] = forward(tiles_ref, rows, picked, row_tiles)
    part_ref[:, tile:] = tail_ref[...]


def second_kernel(
    table_ref, part_ref, other_ref, scal_ref, tiles_ref, send_ref, image_ref, gamma_ref
):
    npath, limit, tile = send_ref.shape
    sums = part_ref[...] + other_ref[...]
    image = sums[:, :tile]
    gamma = sums[1:2, tile : tile + 1] / (scal_ref[0:1, 0:1] + EPS)
    image_ref[...] = image
    gamma_ref[...] = jnp.broadcast_to(gamma, gamma_ref.shape)
    rows, cols, count = slots_of(table_ref)
    place, _ = placement(cols, count, npath, limit)
    prods = backward(tiles_ref, rows, image - gamma * data_of(table_ref))
    send_ref[...] = dot(place, prods, 1, 0).astype(BF16).reshape(npath, limit, tile)


def second_owner_kernel(recv_ref, index_ref, own_ref, send_ref, next_ref, scal_ref):
    npath, limit, tile = recv_ref.shape
    rows = npath * limit
    hot = hot_of(index_ref[:, :, tile:].reshape(rows, META).astype(F32))
    own = dot(hot, recv_ref[...].reshape(rows, tile), 0, 0)
    next_ref[...] = own
    before = own_ref[...]
    scal_ref[...] = jnp.zeros_like(scal_ref)
    for k, value in enumerate((before * before, before * own, own * own)):
        scal_ref[k : k + 1, :] = jnp.broadcast_to(total(value), (1, META))
    send_ref[...] = dot(hot, own.astype(BF16), 1, 0).astype(BF16).reshape(npath, limit, tile)


def third_kernel(table_ref, part_ref, other_ref, image_ref, send_ref, next_ref):
    npath = send_ref.shape[0]
    tile = image_ref.shape[1]
    sums = part_ref[...] + other_ref[...]
    z, x, d = sums[:, :tile], image_ref[...], data_of(table_ref)
    next_ref[...] = z
    values = [total(a * b) for a, b in ((d, d), (d, x), (x, x), (d, z), (x, z), (z, z))]
    values += [sums[k : k + 1, tile : tile + 1] for k in range(3)]
    lane = iota((1, META), 1)
    lines = [pieces(lane, v) for v in values[:8]]
    lines[0] += pieces(lane - 3, values[8])
    message = jnp.concatenate(lines, axis=0).astype(BF16)
    for q in range(npath):
        send_ref[q] = message


def final_kernel(
    total_rows, table_ref, recv_ref, next_ref, image_ref, own0_ref, own1_ref, gamma_ref,
    solution_ref, out_ref,
):
    sums = jnp.sum(recv_ref[...].astype(F32), axis=0)
    dd, dx, xx, dz, xz, zz, vv, vy = [sum_pieces(sums[k : k + 1]) for k in range(8)]
    lane = iota((1, META), 1)
    yy = total(jnp.where((lane >= 4) & (lane <= 6), sums[0:1], 0.0))
    beta0_sq = dd + EPS
    beta0 = jnp.sqrt(beta0_sq)
    alpha0_sq = vv / beta0_sq + EPS
    alpha0 = jnp.sqrt(alpha0_sq)
    scale0 = 1.0 / (beta0 * alpha0)
    beta1_sq = xx - alpha0_sq * (2.0 * dx - alpha0_sq * dd)
    beta1_sq = (jnp.sqrt(jnp.maximum(beta1_sq, 0.0)) * scale0) ** 2 + EPS
    beta1 = jnp.sqrt(beta1_sq)
    kappa = gamma_ref[0:1, 0:1] - alpha0_sq - beta1_sq
    scale1 = scale0 / beta1
    alpha1_sq = jnp.maximum(yy + kappa * (2.0 * vy + kappa * vv), 0.0)
    alpha1_sq = (jnp.sqrt(alpha1_sq) * scale1) ** 2 + EPS
    alpha1 = jnp.sqrt(alpha1_sq)
    scale2 = scale1 / alpha1
    lam, mu = kappa - alpha1_sq, alpha1_sq * alpha0_sq
    norm = zz + lam * lam * xx + mu * mu * dd + 2.0 * (lam * xz + mu * dz + lam * mu * dx)
    beta2 = jnp.sqrt((jnp.sqrt(jnp.maximum(norm, 0.0)) * scale2) ** 2 + EPS)
    rho1 = jnp.sqrt(alpha0_sq + beta1_sq)
    cosine, sine = alpha0 / rho1, beta1 / rho1
    theta = sine * alpha1
    rhobar = -cosine * alpha1
    phi1, phibar = cosine * beta0, sine * beta0
    rho2 = jnp.sqrt(rhobar * rhobar + beta2 * beta2)
    phi2 = rhobar / rho2 * phibar
    right0 = own0_ref[...] * scale0
    right1 = (own1_ref[...] + kappa * own0_ref[...]) * scale2
    search = right1 - (theta / rho1) * right0
    answer = (phi1 / rho1) * right0 + (phi2 / rho2) * search
    store_pairs(solution_ref, answer, answer.shape[0])
    left = (next_ref[...] + lam * image_ref[...] + mu * data_of(table_ref)) * scale2
    left = left * (total_rows**0.5 / beta2)
    store_pairs(out_ref, left, left.shape[0])


def call(kernel, ins, outs, scratch=(), flops=0, moved=0, room=LIMIT):
    shapes = [jax.ShapeDtypeStruct(s, d) for s, d in outs]
    return pl.pallas_call(
        kernel,
        in_specs=ins,
        out_specs=[VMEM] * len(outs),
        out_shape=shapes,
        scratch_shapes=scratch,
        compiler_params=pltpu.CompilerParams(vmem_limit_bytes=room),
        cost_estimate=pl.CostEstimate(flops=flops, bytes_accessed=moved, transcendentals=0),
    )


def on_device(tiles, tile_rows, tile_cols, tile_counts, data):
    slots, tile, _ = tiles.shape
    row_tiles = data.shape[0] // tile
    npath = lax.axis_size("path")
    limit = max(2, max(slots // 8, (slots + npath - 1) // npath))
    named = jnp.concatenate([tile_cols, tile_rows, jnp.broadcast_to(tile_counts, (META,))])
    named = jnp.pad(named.astype(F32), (0, 8 * META - named.shape[0]))
    table = jnp.concatenate([data, named]).reshape(-1, META)
    payload = ((npath, limit, tile), BF16)
    scal = ((8, META), F32)
    own_shape = ((CT_DEV, tile), F32)
    left_shape = ((row_tiles, tile), F32)
    part_shape = ((row_tiles, tile + META), F32)
    work = dict(flops=2 * 8 * tiles.size, moved=2 * tiles.size)

    def swap(x):
        return lax.all_to_all(x, "path", 0, 0, tiled=True)

    def other_half(x):
        return lax.ppermute(x, "mp", [(0, 1), (1, 0)])

    send, tiles = call(
        first_kernel,
        [VMEM, HBM],
        [((npath, limit, tile + META), BF16), (tiles.shape, tiles.dtype)],
        scratch=[pltpu.SemaphoreType.DMA((CHUNKS,))],
        room=FIRST_LIMIT,
        **work,
    )(table, tiles)
    index = swap(send)
    send, own0, scal0 = call(first_owner_kernel, [VMEM], [payload, own_shape, scal])(index)
    pass_forward = call(forward_kernel, [VMEM] * 4, [part_shape], **work)
    (part,) = pass_forward(table, swap(send), scal0, tiles)
    send, image, gamma = call(second_kernel, [VMEM] * 5, [payload, left_shape, scal], **work)(
        table, part, other_half(part), scal0, tiles
    )
    send, own1, scal1 = call(second_owner_kernel, [VMEM] * 3, [payload, own_shape, scal])(
        swap(send), index, own0
    )
    (part,) = pass_forward(table, swap(send), scal1, tiles)
    send, mixed = call(third_kernel, [VMEM] * 4, [((npath, 8, META), BF16), left_shape])(
        table, part, other_half(part), image
    )
    total_rows = row_tiles * tile * npath

    def last(*refs):
        final_kernel(total_rows, *refs)

    solution, left = call(
        last, [VMEM] * 7, [((CT_DEV * 2, tile // 2), F32), ((row_tiles * 2, tile // 2), F32)]
    )(table, swap(send), mixed, image, own0, own1, gamma)
    return solution.reshape(-1), left.reshape(-1)


def solution(mesh):
    placed = (
        P(("path", "mp"), None, None),
        P(("path", "mp")),
        P(("path", "mp")),
        P(("path", "mp")),
        P(("period", "path")),
    )
    return jax.shard_map(
        on_device,
        mesh=mesh,
        in_specs=placed,
        out_specs=(P(("period", "path", "mp")), P(("period", "path"))),
        check_vma=False,
    )
```

time: 103 us -> 97 us (0.942)
  blocking collectives: 84.9 us -> 78.3 us
    all_to_all x4 -> x5, blocking collectives: 84.9 us -> 78.3 us  [swap(): return lax.all_to_all(x, 'path', 0, 0, tiled=True)]
    pallas_call x4 -> x5, Pallas kernels: 11.4 us -> 11.7 us  [the longest x1 4.69 us: on_device(): call(first_kernel, [VMEM, HBM], [((npath, limit, tile + META), BF16), (ti...]
where the time goes in v5:
time: 97 us; the launch traced here: 96.6 us
  blocking collectives  78.3 us (81%)
  Pallas kernels  13.1 us (14%)
  waiting for transfers between devices  2.39 us (2%)
  other arithmetic  1.45 us (1%)
  between operations  1.34 us (1%)
    all_to_all x5, blocking collectives, swap(): return lax.all_to_all(x, 'path', 0, 0, tiled=True)  78.3 us
    pallas_call x1, Pallas kernels, on_device(): call(first_kernel, [VMEM, HBM], [((npath, limit, tile + META), BF16), (ti...  4.69 us
    pallas_call x1, Pallas kernels, on_device(): part, = pass_forward(table, swap(send), scal0, tiles)  2.48 us
    pallas_call x1, Pallas kernels, on_device(): part, = pass_forward(table, swap(send), scal1, tiles)  2.48 us
    ppermute x2, waiting for transfers between devices, other_half(): return lax.ppermute(x, 'mp', [(0, 1), (1, 0)])  2.39 us
  transfers between devices with their start and end apart: 2, of which 2 were waited for; matrix products, arithmetic and copies ran while one was open for 0% of the time, Pallas kernels for 0%

profile of v5, /device:TPU:16, one launch (start us, length us, event | category | flops | bytes accessed | tf_op | source)
XLA Modules:
  0.0 96.6 jit_solution(10993066289150590505)
XLA Ops:
  1.3 0.8 add_convert_fusion
  2.0 0.7 fusion.table_ref.refs_0_
  2.7 4.7 %shard_map.68 = (bf16[32,8,384]{2,1,0:T(8,128)(2,1)S(1)}, bf16[64,256,256]{2,1,0:T(8,128)(2,1)S(1)}) custom-call(f32[24,128]{1,0:T(8,128)S(1)} %fusion.table_ref.refs_0_, bf16[64,256,256]{2,1,0:T(8,128)(2,1)} %tiles_ref.1), custom_call_target="tpu_custom_call" | custom-call | flops 67108864 | bytes 8388608 | tf_op jit(solution)/shard_map/pallas_call | solution.py:316
  7.4 22.4 %all_to_all.25.recv_ref.index_ref = bf16[32,8,384]{2,1,0:T(8,128)(2,1)S(1)} all-to-all(bf16[32,8,384]{2,1,0:T(8,128)(2,1)S(1)} %get-tuple-element.17), channel_id=1, replica_groups=mesh['path'=32,'mp'=2,'period'=4] {'path'}, dimensions={0} | all-to-all | bytes 393216 | tf_op jit(solution)/shard_map/all_to_all | solution.py:311
  29.9 0.4 shard_map.69
  30.3 14.4 %all_to_all.26.recv_ref = bf16[32,8,256]{2,1,0:T(8,128)(2,1)S(1)} all-to-all(bf16[32,8,256]{2,1,0:T(8,128)(2,1)S(1)} %get-tuple-element.18), channel_id=1, replica_groups=mesh['path'=32,'mp'=2,'period'=4] {'path'}, dimensions={0} | all-to-all | bytes 262144 | tf_op jit(solution)/shard_map/all_to_all | solution.py:311
  44.7 2.5 %shard_map.70.part_ref = f32[8,384]{1,0:T(8,128)S(1)} custom-call(f32[24,128]{1,0:T(8,128)S(1)} %fusion.table_ref.refs_0_, bf16[32,8,256]{2,1,0:T(8,128)(2,1)S(1)} %all_to_all.26.recv_ref, f32[8,128]{1,0:T(8,128)S(1)} %get-tuple-element.19.tail_ref.scal_ref, bf16[64,256,256]{2,1,0:T(8,128)(2,1)S(1)} %get-tuple-element.20.tiles_ref), custom_call_target="tpu_custom_call" | custom-call | flops 67108864 | bytes 8388608 | tf_op jit(solution)/shard_map/pallas_call | solution.py:327
  47.2 0.0 collective-permute-start
  47.2 1.2 %collective-permute-done.other_ref = f32[8,384]{1,0:T(8,128)S(1)} collective-permute-done((f32[8,384]{1,0:T(8,128)S(1)}, f32[8,384]{1,0:T(8,128)S(1)}, u32[]{:S(2)}, u32[]{:S(2)}) %collective-permute-start) | collective-permute-done | bytes 12320 | tf_op jit(solution)/shard_map/ppermute | solution.py:314
  48.4 1.6 %shard_map.71 = (bf16[32,8,256]{2,1,0:T(8,128)(2,1)S(1)}, f32[8,256]{1,0:T(8,128)S(1)}, f32[8,128]{1,0:T(8,128)S(1)}) custom-call(f32[24,128]{1,0:T(8,128)S(1)} %fusion.table_ref.refs_0_, f32[8,384]{1,0:T(8,128)S(1)} %shard_map.70.part_ref, f32[8,384]{1,0:T(8,128)S(1)} %collective-permute-done.other_ref, f32[8,128]{1,0:T(8,128)S(1)} %get-tuple-element.19.tail_ref.scal_ref, ...), custom_call_target="tpu_custom_call" | custom-call | flops 67108864 | bytes 8388608 | tf_op jit(solution)/shard_map/pallas_call | solution.py:328
  50.0 14.0 %all_to_all.27.recv_ref = bf16[32,8,256]{2,1,0:T(8,128)(2,1)S(1)} all-to-all(bf16[32,8,256]{2,1,0:T(8,128)(2,1)S(1)} %get-tuple-element.21), channel_id=1, replica_groups=mesh['path'=32,'mp'=2,'period'=4] {'path'}, dimensions={0} | all-to-all | bytes 262144 | tf_op jit(solution)/shard_map/all_to_all | solution.py:311
  64.1 0.4 shard_map.72
  64.5 13.9 %all_to_all.28.recv_ref = bf16[32,8,256]{2,1,0:T(8,128)(2,1)S(1)} all-to-all(bf16[32,8,256]{2,1,0:T(8,128)(2,1)S(1)} %get-tuple-element.23), channel_id=1, replica_groups=mesh['path'=32,'mp'=2,'period'=4] {'path'}, dimensions={0} | all-to-all | bytes 262144 | tf_op jit(solution)/shard_map/all_to_all | solution.py:311
  78.4 2.5 %shard_map.73.part_ref = f32[8,384]{1,0:T(8,128)S(1)} custom-call(f32[24,128]{1,0:T(8,128)S(1)} %fusion.table_ref.refs_0_, bf16[32,8,256]{2,1,0:T(8,128)(2,1)S(1)} %all_to_all.28.recv_ref, f32[8,128]{1,0:T(8,128)S(1)} %get-tuple-element.24.tail_ref, bf16[64,256,256]{2,1,0:T(8,128)(2,1)S(1)} %get-tuple-element.20.tiles_ref), custom_call_target="tpu_custom_call" | custom-call | flops 67108864 | bytes 8388608 | tf_op jit(solution)/shard_map/pallas_call | solution.py:334
  80.9 0.0 collective-permute-start.1
  80.9 1.2 %collective-permute-done.1.other_ref = f32[8,384]{1,0:T(8,128)S(1)} collective-permute-done((f32[8,384]{1,0:T(8,128)S(1)}, f32[8,384]{1,0:T(8,128)S(1)}, u32[]{:S(2)}, u32[]{:S(2)}) %collective-permute-start.1) | collective-permute-done | bytes 12320 | tf_op jit(solution)/shard_map/ppermute | solution.py:314
  82.1 0.1 shard_map.74
  82.3 13.5 %all_to_all.29.refs_1_ = bf16[32,8,128]{2,1,0:T(8,128)(2,1)S(1)} all-to-all(bf16[32,8,128]{2,1,0:T(8,128)(2,1)S(1)} %get-tuple-element.26), channel_id=1, replica_groups=mesh['path'=32,'mp'=2,'period'=4] {'path'}, dimensions={0} | all-to-all | bytes 131072 | tf_op jit(solution)/shard_map/all_to_all | solution.py:311
  95.7 0.9 shard_map.75
  (1 shorter events, 0.0 us)
Async XLA Ops:
  47.2 1.2 %collective-permute-start = (f32[8,384]{1,0:T(8,128)S(1)}, f32[8,384]{1,0:T(8,128)S(1)}, u32[]{:S(2)}, u32[]{:S(2)}) collective-permute-start(f32[8,384]{1,0:T(8,128)S(1)} %shard_map.70.part_ref), channel_id=1, source_target_pairs={{0,4},{4,0},{1,5},{5,1},{2,6},{6,2},{3,7},{7,3},{8,12},{12,8},{9,1... | collective-permute-start | bytes 36872 | tf_op jit(solution)/shard_map/ppermute | solution.py:314
  80.9 1.2 %collective-permute-start.1 = (f32[8,384]{1,0:T(8,128)S(1)}, f32[8,384]{1,0:T(8,128)S(1)}, u32[]{:S(2)}, u32[]{:S(2)}) collective-permute-start(f32[8,384]{1,0:T(8,128)S(1)} %shard_map.73.part_ref), channel_id=1, source_target_pairs={{0,4},{4,0},{1,5},{5,1},{2,6},{6,2},{3,7},{7,3},{8,12},{12,8},{9,1... | collective-permute-start | bytes 36872 | tf_op jit(solution)/shard_map/ppermute | solution.py:314

commit v6 on v5

--- a/solution.py
+++ b/solution.py
@@ -143,12 +143,13 @@
     return acc
 
 
-def first_kernel(table_ref, tiles_ref, send_ref, held_ref, sems):
+def first_kernel(table_ref, tiles_ref, send_ref, held_ref, place_ref, sems):
     npath, limit, width = send_ref.shape
     copies = start_tiles(tiles_ref, held_ref, sems)
     left = data_of(table_ref)
     rows, cols, count = slots_of(table_ref)
     place, inside = placement(cols, count, npath, limit)
+    place_ref[...] = place
     slots = cols.shape[1]
     meta = jnp.where(iota((slots, META), 1) == 0, column_of(inside) + 1, 0)
     prods = backward(held_ref, rows, left, copies)
@@ -183,18 +184,18 @@
     send_ref[...] = dot(hot, own.astype(BF16), 1, 0).astype(BF16).reshape(npath, limit, tile)
 
 
-def forward_kernel(table_ref, recv_ref, tail_ref, tiles_ref, part_ref):
+def forward_kernel(table_ref, place_ref, recv_ref, tail_ref, tiles_ref, part_ref):
     npath, limit, tile = recv_ref.shape
     row_tiles = part_ref.shape[0]
-    rows, cols, count = slots_of(table_ref)
-    place, _ = placement(cols, count, npath, limit)
-    picked = dot(place, recv_ref[...].reshape(npath * limit, tile), 0, 0)
+    rows = slots_of(table_ref)[0]
+    picked = dot(place_ref[...], recv_ref[...].reshape(npath * limit, tile), 0, 0)
     part_ref[:, :tile] = forward(tiles_ref, rows, picked, row_tiles)
     part_ref[:, tile:] = tail_ref[...]
 
 
 def second_kernel(
-    table_ref, part_ref, other_ref, scal_ref, tiles_ref, send_ref, image_ref, gamma_ref
+    table_ref, place_ref, part_ref, other_ref, scal_ref, tiles_ref,
+    send_ref, image_ref, gamma_ref,
 ):
     npath, limit, tile = send_ref.shape
     sums = part_ref[...] + other_ref[...]
@@ -202,10 +203,9 @@
     gamma = sums[1:2, tile : tile + 1] / (scal_ref[0:1, 0:1] + EPS)
     image_ref[...] = image
     gamma_ref[...] = jnp.broadcast_to(gamma, gamma_ref.shape)
-    rows, cols, count = slots_of(table_ref)
-    place, _ = placement(cols, count, npath, limit)
+    rows = slots_of(table_ref)[0]
     prods = backward(tiles_ref, rows, image - gamma * data_of(table_ref))
-    send_ref[...] = dot(place, prods, 1, 0).astype(BF16).reshape(npath, limit, tile)
+    send_ref[...] = dot(place_ref[...], prods, 1, 0).astype(BF16).reshape(npath, limit, tile)
 
 
 def second_owner_kernel(recv_ref, index_ref, own_ref, send_ref, next_ref, scal_ref):
@@ -297,9 +297,13 @@
     row_tiles = data.shape[0] // tile
     npath = lax.axis_size("path")
     limit = max(2, max(slots // 8, (slots + npath - 1) // npath))
-    named = jnp.concatenate([tile_cols, tile_rows, jnp.broadcast_to(tile_counts, (META,))])
-    named = jnp.pad(named.astype(F32), (0, 8 * META - named.shape[0]))
-    table = jnp.concatenate([data, named]).reshape(-1, META)
+    cells = data.shape[0] + 8 * META
+    named, start = 0, data.shape[0]
+    for x in (tile_cols, tile_rows, tile_counts):
+        named += jnp.pad(x, (start, cells - start - x.shape[0]))
+        start += x.shape[0]
+    table = named.astype(F32) + jnp.pad(data, (0, cells - data.shape[0]))
+    table = table.reshape(-1, META)
     payload = ((npath, limit, tile), BF16)
     scal = ((8, META), F32)
     own_shape = ((CT_DEV, tile), F32)
@@ -313,25 +317,29 @@
     def other_half(x):
         return lax.ppermute(x, "mp", [(0, 1), (1, 0)])
 
-    send, tiles = call(
+    send, tiles, place = call(
         first_kernel,
         [VMEM, HBM],
-        [((npath, limit, tile + META), BF16), (tiles.shape, tiles.dtype)],
+        [
+            ((npath, limit, tile + META), BF16),
+            (tiles.shape, tiles.dtype),
+            ((npath * limit, slots), BF16),
+        ],
         scratch=[pltpu.SemaphoreType.DMA((CHUNKS,))],
         room=FIRST_LIMIT,
         **work,
     )(table, tiles)
     index = swap(send)
     send, own0, scal0 = call(first_owner_kernel, [VMEM], [payload, own_shape, scal])(index)
-    pass_forward = call(forward_kernel, [VMEM] * 4, [part_shape], **work)
-    (part,) = pass_forward(table, swap(send), scal0, tiles)
-    send, image, gamma = call(second_kernel, [VMEM] * 5, [payload, left_shape, scal], **work)(
-        table, part, other_half(part), scal0, tiles
+    pass_forward = call(forward_kernel, [VMEM] * 5, [part_shape], **work)
+    (part,) = pass_forward(table, place, swap(send), scal0, tiles)
+    send, image, gamma = call(second_kernel, [VMEM] * 6, [payload, left_shape, scal], **work)(
+        table, place, part, other_half(part), scal0, tiles
     )
     send, own1, scal1 = call(second_owner_kernel, [VMEM] * 3, [payload, own_shape, scal])(
         swap(send), index, own0
     )
-    (part,) = pass_forward(table, swap(send), scal1, tiles)
+    (part,) = pass_forward(table, place, swap(send), scal1, tiles)
     send, mixed = call(third_kernel, [VMEM] * 4, [((npath, 8, META), BF16), left_shape])(
         table, part, other_half(part), image
     )

time: 97 us -> 96 us (0.990)
  no operation moved by 1% of the time
where the time goes in v6:
time: 96 us; the launch traced here: 95.7 us
  blocking collectives  78.2 us (81%)
  Pallas kernels  12.9 us (13%)
  waiting for transfers between devices  2.39 us (2%)
  between operations  1.34 us (1%)
    all_to_all x5, blocking collectives, swap(): return lax.all_to_all(x, 'path', 0, 0, tiled=True)  78.2 us
    pallas_call x1, Pallas kernels, on_device(): call(first_kernel, [VMEM, HBM], [((npath, limit, tile + META), BF16), (ti...  4.69 us
    ppermute x2, waiting for transfers between devices, other_half(): return lax.ppermute(x, 'mp', [(0, 1), (1, 0)])  2.39 us
    pallas_call x1, Pallas kernels, on_device(): part, = pass_forward(table, place, swap(send), scal0, tiles)  2.36 us
    pallas_call x1, Pallas kernels, on_device(): part, = pass_forward(table, place, swap(send), scal1, tiles)  2.36 us
  transfers between devices with their start and end apart: 2, of which 2 were waited for; matrix products, arithmetic and copies ran while one was open for 0% of the time, Pallas kernels for 0%

profile of v6, /device:TPU:16, one launch (start us, length us, event | category | flops | bytes accessed | tf_op | source)
XLA Modules:
  0.0 95.7 jit_solution(8779233402846046810)
XLA Ops:
  1.3 0.8 add_bitcast_fusion.table_ref.refs_0_
  2.1 4.7 %shard_map.68 = (bf16[32,8,384]{2,1,0:T(8,128)(2,1)S(1)}, bf16[64,256,256]{2,1,0:T(8,128)(2,1)S(1)}, bf16[256,64]{1,0:T(8,128)(2,1)S(1)}) custom-call(f32[24,128]{1,0:T(8,128)S(1)} %add_bitcast_fusion.table_ref.refs_0_, bf16[64,256,256]{2,1,0:T(8,128)(2,1)} %tiles_ref.1), custom_call_target="tpu_custom_call" | custom-call | flops 67108864 | bytes 8388608 | tf_op jit(solution)/shard_map/pallas_call | solution.py:320
  6.8 22.4 %all_to_all.25.recv_ref.index_ref = bf16[32,8,384]{2,1,0:T(8,128)(2,1)S(1)} all-to-all(bf16[32,8,384]{2,1,0:T(8,128)(2,1)S(1)} %get-tuple-element.19), channel_id=1, replica_groups=mesh['path'=32,'mp'=2,'period'=4] {'path'}, dimensions={0} | all-to-all | bytes 393216 | tf_op jit(solution)/shard_map/all_to_all | solution.py:315
  29.2 0.4 shard_map.69
  29.6 14.4 %all_to_all.26.recv_ref = bf16[32,8,256]{2,1,0:T(8,128)(2,1)S(1)} all-to-all(bf16[32,8,256]{2,1,0:T(8,128)(2,1)S(1)} %get-tuple-element.20), channel_id=1, replica_groups=mesh['path'=32,'mp'=2,'period'=4] {'path'}, dimensions={0} | all-to-all | bytes 262144 | tf_op jit(solution)/shard_map/all_to_all | solution.py:315
  44.0 2.4 %shard_map.70.part_ref = f32[8,384]{1,0:T(8,128)S(1)} custom-call(f32[24,128]{1,0:T(8,128)S(1)} %add_bitcast_fusion.table_ref.refs_0_, bf16[256,64]{1,0:T(8,128)(2,1)S(1)} %get-tuple-element.18.place_ref, bf16[32,8,256]{2,1,0:T(8,128)(2,1)S(1)} %all_to_all.26.recv_ref, f32[8,128]{1,0:T(8,128)S(1)} %get-tuple-element.21.tail_ref.scal_ref, ...), custom_call_target="tpu_custom_call" | custom-call | flops 67108864 | bytes 8388608 | tf_op jit(solution)/shard_map/pallas_call | solution.py:335
  46.4 0.0 collective-permute-start
  46.4 1.2 %collective-permute-done.other_ref = f32[8,384]{1,0:T(8,128)S(1)} collective-permute-done((f32[8,384]{1,0:T(8,128)S(1)}, f32[8,384]{1,0:T(8,128)S(1)}, u32[]{:S(2)}, u32[]{:S(2)}) %collective-permute-start) | collective-permute-done | bytes 12320 | tf_op jit(solution)/shard_map/ppermute | solution.py:318
  47.6 1.6 %shard_map.71 = (bf16[32,8,256]{2,1,0:T(8,128)(2,1)S(1)}, f32[8,256]{1,0:T(8,128)S(1)}, f32[8,128]{1,0:T(8,128)S(1)}) custom-call(f32[24,128]{1,0:T(8,128)S(1)} %add_bitcast_fusion.table_ref.refs_0_, bf16[256,64]{1,0:T(8,128)(2,1)S(1)} %get-tuple-element.18.place_ref, f32[8,384]{1,0:T(8,128)S(1)} %shard_map.70.part_ref, ...), custom_call_target="tpu_custom_call" | custom-call | flops 67108864 | bytes 8388608 | tf_op jit(solution)/shard_map/pallas_call | solution.py:336
  49.2 14.0 %all_to_all.27.recv_ref = bf16[32,8,256]{2,1,0:T(8,128)(2,1)S(1)} all-to-all(bf16[32,8,256]{2,1,0:T(8,128)(2,1)S(1)} %get-tuple-element.23), channel_id=1, replica_groups=mesh['path'=32,'mp'=2,'period'=4] {'path'}, dimensions={0} | all-to-all | bytes 262144 | tf_op jit(solution)/shard_map/all_to_all | solution.py:315
  63.3 0.4 shard_map.72
  63.7 13.9 %all_to_all.28.recv_ref = bf16[32,8,256]{2,1,0:T(8,128)(2,1)S(1)} all-to-all(bf16[32,8,256]{2,1,0:T(8,128)(2,1)S(1)} %get-tuple-element.25), channel_id=1, replica_groups=mesh['path'=32,'mp'=2,'period'=4] {'path'}, dimensions={0} | all-to-all | bytes 262144 | tf_op jit(solution)/shard_map/all_to_all | solution.py:315
  77.6 2.4 %shard_map.73.part_ref = f32[8,384]{1,0:T(8,128)S(1)} custom-call(f32[24,128]{1,0:T(8,128)S(1)} %add_bitcast_fusion.table_ref.refs_0_, bf16[256,64]{1,0:T(8,128)(2,1)S(1)} %get-tuple-element.18.place_ref, bf16[32,8,256]{2,1,0:T(8,128)(2,1)S(1)} %all_to_all.28.recv_ref, f32[8,128]{1,0:T(8,128)S(1)} %get-tuple-element.26.tail_ref, ...), custom_call_target="tpu_custom_call" | custom-call | flops 67108864 | bytes 8388608 | tf_op jit(solution)/shard_map/pallas_call | solution.py:342
  80.0 0.0 collective-permute-start.1
  80.0 1.2 %collective-permute-done.1.other_ref = f32[8,384]{1,0:T(8,128)S(1)} collective-permute-done((f32[8,384]{1,0:T(8,128)S(1)}, f32[8,384]{1,0:T(8,128)S(1)}, u32[]{:S(2)}, u32[]{:S(2)}) %collective-permute-start.1) | collective-permute-done | bytes 12320 | tf_op jit(solution)/shard_map/ppermute | solution.py:318
  81.2 0.1 shard_map.74
  81.3 13.5 %all_to_all.29.refs_1_ = bf16[32,8,128]{2,1,0:T(8,128)(2,1)S(1)} all-to-all(bf16[32,8,128]{2,1,0:T(8,128)(2,1)S(1)} %get-tuple-element.28), channel_id=1, replica_groups=mesh['path'=32,'mp'=2,'period'=4] {'path'}, dimensions={0} | all-to-all | bytes 131072 | tf_op jit(solution)/shard_map/all_to_all | solution.py:315
  94.8 0.9 shard_map.75
Async XLA Ops:
  46.4 1.2 %collective-permute-start = (f32[8,384]{1,0:T(8,128)S(1)}, f32[8,384]{1,0:T(8,128)S(1)}, u32[]{:S(2)}, u32[]{:S(2)}) collective-permute-start(f32[8,384]{1,0:T(8,128)S(1)} %shard_map.70.part_ref), channel_id=1, source_target_pairs={{0,4},{4,0},{1,5},{5,1},{2,6},{6,2},{3,7},{7,3},{8,12},{12,8},{9,1... | collective-permute-start | bytes 36872 | tf_op jit(solution)/shard_map/ppermute | solution.py:318
  80.0 1.2 %collective-permute-start.1 = (f32[8,384]{1,0:T(8,128)S(1)}, f32[8,384]{1,0:T(8,128)S(1)}, u32[]{:S(2)}, u32[]{:S(2)}) collective-permute-start(f32[8,384]{1,0:T(8,128)S(1)} %shard_map.73.part_ref), channel_id=1, source_target_pairs={{0,4},{4,0},{1,5},{5,1},{2,6},{6,2},{3,7},{7,3},{8,12},{12,8},{9,1... | collective-permute-start | bytes 36872 | tf_op jit(solution)/shard_map/ppermute | solution.py:318

commit v7 on v6

--- a/solution.py
+++ b/solution.py
@@ -14,6 +14,7 @@
 F32 = jnp.float32
 BF16 = jnp.bfloat16
 VMEM = pl.BlockSpec(memory_space=pltpu.VMEM)
+SMEM = pl.BlockSpec(memory_space=pltpu.SMEM)
 HBM = pl.BlockSpec(memory_space=pltpu.HBM)
 
 
@@ -110,7 +111,7 @@
     return copies
 
 
-def backward(held, rows, left, copies=None):
+def backward_parts(held, rows, left, copies=None):
     slots, tile = held.shape[0], held.shape[1]
     row_tiles = left.shape[0]
     row_hot = onehot(iota((row_tiles, slots), 0) == rows)
@@ -119,7 +120,6 @@
     low = dot(row_hot, both[row_tiles:], 0, 0)
     step = slots // CHUNKS
     sub = iota((2 * step, tile), 0)
-    out = []
     for k in range(CHUNKS):
         if copies is not None:
             copies[k].wait()
@@ -129,8 +129,11 @@
         for i in range(step):
             mine = (sub == i) | (sub == i + step)
             acc += dot(jnp.where(mine, block, 0.0).astype(BF16), held[k * step + i], 1, 0)
-        out.append(fold(acc).astype(BF16))
-    return jnp.concatenate(out, axis=0)
+        yield fold(acc).astype(BF16)
+
+
+def backward(held, rows, left):
+    return jnp.concatenate(list(backward_parts(held, rows, left)), axis=0)
 
 
 def forward(held, rows, picked, row_tiles):
@@ -143,23 +146,50 @@
     return acc
 
 
-def first_kernel(table_ref, tiles_ref, send_ref, held_ref, place_ref, sems):
+def first_kernel(
+    data_ref, cols_ref, rows_ref, count_ref, tiles_ref,
+    send_ref, held_ref, place_ref, table_ref, cols_buf, rows_buf, sems, small,
+):
     npath, limit, width = send_ref.shape
+    lines = data_ref.shape[0]
+    pairs = (
+        (data_ref, table_ref.at[:lines]), (cols_ref, cols_buf), (rows_ref, rows_buf)
+    )
+    loads = [pltpu.make_async_copy(a, b, small.at[k]) for k, (a, b) in enumerate(pairs)]
+    for load in loads:
+        load.start()
     copies = start_tiles(tiles_ref, held_ref, sems)
+    for load in loads:
+        load.wait()
+    named = jnp.concatenate([cols_buf[...], rows_buf[...]], axis=1).astype(F32)
+    table_ref[lines:, :] = jnp.where(iota((8, META), 0) == 0, named, 1.0 * count_ref[0])
     left = data_of(table_ref)
     rows, cols, count = slots_of(table_ref)
     place, inside = placement(cols, count, npath, limit)
     place_ref[...] = place
     slots = cols.shape[1]
     meta = jnp.where(iota((slots, META), 1) == 0, column_of(inside) + 1, 0)
-    prods = backward(held_ref, rows, left, copies)
-    tile = prods.shape[1]
-    terms = jnp.concatenate([prods, meta.astype(F32).astype(BF16)], axis=1)
-    out = dot(place, terms, 1, 0)
+    meta = meta.astype(F32).astype(BF16)
+    live = column_of(jnp.where(iota(cols.shape, 1) < count, 1, 0)).astype(F32)
+    tile = left.shape[1]
+    parts, norm = [], jnp.zeros((1, 1), F32)
+    for k, part in enumerate(backward_parts(held_ref, rows, left, copies)):
+        step = part.shape[0]
+        kept = part.astype(F32) * live[k * step : (k + 1) * step]
+        norm += total(kept * kept)
+        parts.append(part)
+        if k >= CHUNKS - 2:
+            before = jnp.zeros(((k + 1) * step - len(parts) * step, tile), BF16)
+            after = jnp.zeros((slots - (k + 1) * step, tile), BF16)
+            terms = jnp.concatenate([x for x in (before, *parts, after) if x.shape[0]], axis=0)
+            if k == CHUNKS - 2:
+                out = dot(place, jnp.concatenate([terms, meta], axis=1), 1, 0)
+            else:
+                last = dot(place, terms, 1, 0)
+            parts = []
     lane = iota((1, META), 1)
-    sent = out[:, :tile]
-    extra = pieces(lane, total(left * left)) + pieces(lane - 3, total(sent * sent))
-    full = jnp.concatenate([sent, out[:, tile:] + extra], axis=1)
+    extra = pieces(lane, total(left * left)) + pieces(lane - 3, norm)
+    full = jnp.concatenate([out[:, :tile] + last, out[:, tile:] + extra], axis=1)
     send_ref[...] = full.astype(BF16).reshape(npath, limit, width)
 
 
@@ -297,13 +327,7 @@
     row_tiles = data.shape[0] // tile
     npath = lax.axis_size("path")
     limit = max(2, max(slots // 8, (slots + npath - 1) // npath))
-    cells = data.shape[0] + 8 * META
-    named, start = 0, data.shape[0]
-    for x in (tile_cols, tile_rows, tile_counts):
-        named += jnp.pad(x, (start, cells - start - x.shape[0]))
-        start += x.shape[0]
-    table = named.astype(F32) + jnp.pad(data, (0, cells - data.shape[0]))
-    table = table.reshape(-1, META)
+    data = data.reshape(-1, META)
     payload = ((npath, limit, tile), BF16)
     scal = ((8, META), F32)
     own_shape = ((CT_DEV, tile), F32)
@@ -317,18 +341,25 @@
     def other_half(x):
         return lax.ppermute(x, "mp", [(0, 1), (1, 0)])
 
-    send, tiles, place = call(
+    inputs = (data, tile_cols.reshape(1, slots), tile_rows.reshape(1, slots), tile_counts, tiles)
+    send, tiles, place, table = call(
         first_kernel,
-        [VMEM, HBM],
+        [HBM] * 3 + [SMEM, HBM],
         [
             ((npath, limit, tile + META), BF16),
             (tiles.shape, tiles.dtype),
             ((npath * limit, slots), BF16),
+            ((data.shape[0] + 8, META), F32),
         ],
-        scratch=[pltpu.SemaphoreType.DMA((CHUNKS,))],
+        scratch=[
+            pltpu.VMEM((1, slots), jnp.int32),
+            pltpu.VMEM((1, slots), jnp.int32),
+            pltpu.SemaphoreType.DMA((CHUNKS,)),
+            pltpu.SemaphoreType.DMA((3,)),
+        ],
         room=FIRST_LIMIT,
         **work,
-    )(table, tiles)
+    )(*[x if x.size == 1 else pltpu.with_memory_space_constraint(x, pltpu.HBM) for x in inputs])
     index = swap(send)
     send, own0, scal0 = call(first_owner_kernel, [VMEM], [payload, own_shape, scal])(index)
     pass_forward = call(forward_kernel, [VMEM] * 5, [part_shape], **work)

time: 96 us -> 97.8 us (1.019)
  Pallas kernels: 12.9 us -> 15.5 us
    pallas_call x1, Pallas kernels: 4.69 us -> 7.32 us  [on_device(): call(first_kernel, [HBM] * 3 + [SMEM, HBM], [((npath, limit, tile + META)...]
where the time goes in v7:
time: 97.8 us; the launch traced here: 97.5 us
  blocking collectives  78.3 us (80%)
  Pallas kernels  15.5 us (16%)
  waiting for transfers between devices  2.39 us (2%)
  between operations  1.34 us (1%)
    all_to_all x5, blocking collectives, swap(): return lax.all_to_all(x, 'path', 0, 0, tiled=True)  78.3 us
    pallas_call x1, Pallas kernels, on_device(): call(first_kernel, [HBM] * 3 + [SMEM, HBM], [((npath, limit, tile + META)...  7.32 us
    ppermute x2, waiting for transfers between devices, other_half(): return lax.ppermute(x, 'mp', [(0, 1), (1, 0)])  2.39 us
    pallas_call x1, Pallas kernels, on_device(): part, = pass_forward(table, place, swap(send), scal1, tiles)  2.36 us
    pallas_call x1, Pallas kernels, on_device(): part, = pass_forward(table, place, swap(send), scal0, tiles)  2.35 us
  transfers between devices with their start and end apart: 2, of which 2 were waited for; matrix products, arithmetic and copies ran while one was open for 0% of the time, Pallas kernels for 0%

profile of v7, /device:TPU:16, one launch (start us, length us, event | category | flops | bytes accessed | tf_op | source)
XLA Modules:
  0.0 97.5 jit_solution(2917960147187386152)
XLA Ops:
  1.3 7.3 %shard_map.68 = (bf16[32,8,384]{2,1,0:T(8,128)(2,1)S(1)}, bf16[64,256,256]{2,1,0:T(8,128)(2,1)S(1)}, bf16[256,64]{1,0:T(8,128)(2,1)S(1)}, f32[24,128]{1,0:T(8,128)S(1)}) custom-call(f32[16,128]{1,0:T(8,128)} %bitcast.5, s32[1,64]{1,0:T(1,128)} %bitcast.6, s32[1,64]{1,0:T(1,128)} %bitcast.7, s32[1]{0:T(128)S(6)} %copy.7.count_ref, bf16[64,256,256]{2,1,0:T(8,128)(2,1)} %tiles_ref.1), custom_call_target="tpu_custom_call" | custom-call | flops 67108864 | bytes 8388608 | tf_op jit(solution)/shard_map/pallas_call | solution.py:345
  8.6 22.4 %all_to_all.25.recv_ref.index_ref = bf16[32,8,384]{2,1,0:T(8,128)(2,1)S(1)} all-to-all(bf16[32,8,384]{2,1,0:T(8,128)(2,1)S(1)} %get-tuple-element.21), channel_id=1, replica_groups=mesh['path'=32,'mp'=2,'period'=4] {'path'}, dimensions={0} | all-to-all | bytes 393216 | tf_op jit(solution)/shard_map/all_to_all | solution.py:339
  31.0 0.4 shard_map.69
  31.5 14.4 %all_to_all.26.recv_ref = bf16[32,8,256]{2,1,0:T(8,128)(2,1)S(1)} all-to-all(bf16[32,8,256]{2,1,0:T(8,128)(2,1)S(1)} %get-tuple-element.22), channel_id=1, replica_groups=mesh['path'=32,'mp'=2,'period'=4] {'path'}, dimensions={0} | all-to-all | bytes 262144 | tf_op jit(solution)/shard_map/all_to_all | solution.py:339
  45.9 2.4 %shard_map.70.part_ref = f32[8,384]{1,0:T(8,128)S(1)} custom-call(f32[24,128]{1,0:T(8,128)S(1)} %get-tuple-element.19.table_ref.refs_0_, bf16[256,64]{1,0:T(8,128)(2,1)S(1)} %get-tuple-element.20.place_ref, bf16[32,8,256]{2,1,0:T(8,128)(2,1)S(1)} %all_to_all.26.recv_ref, f32[8,128]{1,0:T(8,128)S(1)} %get-tuple-element.23.tail_ref.scal_ref, ...), custom_call_target="tpu_custom_call" | custom-call | flops 67108864 | bytes 8388608 | tf_op jit(solution)/shard_map/pallas_call | solution.py:366
  48.2 0.0 collective-permute-start
  48.2 1.2 %collective-permute-done.other_ref = f32[8,384]{1,0:T(8,128)S(1)} collective-permute-done((f32[8,384]{1,0:T(8,128)S(1)}, f32[8,384]{1,0:T(8,128)S(1)}, u32[]{:S(2)}, u32[]{:S(2)}) %collective-permute-start) | collective-permute-done | bytes 12320 | tf_op jit(solution)/shard_map/ppermute | solution.py:342
  49.4 1.6 %shard_map.71 = (bf16[32,8,256]{2,1,0:T(8,128)(2,1)S(1)}, f32[8,256]{1,0:T(8,128)S(1)}, f32[8,128]{1,0:T(8,128)S(1)}) custom-call(f32[24,128]{1,0:T(8,128)S(1)} %get-tuple-element.19.table_ref.refs_0_, bf16[256,64]{1,0:T(8,128)(2,1)S(1)} %get-tuple-element.20.place_ref, f32[8,384]{1,0:T(8,128)S(1)} %shard_map.70.part_ref, ...), custom_call_target="tpu_custom_call" | custom-call | flops 67108864 | bytes 8388608 | tf_op jit(solution)/shard_map/pallas_call | solution.py:367
  51.1 14.0 %all_to_all.27.recv_ref = bf16[32,8,256]{2,1,0:T(8,128)(2,1)S(1)} all-to-all(bf16[32,8,256]{2,1,0:T(8,128)(2,1)S(1)} %get-tuple-element.25), channel_id=1, replica_groups=mesh['path'=32,'mp'=2,'period'=4] {'path'}, dimensions={0} | all-to-all | bytes 262144 | tf_op jit(solution)/shard_map/all_to_all | solution.py:339
  65.1 0.4 shard_map.72
  65.5 13.9 %all_to_all.28.recv_ref = bf16[32,8,256]{2,1,0:T(8,128)(2,1)S(1)} all-to-all(bf16[32,8,256]{2,1,0:T(8,128)(2,1)S(1)} %get-tuple-element.27), channel_id=1, replica_groups=mesh['path'=32,'mp'=2,'period'=4] {'path'}, dimensions={0} | all-to-all | bytes 262144 | tf_op jit(solution)/shard_map/all_to_all | solution.py:339
  79.5 2.4 %shard_map.73.part_ref = f32[8,384]{1,0:T(8,128)S(1)} custom-call(f32[24,128]{1,0:T(8,128)S(1)} %get-tuple-element.19.table_ref.refs_0_, bf16[256,64]{1,0:T(8,128)(2,1)S(1)} %get-tuple-element.20.place_ref, bf16[32,8,256]{2,1,0:T(8,128)(2,1)S(1)} %all_to_all.28.recv_ref, f32[8,128]{1,0:T(8,128)S(1)} %get-tuple-element.28.tail_ref, ...), custom_call_target="tpu_custom_call" | custom-call | flops 67108864 | bytes 8388608 | tf_op jit(solution)/shard_map/pallas_call | solution.py:373
  81.8 0.0 collective-permute-start.1
  81.8 1.2 %collective-permute-done.1.other_ref = f32[8,384]{1,0:T(8,128)S(1)} collective-permute-done((f32[8,384]{1,0:T(8,128)S(1)}, f32[8,384]{1,0:T(8,128)S(1)}, u32[]{:S(2)}, u32[]{:S(2)}) %collective-permute-start.1) | collective-permute-done | bytes 12320 | tf_op jit(solution)/shard_map/ppermute | solution.py:342
  83.0 0.1 shard_map.74
  83.2 13.5 %all_to_all.29.refs_1_ = bf16[32,8,128]{2,1,0:T(8,128)(2,1)S(1)} all-to-all(bf16[32,8,128]{2,1,0:T(8,128)(2,1)S(1)} %get-tuple-element.30), channel_id=1, replica_groups=mesh['path'=32,'mp'=2,'period'=4] {'path'}, dimensions={0} | all-to-all | bytes 131072 | tf_op jit(solution)/shard_map/all_to_all | solution.py:339
  96.6 0.9 shard_map.75
Async XLA Ops:
  48.2 1.2 %collective-permute-start = (f32[8,384]{1,0:T(8,128)S(1)}, f32[8,384]{1,0:T(8,128)S(1)}, u32[]{:S(2)}, u32[]{:S(2)}) collective-permute-start(f32[8,384]{1,0:T(8,128)S(1)} %shard_map.70.part_ref), channel_id=1, source_target_pairs={{0,4},{4,0},{1,5},{5,1},{2,6},{6,2},{3,7},{7,3},{8,12},{12,8},{9,1... | collective-permute-start | bytes 36872 | tf_op jit(solution)/shard_map/ppermute | solution.py:342
  81.8 1.2 %collective-permute-start.1 = (f32[8,384]{1,0:T(8,128)S(1)}, f32[8,384]{1,0:T(8,128)S(1)}, u32[]{:S(2)}, u32[]{:S(2)}) collective-permute-start(f32[8,384]{1,0:T(8,128)S(1)} %shard_map.73.part_ref), channel_id=1, source_target_pairs={{0,4},{4,0},{1,5},{5,1},{2,6},{6,2},{3,7},{7,3},{8,12},{12,8},{9,1... | collective-permute-start | bytes 36872 | tf_op jit(solution)/shard_map/ppermute | solution.py:342

commit v8 on v6

--- a/solution.py
+++ b/solution.py
@@ -8,9 +8,10 @@
 CT_DEV = 32
 EPS = 1e-12
 CHUNKS = 8
+TURNED = 8
 META = 128
 LIMIT = 12 << 20
-FIRST_LIMIT = 40 << 20
+FIRST_LIMIT = 16 << 20
 F32 = jnp.float32
 BF16 = jnp.bfloat16
 VMEM = pl.BlockSpec(memory_space=pltpu.VMEM)
@@ -110,7 +111,7 @@
     return copies
 
 
-def backward(held, rows, left, copies=None):
+def backward(held, rows, left, copies=None, turned=None):
     slots, tile = held.shape[0], held.shape[1]
     row_tiles = left.shape[0]
     row_hot = onehot(iota((row_tiles, slots), 0) == rows)
@@ -130,20 +131,29 @@
             mine = (sub == i) | (sub == i + step)
             acc += dot(jnp.where(mine, block, 0.0).astype(BF16), held[k * step + i], 1, 0)
         out.append(fold(acc).astype(BF16))
+        if turned is not None and k < CHUNKS - 1:
+            for i in range(TURNED):
+                turned[k * TURNED + i] = held[k * step + i].T
     return jnp.concatenate(out, axis=0)
 
 
-def forward(held, rows, picked, row_tiles):
+def forward(held, turned, rows, picked, row_tiles):
     slots, tile = held.shape[0], held.shape[1]
     row_hot = jnp.where(iota((row_tiles, slots), 0) == rows, 1.0, 0.0)
     acc = jnp.zeros((row_tiles, tile), F32)
     for s in range(slots):
         lhs = row_hot[:, s : s + 1] * picked[s : s + 1, :]
-        acc += dot(lhs.astype(BF16), held[s], 1, 1)
+        k, i = divmod(s, slots // CHUNKS)
+        if i < TURNED and k < CHUNKS - 1:
+            acc += dot(lhs.astype(BF16), turned[k * TURNED + i], 1, 0)
+        else:
+            acc += dot(lhs.astype(BF16), held[s], 1, 1)
     return acc
 
 
-def first_kernel(table_ref, tiles_ref, send_ref, held_ref, place_ref, sems):
+def first_kernel(
+    table_ref, tiles_ref, send_ref, held_ref, place_ref, turned_ref, sems
+):
     npath, limit, width = send_ref.shape
     copies = start_tiles(tiles_ref, held_ref, sems)
     left = data_of(table_ref)
@@ -152,7 +162,7 @@
     place_ref[...] = place
     slots = cols.shape[1]
     meta = jnp.where(iota((slots, META), 1) == 0, column_of(inside) + 1, 0)
-    prods = backward(held_ref, rows, left, copies)
+    prods = backward(held_ref, rows, left, copies, turned_ref)
     tile = prods.shape[1]
     terms = jnp.concatenate([prods, meta.astype(F32).astype(BF16)], axis=1)
     out = dot(place, terms, 1, 0)
@@ -184,12 +194,14 @@
     send_ref[...] = dot(hot, own.astype(BF16), 1, 0).astype(BF16).reshape(npath, limit, tile)
 
 
-def forward_kernel(table_ref, place_ref, recv_ref, tail_ref, tiles_ref, part_ref):
+def forward_kernel(
+    table_ref, place_ref, recv_ref, tail_ref, tiles_ref, turned_ref, part_ref
+):
     npath, limit, tile = recv_ref.shape
     row_tiles = part_ref.shape[0]
     rows = slots_of(table_ref)[0]
     picked = dot(place_ref[...], recv_ref[...].reshape(npath * limit, tile), 0, 0)
-    part_ref[:, :tile] = forward(tiles_ref, rows, picked, row_tiles)
+    part_ref[:, :tile] = forward(tiles_ref, turned_ref, rows, picked, row_tiles)
     part_ref[:, tile:] = tail_ref[...]
 
 
@@ -317,29 +329,30 @@
     def other_half(x):
         return lax.ppermute(x, "mp", [(0, 1), (1, 0)])
 
-    send, tiles, place = call(
+    send, tiles, place, turned = call(
         first_kernel,
         [VMEM, HBM],
         [
             ((npath, limit, tile + META), BF16),
             (tiles.shape, tiles.dtype),
             ((npath * limit, slots), BF16),
+            (((CHUNKS - 1) * TURNED, tile, tile), tiles.dtype),
         ],
         scratch=[pltpu.SemaphoreType.DMA((CHUNKS,))],
         room=FIRST_LIMIT,
         **work,
-    )(table, tiles)
+    )(table, pltpu.with_memory_space_constraint(tiles, pltpu.HBM))
     index = swap(send)
     send, own0, scal0 = call(first_owner_kernel, [VMEM], [payload, own_shape, scal])(index)
-    pass_forward = call(forward_kernel, [VMEM] * 5, [part_shape], **work)
-    (part,) = pass_forward(table, place, swap(send), scal0, tiles)
+    pass_forward = call(forward_kernel, [VMEM] * 6, [part_shape], **work)
+    (part,) = pass_forward(table, place, swap(send), scal0, tiles, turned)
     send, image, gamma = call(second_kernel, [VMEM] * 6, [payload, left_shape, scal], **work)(
         table, place, part, other_half(part), scal0, tiles
     )
     send, own1, scal1 = call(second_owner_kernel, [VMEM] * 3, [payload, own_shape, scal])(
         swap(send), index, own0
     )
-    (part,) = pass_forward(table, place, swap(send), scal1, tiles)
+    (part,) = pass_forward(table, place, swap(send), scal1, tiles, turned)
     send, mixed = call(third_kernel, [VMEM] * 4, [((npath, 8, META), BF16), left_shape])(
         table, part, other_half(part), image
     )

time: 96 us -> 94.2 us (0.981)
  Pallas kernels: 12.9 us -> 11.1 us
    pallas_call x2, Pallas kernels: 4.71 us -> 2.91 us  [the longest x1 1.45 us: on_device(): part, = pass_forward(table, place, swap(send), scal0, tiles, turned)]
where the time goes in v8:
time: 94.2 us; the launch traced here: 93.9 us
  blocking collectives  78.3 us (83%)
  Pallas kernels  11.1 us (12%)
  waiting for transfers between devices  2.38 us (3%)
  between operations  1.34 us (1%)
    all_to_all x5, blocking collectives, swap(): return lax.all_to_all(x, 'path', 0, 0, tiled=True)  78.3 us
    pallas_call x1, Pallas kernels, on_device(): call(first_kernel, [VMEM, HBM], [((npath, limit, tile + META), BF16), (ti...  4.69 us
    ppermute x2, waiting for transfers between devices, other_half(): return lax.ppermute(x, 'mp', [(0, 1), (1, 0)])  2.38 us
  transfers between devices with their start and end apart: 2, of which 2 were waited for; matrix products, arithmetic and copies ran while one was open for 0% of the time, Pallas kernels for 0%

profile of v8, /device:TPU:16, one launch (start us, length us, event | category | flops | bytes accessed | tf_op | source)
XLA Modules:
  0.0 93.9 jit_solution(18065926576722754136)
XLA Ops:
  1.3 0.8 add_bitcast_fusion.table_ref.refs_0_
  2.1 4.7 %shard_map.68 = (bf16[32,8,384]{2,1,0:T(8,128)(2,1)S(1)}, bf16[64,256,256]{2,1,0:T(8,128)(2,1)S(1)}, bf16[256,64]{1,0:T(8,128)(2,1)S(1)}, bf16[56,256,256]{2,1,0:T(8,128)(2,1)S(1)}) custom-call(f32[24,128]{1,0:T(8,128)S(1)} %add_bitcast_fusion.table_ref.refs_0_, bf16[64,256,256]{2,1,0:T(8,128)(2,1)} %tiles_ref.1), custom_call_target="tpu_custom_call" | custom-call | flops 67108864 | bytes 8388608 | tf_op jit(solution)/shard_map/pallas_call | solution.py:332
  6.8 22.4 %all_to_all.25.recv_ref.index_ref = bf16[32,8,384]{2,1,0:T(8,128)(2,1)S(1)} all-to-all(bf16[32,8,384]{2,1,0:T(8,128)(2,1)S(1)} %get-tuple-element.20), channel_id=1, replica_groups=mesh['path'=32,'mp'=2,'period'=4] {'path'}, dimensions={0} | all-to-all | bytes 393216 | tf_op jit(solution)/shard_map/all_to_all | solution.py:327
  29.2 0.4 shard_map.69
  29.6 14.4 %all_to_all.26.recv_ref = bf16[32,8,256]{2,1,0:T(8,128)(2,1)S(1)} all-to-all(bf16[32,8,256]{2,1,0:T(8,128)(2,1)S(1)} %get-tuple-element.21), channel_id=1, replica_groups=mesh['path'=32,'mp'=2,'period'=4] {'path'}, dimensions={0} | all-to-all | bytes 262144 | tf_op jit(solution)/shard_map/all_to_all | solution.py:327
  44.0 1.5 %shard_map.70.part_ref = f32[8,384]{1,0:T(8,128)S(1)} custom-call(f32[24,128]{1,0:T(8,128)S(1)} %add_bitcast_fusion.table_ref.refs_0_, bf16[256,64]{1,0:T(8,128)(2,1)S(1)} %get-tuple-element.19.place_ref, bf16[32,8,256]{2,1,0:T(8,128)(2,1)S(1)} %all_to_all.26.recv_ref, f32[8,128]{1,0:T(8,128)S(1)} %get-tuple-element.22.tail_ref.scal_ref, ...), custom_call_target="tpu_custom_call" | custom-call | flops 67108864 | bytes 8388608 | tf_op jit(solution)/shard_map/pallas_call | solution.py:348
  45.5 0.0 collective-permute-start
  45.5 1.2 %collective-permute-done.other_ref = f32[8,384]{1,0:T(8,128)S(1)} collective-permute-done((f32[8,384]{1,0:T(8,128)S(1)}, f32[8,384]{1,0:T(8,128)S(1)}, u32[]{:S(2)}, u32[]{:S(2)}) %collective-permute-start) | collective-permute-done | bytes 12320 | tf_op jit(solution)/shard_map/ppermute | solution.py:330
  46.7 1.6 %shard_map.71 = (bf16[32,8,256]{2,1,0:T(8,128)(2,1)S(1)}, f32[8,256]{1,0:T(8,128)S(1)}, f32[8,128]{1,0:T(8,128)S(1)}) custom-call(f32[24,128]{1,0:T(8,128)S(1)} %add_bitcast_fusion.table_ref.refs_0_, bf16[256,64]{1,0:T(8,128)(2,1)S(1)} %get-tuple-element.19.place_ref, f32[8,384]{1,0:T(8,128)S(1)} %shard_map.70.part_ref, ...), custom_call_target="tpu_custom_call" | custom-call | flops 67108864 | bytes 8388608 | tf_op jit(solution)/shard_map/pallas_call | solution.py:349
  48.3 14.0 %all_to_all.27.recv_ref = bf16[32,8,256]{2,1,0:T(8,128)(2,1)S(1)} all-to-all(bf16[32,8,256]{2,1,0:T(8,128)(2,1)S(1)} %get-tuple-element.25), channel_id=1, replica_groups=mesh['path'=32,'mp'=2,'period'=4] {'path'}, dimensions={0} | all-to-all | bytes 262144 | tf_op jit(solution)/shard_map/all_to_all | solution.py:327
  62.4 0.4 shard_map.72
  62.8 13.9 %all_to_all.28.recv_ref = bf16[32,8,256]{2,1,0:T(8,128)(2,1)S(1)} all-to-all(bf16[32,8,256]{2,1,0:T(8,128)(2,1)S(1)} %get-tuple-element.27), channel_id=1, replica_groups=mesh['path'=32,'mp'=2,'period'=4] {'path'}, dimensions={0} | all-to-all | bytes 262144 | tf_op jit(solution)/shard_map/all_to_all | solution.py:327
  76.8 1.5 %shard_map.73.part_ref = f32[8,384]{1,0:T(8,128)S(1)} custom-call(f32[24,128]{1,0:T(8,128)S(1)} %add_bitcast_fusion.table_ref.refs_0_, bf16[256,64]{1,0:T(8,128)(2,1)S(1)} %get-tuple-element.19.place_ref, bf16[32,8,256]{2,1,0:T(8,128)(2,1)S(1)} %all_to_all.28.recv_ref, f32[8,128]{1,0:T(8,128)S(1)} %get-tuple-element.28.tail_ref, ...), custom_call_target="tpu_custom_call" | custom-call | flops 67108864 | bytes 8388608 | tf_op jit(solution)/shard_map/pallas_call | solution.py:355
  78.2 0.0 collective-permute-start.1
  78.3 1.2 %collective-permute-done.1.other_ref = f32[8,384]{1,0:T(8,128)S(1)} collective-permute-done((f32[8,384]{1,0:T(8,128)S(1)}, f32[8,384]{1,0:T(8,128)S(1)}, u32[]{:S(2)}, u32[]{:S(2)}) %collective-permute-start.1) | collective-permute-done | bytes 12320 | tf_op jit(solution)/shard_map/ppermute | solution.py:330
  79.5 0.1 shard_map.74
  79.6 13.5 %all_to_all.29.refs_1_ = bf16[32,8,128]{2,1,0:T(8,128)(2,1)S(1)} all-to-all(bf16[32,8,128]{2,1,0:T(8,128)(2,1)S(1)} %get-tuple-element.30), channel_id=1, replica_groups=mesh['path'=32,'mp'=2,'period'=4] {'path'}, dimensions={0} | all-to-all | bytes 131072 | tf_op jit(solution)/shard_map/all_to_all | solution.py:327
  93.0 0.9 shard_map.75
Async XLA Ops:
  45.5 1.2 %collective-permute-start = (f32[8,384]{1,0:T(8,128)S(1)}, f32[8,384]{1,0:T(8,128)S(1)}, u32[]{:S(2)}, u32[]{:S(2)}) collective-permute-start(f32[8,384]{1,0:T(8,128)S(1)} %shard_map.70.part_ref), channel_id=1, source_target_pairs={{0,4},{4,0},{1,5},{5,1},{2,6},{6,2},{3,7},{7,3},{8,12},{12,8},{9,1... | collective-permute-start | bytes 36872 | tf_op jit(solution)/shard_map/ppermute | solution.py:330
  78.2 1.2 %collective-permute-start.1 = (f32[8,384]{1,0:T(8,128)S(1)}, f32[8,384]{1,0:T(8,128)S(1)}, u32[]{:S(2)}, u32[]{:S(2)}) collective-permute-start(f32[8,384]{1,0:T(8,128)S(1)} %shard_map.73.part_ref), channel_id=1, source_target_pairs={{0,4},{4,0},{1,5},{5,1},{2,6},{6,2},{3,7},{7,3},{8,12},{12,8},{9,1... | collective-permute-start | bytes 36872 | tf_op jit(solution)/shard_map/ppermute | solution.py:330

commit v9 on v8

--- a/solution.py
+++ b/solution.py
@@ -15,6 +15,7 @@
 F32 = jnp.float32
 BF16 = jnp.bfloat16
 VMEM = pl.BlockSpec(memory_space=pltpu.VMEM)
+SMEM = pl.BlockSpec(memory_space=pltpu.SMEM)
 HBM = pl.BlockSpec(memory_space=pltpu.HBM)
 
 
@@ -107,7 +108,7 @@
     for k in range(CHUNKS):
         part = pl.ds(k * step, step)
         copies.append(pltpu.make_async_copy(tiles_ref.at[part], held.at[part], sems.at[k]))
-        copies[-1].start()
+        copies[-1].start(priority=1)
     return copies
 
 
@@ -152,10 +153,20 @@
 
 
 def first_kernel(
-    table_ref, tiles_ref, send_ref, held_ref, place_ref, turned_ref, sems
+    data_ref, cols_ref, rows_ref, count_ref, tiles_ref,
+    send_ref, held_ref, place_ref, turned_ref, table_ref, cols_buf, rows_buf, sems, small,
 ):
     npath, limit, width = send_ref.shape
+    lines = data_ref.shape[0]
+    pairs = ((data_ref, table_ref.at[:lines]), (cols_ref, cols_buf), (rows_ref, rows_buf))
+    loads = [pltpu.make_async_copy(a, b, small.at[k]) for k, (a, b) in enumerate(pairs)]
+    for load in loads:
+        load.start()
     copies = start_tiles(tiles_ref, held_ref, sems)
+    for load in loads:
+        load.wait()
+    named = jnp.concatenate([cols_buf[...], rows_buf[...]], axis=1).astype(F32)
+    table_ref[lines:, :] = jnp.where(iota((8, META), 0) == 0, named, 1.0 * count_ref[0])
     left = data_of(table_ref)
     rows, cols, count = slots_of(table_ref)
     place, inside = placement(cols, count, npath, limit)
@@ -309,13 +320,7 @@
     row_tiles = data.shape[0] // tile
     npath = lax.axis_size("path")
     limit = max(2, max(slots // 8, (slots + npath - 1) // npath))
-    cells = data.shape[0] + 8 * META
-    named, start = 0, data.shape[0]
-    for x in (tile_cols, tile_rows, tile_counts):
-        named += jnp.pad(x, (start, cells - start - x.shape[0]))
-        start += x.shape[0]
-    table = named.astype(F32) + jnp.pad(data, (0, cells - data.shape[0]))
-    table = table.reshape(-1, META)
+    data = data.reshape(-1, META)
     payload = ((npath, limit, tile), BF16)
     scal = ((8, META), F32)
     own_shape = ((CT_DEV, tile), F32)
@@ -329,19 +334,27 @@
     def other_half(x):
         return lax.ppermute(x, "mp", [(0, 1), (1, 0)])
 
-    send, tiles, place, turned = call(
+    inputs = [data, tile_cols.reshape(1, slots), tile_rows.reshape(1, slots), tiles]
+    inputs = [pltpu.with_memory_space_constraint(x, pltpu.HBM) for x in inputs]
+    send, tiles, place, turned, table = call(
         first_kernel,
-        [VMEM, HBM],
+        [HBM] * 3 + [SMEM, HBM],
         [
             ((npath, limit, tile + META), BF16),
             (tiles.shape, tiles.dtype),
             ((npath * limit, slots), BF16),
             (((CHUNKS - 1) * TURNED, tile, tile), tiles.dtype),
+            ((data.shape[0] + 8, META), F32),
         ],
-        scratch=[pltpu.SemaphoreType.DMA((CHUNKS,))],
+        scratch=[
+            pltpu.VMEM((1, slots), jnp.int32),
+            pltpu.VMEM((1, slots), jnp.int32),
+            pltpu.SemaphoreType.DMA((CHUNKS,)),
+            pltpu.SemaphoreType.DMA((3,)),
+        ],
         room=FIRST_LIMIT,
         **work,
-    )(table, pltpu.with_memory_space_constraint(tiles, pltpu.HBM))
+    )(*inputs[:3], tile_counts, inputs[3])
     index = swap(send)
     send, own0, scal0 = call(first_owner_kernel, [VMEM], [payload, own_shape, scal])(index)
     pass_forward = call(forward_kernel, [VMEM] * 6, [part_shape], **work)

time: 94.2 us -> 93.5 us (level)
  no operation moved by 1% of the time
where the time goes in v9:
time: 93.5 us; the launch traced here: 93.2 us
  blocking collectives  78.3 us (84%)
  Pallas kernels  11.1 us (12%)
  waiting for transfers between devices  2.38 us (3%)
  between operations  1.34 us (1%)
    all_to_all x5, blocking collectives, swap(): return lax.all_to_all(x, 'path', 0, 0, tiled=True)  78.3 us
    pallas_call x1, Pallas kernels, on_device(): call(first_kernel, [HBM] * 3 + [SMEM, HBM], [((npath, limit, tile + META)...  4.75 us
    ppermute x2, waiting for transfers between devices, other_half(): return lax.ppermute(x, 'mp', [(0, 1), (1, 0)])  2.38 us
  transfers between devices with their start and end apart: 2, of which 2 were waited for; matrix products, arithmetic and copies ran while one was open for 0% of the time, Pallas kernels for 0%

profile of v9, /device:TPU:16, one launch (start us, length us, event | category | flops | bytes accessed | tf_op | source)
XLA Modules:
  0.0 93.2 jit_solution(16654027307314452163)
XLA Ops:
  1.3 4.8 %shard_map.68 = (bf16[32,8,384]{2,1,0:T(8,128)(2,1)S(1)}, bf16[64,256,256]{2,1,0:T(8,128)(2,1)S(1)}, bf16[256,64]{1,0:T(8,128)(2,1)S(1)}, bf16[56,256,256]{2,1,0:T(8,128)(2,1)S(1)}, f32[24,128]{1,0:T(8,128)S(1)}) custom-call(f32[16,128]{1,0:T(8,128)} %bitcast.5, s32[1,64]{1,0:T(1,128)} %bitcast.6, s32[1,64]{1,0:T(1,128)} %bitcast.7, s32[1]{0:T(128)S(6)} %copy.7.count_ref, ...), custom_call_target="tpu_custom_call" | custom-call | flops 67108864 | bytes 8388608 | tf_op jit(solution)/shard_map/pallas_call | solution.py:339
  6.0 22.4 %all_to_all.25.recv_ref.index_ref = bf16[32,8,384]{2,1,0:T(8,128)(2,1)S(1)} all-to-all(bf16[32,8,384]{2,1,0:T(8,128)(2,1)S(1)} %get-tuple-element.22), channel_id=1, replica_groups=mesh['path'=32,'mp'=2,'period'=4] {'path'}, dimensions={0} | all-to-all | bytes 393216 | tf_op jit(solution)/shard_map/all_to_all | solution.py:332
  28.5 0.4 shard_map.69
  28.9 14.4 %all_to_all.26.recv_ref = bf16[32,8,256]{2,1,0:T(8,128)(2,1)S(1)} all-to-all(bf16[32,8,256]{2,1,0:T(8,128)(2,1)S(1)} %get-tuple-element.23), channel_id=1, replica_groups=mesh['path'=32,'mp'=2,'period'=4] {'path'}, dimensions={0} | all-to-all | bytes 262144 | tf_op jit(solution)/shard_map/all_to_all | solution.py:332
  43.3 1.5 %shard_map.70.part_ref = f32[8,384]{1,0:T(8,128)S(1)} custom-call(f32[24,128]{1,0:T(8,128)S(1)} %get-tuple-element.20.table_ref.refs_0_, bf16[256,64]{1,0:T(8,128)(2,1)S(1)} %get-tuple-element.21.place_ref, bf16[32,8,256]{2,1,0:T(8,128)(2,1)S(1)} %all_to_all.26.recv_ref, f32[8,128]{1,0:T(8,128)S(1)} %get-tuple-element.24.tail_ref.scal_ref, ...), custom_call_target="tpu_custom_call" | custom-call | flops 67108864 | bytes 8388608 | tf_op jit(solution)/shard_map/pallas_call | solution.py:361
  44.8 0.0 collective-permute-start
  44.8 1.2 %collective-permute-done.other_ref = f32[8,384]{1,0:T(8,128)S(1)} collective-permute-done((f32[8,384]{1,0:T(8,128)S(1)}, f32[8,384]{1,0:T(8,128)S(1)}, u32[]{:S(2)}, u32[]{:S(2)}) %collective-permute-start) | collective-permute-done | bytes 12320 | tf_op jit(solution)/shard_map/ppermute | solution.py:335
  46.0 1.6 %shard_map.71 = (bf16[32,8,256]{2,1,0:T(8,128)(2,1)S(1)}, f32[8,256]{1,0:T(8,128)S(1)}, f32[8,128]{1,0:T(8,128)S(1)}) custom-call(f32[24,128]{1,0:T(8,128)S(1)} %get-tuple-element.20.table_ref.refs_0_, bf16[256,64]{1,0:T(8,128)(2,1)S(1)} %get-tuple-element.21.place_ref, f32[8,384]{1,0:T(8,128)S(1)} %shard_map.70.part_ref, ...), custom_call_target="tpu_custom_call" | custom-call | flops 67108864 | bytes 8388608 | tf_op jit(solution)/shard_map/pallas_call | solution.py:362
  47.6 14.0 %all_to_all.27.recv_ref = bf16[32,8,256]{2,1,0:T(8,128)(2,1)S(1)} all-to-all(bf16[32,8,256]{2,1,0:T(8,128)(2,1)S(1)} %get-tuple-element.27), channel_id=1, replica_groups=mesh['path'=32,'mp'=2,'period'=4] {'path'}, dimensions={0} | all-to-all | bytes 262144 | tf_op jit(solution)/shard_map/all_to_all | solution.py:332
  61.7 0.4 shard_map.72
  62.1 13.9 %all_to_all.28.recv_ref = bf16[32,8,256]{2,1,0:T(8,128)(2,1)S(1)} all-to-all(bf16[32,8,256]{2,1,0:T(8,128)(2,1)S(1)} %get-tuple-element.29), channel_id=1, replica_groups=mesh['path'=32,'mp'=2,'period'=4] {'path'}, dimensions={0} | all-to-all | bytes 262144 | tf_op jit(solution)/shard_map/all_to_all | solution.py:332
  76.0 1.5 %shard_map.73.part_ref = f32[8,384]{1,0:T(8,128)S(1)} custom-call(f32[24,128]{1,0:T(8,128)S(1)} %get-tuple-element.20.table_ref.refs_0_, bf16[256,64]{1,0:T(8,128)(2,1)S(1)} %get-tuple-element.21.place_ref, bf16[32,8,256]{2,1,0:T(8,128)(2,1)S(1)} %all_to_all.28.recv_ref, f32[8,128]{1,0:T(8,128)S(1)} %get-tuple-element.30.tail_ref, ...), custom_call_target="tpu_custom_call" | custom-call | flops 67108864 | bytes 8388608 | tf_op jit(solution)/shard_map/pallas_call | solution.py:368
  77.5 0.0 collective-permute-start.1
  77.5 1.2 %collective-permute-done.1.other_ref = f32[8,384]{1,0:T(8,128)S(1)} collective-permute-done((f32[8,384]{1,0:T(8,128)S(1)}, f32[8,384]{1,0:T(8,128)S(1)}, u32[]{:S(2)}, u32[]{:S(2)}) %collective-permute-start.1) | collective-permute-done | bytes 12320 | tf_op jit(solution)/shard_map/ppermute | solution.py:335
  78.7 0.1 shard_map.74
  78.9 13.5 %all_to_all.29.refs_1_ = bf16[32,8,128]{2,1,0:T(8,128)(2,1)S(1)} all-to-all(bf16[32,8,128]{2,1,0:T(8,128)(2,1)S(1)} %get-tuple-element.32), channel_id=1, replica_groups=mesh['path'=32,'mp'=2,'period'=4] {'path'}, dimensions={0} | all-to-all | bytes 131072 | tf_op jit(solution)/shard_map/all_to_all | solution.py:332
  92.3 0.9 shard_map.75
Async XLA Ops:
  44.8 1.2 %collective-permute-start = (f32[8,384]{1,0:T(8,128)S(1)}, f32[8,384]{1,0:T(8,128)S(1)}, u32[]{:S(2)}, u32[]{:S(2)}) collective-permute-start(f32[8,384]{1,0:T(8,128)S(1)} %shard_map.70.part_ref), channel_id=1, source_target_pairs={{0,4},{4,0},{1,5},{5,1},{2,6},{6,2},{3,7},{7,3},{8,12},{12,8},{9,1... | collective-permute-start | bytes 36872 | tf_op jit(solution)/shard_map/ppermute | solution.py:335
  77.5 1.2 %collective-permute-start.1 = (f32[8,384]{1,0:T(8,128)S(1)}, f32[8,384]{1,0:T(8,128)S(1)}, u32[]{:S(2)}, u32[]{:S(2)}) collective-permute-start(f32[8,384]{1,0:T(8,128)S(1)} %shard_map.73.part_ref), channel_id=1, source_target_pairs={{0,4},{4,0},{1,5},{5,1},{2,6},{6,2},{3,7},{7,3},{8,12},{12,8},{9,1... | collective-permute-start | bytes 36872 | tf_op jit(solution)/shard_map/ppermute | solution.py:335

commit v10 on v9

--- a/solution.py
+++ b/solution.py
@@ -132,7 +132,7 @@
             mine = (sub == i) | (sub == i + step)
             acc += dot(jnp.where(mine, block, 0.0).astype(BF16), held[k * step + i], 1, 0)
         out.append(fold(acc).astype(BF16))
-        if turned is not None and k < CHUNKS - 1:
+        if turned is not None:
             for i in range(TURNED):
                 turned[k * TURNED + i] = held[k * step + i].T
     return jnp.concatenate(out, axis=0)
@@ -145,7 +145,7 @@
     for s in range(slots):
         lhs = row_hot[:, s : s + 1] * picked[s : s + 1, :]
         k, i = divmod(s, slots // CHUNKS)
-        if i < TURNED and k < CHUNKS - 1:
+        if i < TURNED:
             acc += dot(lhs.astype(BF16), turned[k * TURNED + i], 1, 0)
         else:
             acc += dot(lhs.astype(BF16), held[s], 1, 1)
@@ -343,7 +343,7 @@
             ((npath, limit, tile + META), BF16),
             (tiles.shape, tiles.dtype),
             ((npath * limit, slots), BF16),
-            (((CHUNKS - 1) * TURNED, tile, tile), tiles.dtype),
+            ((CHUNKS * TURNED, tile, tile), tiles.dtype),
             ((data.shape[0] + 8, META), F32),
         ],
         scratch=[

time: 93.5 us -> 93.2 us (level)
  no operation moved by 1% of the time
where the time goes in v10:
time: 93.2 us; the launch traced here: 92.9 us
  blocking collectives  78.3 us (84%)
  Pallas kernels  10.9 us (12%)
  waiting for transfers between devices  2.38 us (3%)
  between operations  1.34 us (1%)
    all_to_all x5, blocking collectives, swap(): return lax.all_to_all(x, 'path', 0, 0, tiled=True)  78.3 us
    pallas_call x1, Pallas kernels, on_device(): call(first_kernel, [HBM] * 3 + [SMEM, HBM], [((npath, limit, tile + META)...  4.76 us
    ppermute x2, waiting for transfers between devices, other_half(): return lax.ppermute(x, 'mp', [(0, 1), (1, 0)])  2.38 us
  transfers between devices with their start and end apart: 2, of which 2 were waited for; matrix products, arithmetic and copies ran while one was open for 0% of the time, Pallas kernels for 0%

profile of v10, /device:TPU:16, one launch (start us, length us, event | category | flops | bytes accessed | tf_op | source)
XLA Modules:
  0.0 92.9 jit_solution(14250174722712911220)
XLA Ops:
  1.3 4.8 %shard_map.68 = (bf16[32,8,384]{2,1,0:T(8,128)(2,1)S(1)}, bf16[64,256,256]{2,1,0:T(8,128)(2,1)S(1)}, bf16[256,64]{1,0:T(8,128)(2,1)S(1)}, bf16[64,256,256]{2,1,0:T(8,128)(2,1)S(1)}, f32[24,128]{1,0:T(8,128)S(1)}) custom-call(f32[16,128]{1,0:T(8,128)} %bitcast.5, s32[1,64]{1,0:T(1,128)} %bitcast.6, s32[1,64]{1,0:T(1,128)} %bitcast.7, s32[1]{0:T(128)S(6)} %copy.7.count_ref, ...), custom_call_target="tpu_custom_call" | custom-call | flops 67108864 | bytes 8388608 | tf_op jit(solution)/shard_map/pallas_call | solution.py:339
  6.0 22.4 %all_to_all.25.recv_ref.index_ref = bf16[32,8,384]{2,1,0:T(8,128)(2,1)S(1)} all-to-all(bf16[32,8,384]{2,1,0:T(8,128)(2,1)S(1)} %get-tuple-element.22), channel_id=1, replica_groups=mesh['path'=32,'mp'=2,'period'=4] {'path'}, dimensions={0} | all-to-all | bytes 393216 | tf_op jit(solution)/shard_map/all_to_all | solution.py:332
  28.5 0.4 shard_map.69
  28.9 14.4 %all_to_all.26.recv_ref = bf16[32,8,256]{2,1,0:T(8,128)(2,1)S(1)} all-to-all(bf16[32,8,256]{2,1,0:T(8,128)(2,1)S(1)} %get-tuple-element.23), channel_id=1, replica_groups=mesh['path'=32,'mp'=2,'period'=4] {'path'}, dimensions={0} | all-to-all | bytes 262144 | tf_op jit(solution)/shard_map/all_to_all | solution.py:332
  43.3 1.3 %shard_map.70.part_ref = f32[8,384]{1,0:T(8,128)S(1)} custom-call(f32[24,128]{1,0:T(8,128)S(1)} %get-tuple-element.20.table_ref.refs_0_, bf16[256,64]{1,0:T(8,128)(2,1)S(1)} %get-tuple-element.21.place_ref, bf16[32,8,256]{2,1,0:T(8,128)(2,1)S(1)} %all_to_all.26.recv_ref, f32[8,128]{1,0:T(8,128)S(1)} %get-tuple-element.24.tail_ref.scal_ref, ...), custom_call_target="tpu_custom_call" | custom-call | flops 67108864 | bytes 8388608 | tf_op jit(solution)/shard_map/pallas_call | solution.py:361
  44.6 0.0 collective-permute-start
  44.7 1.2 %collective-permute-done.other_ref = f32[8,384]{1,0:T(8,128)S(1)} collective-permute-done((f32[8,384]{1,0:T(8,128)S(1)}, f32[8,384]{1,0:T(8,128)S(1)}, u32[]{:S(2)}, u32[]{:S(2)}) %collective-permute-start) | collective-permute-done | bytes 12320 | tf_op jit(solution)/shard_map/ppermute | solution.py:335
  45.8 1.6 %shard_map.71 = (bf16[32,8,256]{2,1,0:T(8,128)(2,1)S(1)}, f32[8,256]{1,0:T(8,128)S(1)}, f32[8,128]{1,0:T(8,128)S(1)}) custom-call(f32[24,128]{1,0:T(8,128)S(1)} %get-tuple-element.20.table_ref.refs_0_, bf16[256,64]{1,0:T(8,128)(2,1)S(1)} %get-tuple-element.21.place_ref, f32[8,384]{1,0:T(8,128)S(1)} %shard_map.70.part_ref, ...), custom_call_target="tpu_custom_call" | custom-call | flops 67108864 | bytes 8388608 | tf_op jit(solution)/shard_map/pallas_call | solution.py:362
  47.5 14.0 %all_to_all.27.recv_ref = bf16[32,8,256]{2,1,0:T(8,128)(2,1)S(1)} all-to-all(bf16[32,8,256]{2,1,0:T(8,128)(2,1)S(1)} %get-tuple-element.27), channel_id=1, replica_groups=mesh['path'=32,'mp'=2,'period'=4] {'path'}, dimensions={0} | all-to-all | bytes 262144 | tf_op jit(solution)/shard_map/all_to_all | solution.py:332
  61.5 0.4 shard_map.72
  62.0 13.9 %all_to_all.28.recv_ref = bf16[32,8,256]{2,1,0:T(8,128)(2,1)S(1)} all-to-all(bf16[32,8,256]{2,1,0:T(8,128)(2,1)S(1)} %get-tuple-element.29), channel_id=1, replica_groups=mesh['path'=32,'mp'=2,'period'=4] {'path'}, dimensions={0} | all-to-all | bytes 262144 | tf_op jit(solution)/shard_map/all_to_all | solution.py:332
  75.9 1.3 %shard_map.73.part_ref = f32[8,384]{1,0:T(8,128)S(1)} custom-call(f32[24,128]{1,0:T(8,128)S(1)} %get-tuple-element.20.table_ref.refs_0_, bf16[256,64]{1,0:T(8,128)(2,1)S(1)} %get-tuple-element.21.place_ref, bf16[32,8,256]{2,1,0:T(8,128)(2,1)S(1)} %all_to_all.28.recv_ref, f32[8,128]{1,0:T(8,128)S(1)} %get-tuple-element.30.tail_ref, ...), custom_call_target="tpu_custom_call" | custom-call | flops 67108864 | bytes 8388608 | tf_op jit(solution)/shard_map/pallas_call | solution.py:368
  77.2 0.0 collective-permute-start.1
  77.3 1.2 %collective-permute-done.1.other_ref = f32[8,384]{1,0:T(8,128)S(1)} collective-permute-done((f32[8,384]{1,0:T(8,128)S(1)}, f32[8,384]{1,0:T(8,128)S(1)}, u32[]{:S(2)}, u32[]{:S(2)}) %collective-permute-start.1) | collective-permute-done | bytes 12320 | tf_op jit(solution)/shard_map/ppermute | solution.py:335
  78.5 0.1 shard_map.74
  78.6 13.5 %all_to_all.29.refs_1_ = bf16[32,8,128]{2,1,0:T(8,128)(2,1)S(1)} all-to-all(bf16[32,8,128]{2,1,0:T(8,128)(2,1)S(1)} %get-tuple-element.32), channel_id=1, replica_groups=mesh['path'=32,'mp'=2,'period'=4] {'path'}, dimensions={0} | all-to-all | bytes 131072 | tf_op jit(solution)/shard_map/all_to_all | solution.py:332
  92.0 0.9 shard_map.75
Async XLA Ops:
  44.6 1.2 %collective-permute-start = (f32[8,384]{1,0:T(8,128)S(1)}, f32[8,384]{1,0:T(8,128)S(1)}, u32[]{:S(2)}, u32[]{:S(2)}) collective-permute-start(f32[8,384]{1,0:T(8,128)S(1)} %shard_map.70.part_ref), channel_id=1, source_target_pairs={{0,4},{4,0},{1,5},{5,1},{2,6},{6,2},{3,7},{7,3},{8,12},{12,8},{9,1... | collective-permute-start | bytes 36872 | tf_op jit(solution)/shard_map/ppermute | solution.py:335
  77.2 1.2 %collective-permute-start.1 = (f32[8,384]{1,0:T(8,128)S(1)}, f32[8,384]{1,0:T(8,128)S(1)}, u32[]{:S(2)}, u32[]{:S(2)}) collective-permute-start(f32[8,384]{1,0:T(8,128)S(1)} %shard_map.73.part_ref), channel_id=1, source_target_pairs={{0,4},{4,0},{1,5},{5,1},{2,6},{6,2},{3,7},{7,3},{8,12},{12,8},{9,1... | collective-permute-start | bytes 36872 | tf_op jit(solution)/shard_map/ppermute | solution.py:335
